TPU v7x, 32 devices: a whole 2x2x4 slice. The times are simulated.
32 devices in a mesh: px: 4 (over y, x), py: 4 (over z), pz: 2 (over core).
Axes of the slice: x: 2, y: 2, z: 4, core: 2. Of those that a mesh axis runs over, the one named last changes fastest.
Arguments:
- rhs: float32 [32, 512, 512], P('pz', 'py', 'px'), may hold values from -4 to 6
- coeff: float32 [32, 512, 512], P('pz', 'py', 'px'), may hold values from 0.1 to 10
- shift: float32 [32, 512, 512], P('pz', 'py', 'px'), may hold values from 0.01 to 0.3
Outputs:
- solution: float32 [32, 512, 512], P('pz', 'py', 'px')
All inputs are finite; a program needn't handle non-finite values.
Results may differ from a plain program's by a relative error of at most 0.0001.
Values sent between devices are 32-bit elements; how exact they have to be, the bound alone decides.
No kernel may reach another device: no remote copies, remote signals or barrier semaphores. Data moves between devices by JAX's collectives and lax.ppermute only.
A program may use at most 256 MiB of HBM per device.

v0:
```python
import jax
import jax.numpy as jnp
from jax import lax
from jax.sharding import PartitionSpec as P

LEVELS = 3
DEG = 4
CDEG = 8


lower_bound = 0.4
upper_bound = 2.0


def extended(array, sides, width):
    for axis, dim in sides:
        peers, length = (lax.axis_size(axis), array.shape[dim])
        up = [(i, (i + 1) % peers) for i in range(peers - 1)]
        down = [(j, i) for i, j in up]
        last = lax.slice_in_dim(array, length - width, length, axis=dim)
        first = lax.slice_in_dim(array, 0, width, axis=dim)
        before = lax.ppermute(last, axis, up)
        after = lax.ppermute(first, axis, down)
        array = jnp.concatenate([before, array, after], axis=dim)
    return array


def neighbour_views(shape):
    result = []
    for axis_index in range(3):
        for offset in (0, 2):
            index_list = [slice(1, 1 + shape[k]) for k in range(3)]
            index_list[axis_index] = slice(offset, offset + shape[axis_index])
            result.append(tuple(index_list))
    return result


def make_level(coeff_pad, shift_field, factor):
    center = coeff_pad[1:-1, 1:-1, 1:-1]
    weights = jnp.zeros_like(center)
    for view in neighbour_views(center.shape):
        weights = weights + 0.5 * (center + coeff_pad[view])
    inverse = 1.0 / (factor * weights + shift_field)
    return (coeff_pad, shift_field, factor, inverse)


def apply_operator(field_pad, level_data):
    coeff_pad, shift_field, factor, inverse = level_data
    center = field_pad[1:-1, 1:-1, 1:-1]
    coeff_center = coeff_pad[1:-1, 1:-1, 1:-1]
    total = jnp.zeros_like(center)
    for view in neighbour_views(center.shape):
        total = total + 0.5 * (coeff_center + coeff_pad[view]) * (center - field_pad[view])
    return factor * total + shift_field * center


def smooth(field, source, level_data, degree, padder):
    inverse = level_data[3]
    theta = 0.5 * (upper_bound + lower_bound)
    delta = 0.5 * (upper_bound - lower_bound)
    sigma = theta / delta
    rho_now = 1.0 / sigma
    if field is None:
        scaled = source * inverse
        update = scaled / theta
        field = update
    else:
        scaled = (source - apply_operator(padder(field), level_data)) * inverse
        update = scaled / theta
        field = field + update
    for sweep_index in range(degree - 1):
        scaled = (source - apply_operator(padder(field), level_data)) * inverse
        rho_next = 1.0 / (2.0 * sigma - rho_now)
        update = rho_next * rho_now * update + 2.0 * rho_next / delta * scaled
        field = field + update
        rho_now = rho_next
    return field


def restrict(field):
    s0, s1, s2 = field.shape
    return field.reshape(s0 // 2, 2, s1 // 2, 2, s2 // 2, 2).mean(axis=(1, 3, 5))


def refine_axis(padded, axis_index):
    count = padded.shape[axis_index] - 2
    center = lax.slice_in_dim(padded, 1, count + 1, axis=axis_index)
    lower = lax.slice_in_dim(padded, 0, count, axis=axis_index)
    upper = lax.slice_in_dim(padded, 2, count + 2, axis=axis_index)
    even_part = 0.75 * center + 0.25 * lower
    odd_part = 0.75 * center + 0.25 * upper
    stacked = jnp.stack([even_part, odd_part], axis=axis_index + 1)
    shape = list(center.shape)
    shape[axis_index] = 2 * count
    return stacked.reshape(shape)


def prolong(padded):
    for axis_index in range(3):
        padded = refine_axis(padded, axis_index)
    return padded


def fine_pad(field):
    return extended(field, (("pz", 0), ("py", 1), ("px", 2)), 1)


def face_pad(field):
    return extended(field, (("pz", 0), ("py", 1), ("px", 2)), 1)


def coarse_face_pad(field):
    return extended(field, (("pz", 0), ("py", 1), ("px", 2)), 1)


def local(rhs, coeff, shift):
    coeff_pad_zero = extended(coeff, (("pz", 0), ("py", 1), ("px", 2)), 1)
    level_zero = make_level(coeff_pad_zero, shift, 1.0)
    field = smooth(None, rhs, level_zero, DEG, fine_pad)
    residual = rhs - apply_operator(fine_pad(field), level_zero)
    fields = [field]
    sources = [rhs, restrict(residual)]
    levels_list = [None]
    coeff_now = restrict(coeff)
    shift_now = restrict(shift)
    for depth in range(1, LEVELS):
        coeff_pad = extended(coeff_now, (("pz", 0), ("py", 1), ("px", 2)), 1)
        levels_list.append(make_level(coeff_pad, shift_now, 0.25**depth))
        coeff_now = restrict(coeff_now)
        shift_now = restrict(shift_now)
    for depth in range(1, LEVELS):
        field = smooth(None, sources[depth], levels_list[depth], DEG, face_pad)
        residual = sources[depth] - apply_operator(face_pad(field), levels_list[depth])
        fields.append(field)
        sources.append(restrict(residual))
    coarse_source = sources[LEVELS]
    coarse_pad = extended(coeff_now, (("pz", 0), ("py", 1), ("px", 2)), 1)
    coarse_level = make_level(coarse_pad, shift_now, 0.25**LEVELS)
    coarse_field = smooth(None, coarse_source, coarse_level, CDEG, coarse_face_pad)
    padded = extended(coarse_field, (("pz", 0), ("py", 1), ("px", 2)), 1)
    for depth in range(LEVELS - 1, 0, -1):
        field = fields[depth] + prolong(padded)
        field = smooth(field, sources[depth], levels_list[depth], DEG, face_pad)
        padded = extended(field, (("pz", 0), ("py", 1), ("px", 2)), 1)
    field = fields[0] + prolong(padded)
    field = smooth(field, rhs, level_zero, DEG, fine_pad)
    return field


def solution(mesh):
    in_specs = (P("pz", "py", "px"), P("pz", "py", "px"), P("pz", "py", "px"))
    out_specs = P("pz", "py", "px")
    return jax.shard_map(local, mesh=mesh, in_specs=in_specs, out_specs=out_specs, check_vma=False)
```

profile of v0, /device:TPU:0, one launch (start us, length us, event | category | flops | bytes accessed | tf_op | source)
XLA Modules:
  0.0 1421.4 jit_solution(751088284458551188)
XLA Ops:
  8.8 5.6 collective-permute-start.2
  38.0 7.3 broadcast_multiply_fusion
  78.3 11.0 multiply_add_fusion.1
  121.0 11.3 fusion.186
  136.0 69.1 %reshape.59 = f32[8,2,64,2,64,2]{5,4,3,2,1,0:T(8,128)} reshape(f32[16,128,128]{2,1,0:T(8,128)} %param.4) | data formatting | bytes 2097152 | tf_op jit(solution)/shard_map/reshape | solution.py:82
  205.1 21.5 %reduce_sum.82 = f32[8,64,64]{2,1,0:T(8,128)} reduce(f32[8,2,64,2,64,2]{5,4,3,2,1,0:T(8,128)} %reshape.59, f32[]{:T(128)} %constant.32.clone.1), dimensions={1,3,5}, to_apply=%region_1.0 | reduce | flops 229376 | bytes 1179652 | tf_op jit(solution)/shard_map/reduce_sum | solution.py:82
  258.0 69.1 %reshape.60 = f32[8,2,64,2,64,2]{5,4,3,2,1,0:T(8,128)} reshape(f32[16,128,128]{2,1,0:T(8,128)} %param.5) | data formatting | bytes 2097152 | tf_op jit(solution)/shard_map/reshape | solution.py:82
  327.1 21.5 %reduce_sum.83 = f32[8,64,64]{2,1,0:T(8,128)} reduce(f32[8,2,64,2,64,2]{5,4,3,2,1,0:T(8,128)} %reshape.60, f32[]{:T(128)} %constant.32.clone.1), dimensions={1,3,5}, to_apply=%region_2.0 | reduce | flops 229376 | bytes 1179652 | tf_op jit(solution)/shard_map/reduce_sum | solution.py:82
  348.6 11.4 fusion.118
  403.8 6.1 collective-permute-start.34
  410.0 7.2 fusion.95
  419.8 69.1 %reshape.58 = f32[8,2,64,2,64,2]{5,4,3,2,1,0:T(8,128)} reshape(f32[16,128,128]{2,1,0:T(8,128)} %copy.312) | data formatting | bytes 2097152 | tf_op jit(solution)/shard_map/reshape | solution.py:82
  489.0 21.5 %reduce_sum.81 = f32[8,64,64]{2,1,0:T(8,128)} reduce(f32[8,2,64,2,64,2]{5,4,3,2,1,0:T(8,128)} %reshape.58, f32[]{:T(128)} %constant.32.clone.1), dimensions={1,3,5}, to_apply=%region_0.0 | reduce | flops 229376 | bytes 1179652 | tf_op jit(solution)/shard_map/reduce_sum | solution.py:82
  537.0 9.7 collective-permute-done.41
  567.5 10.0 div.94
  608.3 10.8 div.96
  657.1 5.8 collective-permute-start.64
  662.9 8.6 collective-permute-done.59
  673.6 10.8 reshape.61
  790.6 6.2 collective-permute-start.94
  1119.1 8.6 collective-permute-done.179
  1149.9 8.6 collective-permute-done.185
  1175.2 5.5 collective-permute-done.190
  1180.7 8.5 collective-permute-done.191
  1205.8 5.5 collective-permute-done.196
  1211.4 8.5 collective-permute-done.197
  1236.5 5.5 collective-permute-done.202
  1242.0 8.5 collective-permute-done.203
  1287.7 10.4 multiply_add_fusion
  1327.7 10.5 fusion.790
  1367.8 10.5 fusion.788
  1407.9 10.5 fusion.8
  (943 shorter events, 921.6 us)
Async XLA Ops:
  23.8 14.2 collective-permute-start.5
  133.4 93.2 %collective-permute-start.18 = (f32[1,128,128]{1,0,2:T(1,128)S(1)}, f32[1,128,128]{1,0,2:T(1,128)S(1)}, u32[]{:S(2)}, u32[]{:S(2)}) collective-permute-start(f32[1,128,128]{1,0,2:T(1,128)S(1)} %get-tuple-element.118), channel_id=1, source_target_pairs={{0,1},{2,3},{4,5},{6,7},{8,9},{10,11},{12,13},{14,15},{16,17},{18,... | collective-permute-start | bytes 196616 | tf_op jit(solution)/shard_map/ppermute | solution.py:22
  134.7 91.9 %collective-permute-start.19 = (f32[1,128,128]{1,0,2:T(1,128)S(1)}, f32[1,128,128]{1,0,2:T(1,128)S(1)}, u32[]{:S(2)}, u32[]{:S(2)}) collective-permute-start(f32[1,128,128]{1,0,2:T(1,128)S(1)} %get-tuple-element.119), channel_id=1, source_target_pairs={{1,0},{3,2},{5,4},{7,6},{9,8},{11,10},{13,12},{15,14},{17,16},{19,... | collective-permute-start | bytes 196616 | tf_op jit(solution)/shard_map/ppermute | solution.py:23
  248.2 100.4 %collective-permute-start.22 = (f32[18,130,1]{1,0,2:T(8,128)}, f32[18,130,1]{1,0,2:T(8,128)}, u32[]{:S(2)}, u32[]{:S(2)}) collective-permute-start(f32[18,130,1]{1,0,2:T(8,128)} %get-tuple-element.78), channel_id=1, source_target_pairs={{0,8},{8,16},{16,24},{1,9},{9,17},{17,25},{2,10},{10,18},{18,26},{... | collective-permute-start | bytes 28088 | tf_op jit(solution)/shard_map/ppermute | solution.py:22
  251.6 97.0 %collective-permute-start.23 = (f32[18,130,1]{1,0,2:T(8,128)}, f32[18,130,1]{1,0,2:T(8,128)}, u32[]{:S(2)}, u32[]{:S(2)}) collective-permute-start(f32[18,130,1]{1,0,2:T(8,128)} %get-tuple-element.79), channel_id=1, source_target_pairs={{8,0},{16,8},{24,16},{9,1},{17,9},{25,17},{10,2},{18,10},{26,18},{... | collective-permute-start | bytes 28088 | tf_op jit(solution)/shard_map/ppermute | solution.py:23
  253.5 111.6 %collective-permute-start.30 = (f32[1,64,64]{2,1,0:T(8,128)}, f32[1,64,64]{2,1,0:T(8,128)}, u32[]{:S(2)}, u32[]{:S(2)}) collective-permute-start(f32[1,64,64]{2,1,0:T(8,128)} %get-tuple-element.190), channel_id=1, source_target_pairs={{0,1},{2,3},{4,5},{6,7},{8,9},{10,11},{12,13},{14,15},{16,17},{18,... | collective-permute-start | bytes 49160 | tf_op jit(solution)/shard_map/ppermute | solution.py:22
  256.3 108.8 %collective-permute-start.31 = (f32[1,64,64]{2,1,0:T(8,128)}, f32[1,64,64]{2,1,0:T(8,128)}, u32[]{:S(2)}, u32[]{:S(2)}) collective-permute-start(f32[1,64,64]{2,1,0:T(8,128)} %get-tuple-element.191), channel_id=1, source_target_pairs={{1,0},{3,2},{5,4},{7,6},{9,8},{11,10},{13,12},{15,14},{17,16},{19,... | collective-permute-start | bytes 49160 | tf_op jit(solution)/shard_map/ppermute | solution.py:23
  366.4 20.8 %collective-permute-start.33 = (f32[10,1,64]{2,1,0:T(1,128)}, f32[10,1,64]{2,1,0:T(1,128)S(1)}, u32[]{:S(2)}, u32[]{:S(2)}) collective-permute-start(f32[10,1,64]{2,1,0:T(1,128)} %get-tuple-element.168), channel_id=1, source_target_pairs={{2,0},{4,2},{6,4},{3,1},{5,3},{7,5},{10,8},{12,10},{14,12},{11,9},... | collective-permute-start | bytes 7688 | tf_op jit(solution)/shard_map/ppermute | solution.py:23
  367.7 19.5 %collective-permute-start.32 = (f32[10,1,64]{2,1,0:T(1,128)}, f32[10,1,64]{2,1,0:T(1,128)S(1)}, u32[]{:S(2)}, u32[]{:S(2)}) collective-permute-start(f32[10,1,64]{2,1,0:T(1,128)} %get-tuple-element.169), channel_id=1, source_target_pairs={{0,2},{2,4},{4,6},{1,3},{3,5},{5,7},{8,10},{10,12},{12,14},{9,11},... | collective-permute-start | bytes 7688 | tf_op jit(solution)/shard_map/ppermute | solution.py:22
  394.6 15.3 %collective-permute-start.28 = (f32[18,130,1]{1,0,2:T(8,128)S(1)}, f32[18,130,1]{1,0,2:T(8,128)S(1)}, u32[]{:S(2)}, u32[]{:S(2)}) collective-permute-start(f32[18,130,1]{1,0,2:T(8,128)S(1)} %get-tuple-element.76), channel_id=1, source_target_pairs={{0,8},{8,16},{16,24},{1,9},{9,17},{17,25},{2,10},{10,18},{18,26},{... | collective-permute-start | bytes 28088 | tf_op jit(solution)/shard_map/ppermute | solution.py:22
  402.5 107.9 %collective-permute-start.35 = (f32[10,66,1]{2,1,0:T(8,128)}, f32[10,66,1]{2,1,0:T(8,128)}, u32[]{:S(2)}, u32[]{:S(2)}) collective-permute-start(f32[10,66,1]{2,1,0:T(8,128)} %get-tuple-element.148), channel_id=1, source_target_pairs={{8,0},{16,8},{24,16},{9,1},{17,9},{25,17},{10,2},{18,10},{26,18},{... | collective-permute-start | bytes 7928 | tf_op jit(solution)/shard_map/ppermute | solution.py:23
  403.8 106.6 %collective-permute-start.34 = (f32[10,66,1]{2,1,0:T(8,128)}, f32[10,66,1]{2,1,0:T(8,128)}, u32[]{:S(2)}, u32[]{:S(2)}) collective-permute-start(f32[10,66,1]{2,1,0:T(8,128)} %get-tuple-element.149), channel_id=1, source_target_pairs={{0,8},{8,16},{16,24},{1,9},{9,17},{17,25},{2,10},{10,18},{18,26},{... | collective-permute-start | bytes 7928 | tf_op jit(solution)/shard_map/ppermute | solution.py:22
  530.2 16.4 %collective-permute-start.41 = (f32[10,66,1]{2,1,0:T(8,128)S(1)}, f32[10,66,1]{2,1,0:T(8,128)S(1)}, u32[]{:S(2)}, u32[]{:S(2)}) collective-permute-start(f32[10,66,1]{2,1,0:T(8,128)S(1)} %get-tuple-element.147), channel_id=1, source_target_pairs={{8,0},{16,8},{24,16},{9,1},{17,9},{25,17},{10,2},{18,10},{26,18},{... | collective-permute-start | bytes 7928 | tf_op jit(solution)/shard_map/ppermute | solution.py:23
  563.3 18.9 %collective-permute-start.46 = (f32[10,66,1]{2,1,0:T(8,128)}, f32[10,66,1]{2,1,0:T(8,128)}, u32[]{:S(2)}, u32[]{:S(2)}) collective-permute-start(f32[10,66,1]{2,1,0:T(8,128)} %get-tuple-element.144), channel_id=1, source_target_pairs={{0,8},{8,16},{16,24},{1,9},{9,17},{17,25},{2,10},{10,18},{18,26},{... | collective-permute-start | bytes 7928 | tf_op jit(solution)/shard_map/ppermute | solution.py:22
  566.2 16.0 %collective-permute-start.47 = (f32[10,66,1]{2,1,0:T(8,128)}, f32[10,66,1]{2,1,0:T(8,128)}, u32[]{:S(2)}, u32[]{:S(2)}) collective-permute-start(f32[10,66,1]{2,1,0:T(8,128)} %get-tuple-element.145), channel_id=1, source_target_pairs={{8,0},{16,8},{24,16},{9,1},{17,9},{25,17},{10,2},{18,10},{26,18},{... | collective-permute-start | bytes 7928 | tf_op jit(solution)/shard_map/ppermute | solution.py:23
  595.4 37.2 %collective-permute-start.60 = (f32[1,32,32]{2,1,0:T(8,128)}, f32[1,32,32]{2,1,0:T(8,128)S(1)}, u32[]{:S(2)}, u32[]{:S(2)}) collective-permute-start(f32[1,32,32]{2,1,0:T(8,128)} %get-tuple-element.256), channel_id=1, source_target_pairs={{0,1},{2,3},{4,5},{6,7},{8,9},{10,11},{12,13},{14,15},{16,17},{18,... | collective-permute-start | bytes 12296 | tf_op jit(solution)/shard_map/ppermute | solution.py:22
  597.2 35.4 %collective-permute-start.61 = (f32[1,32,32]{2,1,0:T(8,128)}, f32[1,32,32]{2,1,0:T(8,128)}, u32[]{:S(2)}, u32[]{:S(2)}) collective-permute-start(f32[1,32,32]{2,1,0:T(8,128)} %get-tuple-element.257), channel_id=1, source_target_pairs={{1,0},{3,2},{5,4},{7,6},{9,8},{11,10},{13,12},{15,14},{17,16},{19,... | collective-permute-start | bytes 12296 | tf_op jit(solution)/shard_map/ppermute | solution.py:23
  600.7 22.4 %collective-permute-start.52 = (f32[10,66,1]{2,1,0:T(8,128)}, f32[10,66,1]{2,1,0:T(8,128)}, u32[]{:S(2)}, u32[]{:S(2)}) collective-permute-start(f32[10,66,1]{2,1,0:T(8,128)} %get-tuple-element.142), channel_id=1, source_target_pairs={{0,8},{8,16},{16,24},{1,9},{9,17},{17,25},{2,10},{10,18},{18,26},{... | collective-permute-start | bytes 7928 | tf_op jit(solution)/shard_map/ppermute | solution.py:22
  606.0 17.1 %collective-permute-start.53 = (f32[10,66,1]{2,1,0:T(8,128)}, f32[10,66,1]{2,1,0:T(8,128)}, u32[]{:S(2)}, u32[]{:S(2)}) collective-permute-start(f32[10,66,1]{2,1,0:T(8,128)} %get-tuple-element.143), channel_id=1, source_target_pairs={{8,0},{16,8},{24,16},{9,1},{17,9},{25,17},{10,2},{18,10},{26,18},{... | collective-permute-start | bytes 7928 | tf_op jit(solution)/shard_map/ppermute | solution.py:23
  649.4 13.5 collective-permute-start.58
  653.7 17.7 %collective-permute-start.59 = (f32[10,66,1]{2,1,0:T(8,128)S(1)}, f32[10,66,1]{2,1,0:T(8,128)S(1)}, u32[]{:S(2)}, u32[]{:S(2)}) collective-permute-start(f32[10,66,1]{2,1,0:T(8,128)S(1)} %get-tuple-element.141), channel_id=1, source_target_pairs={{8,0},{16,8},{24,16},{9,1},{17,9},{25,17},{10,2},{18,10},{26,18},{... | collective-permute-start | bytes 7928 | tf_op jit(solution)/shard_map/ppermute | solution.py:23
  655.8 33.3 %collective-permute-start.65 = (f32[6,34,1]{2,1,0:T(8,128)}, f32[6,34,1]{2,1,0:T(8,128)}, u32[]{:S(2)}, u32[]{:S(2)}) collective-permute-start(f32[6,34,1]{2,1,0:T(8,128)} %get-tuple-element.214), channel_id=1, source_target_pairs={{8,0},{16,8},{24,16},{9,1},{17,9},{25,17},{10,2},{18,10},{26,18},{... | collective-permute-start | bytes 2456 | tf_op jit(solution)/shard_map/ppermute | solution.py:23
  657.1 32.0 %collective-permute-start.64 = (f32[6,34,1]{2,1,0:T(8,128)}, f32[6,34,1]{2,1,0:T(8,128)}, u32[]{:S(2)}, u32[]{:S(2)}) collective-permute-start(f32[6,34,1]{2,1,0:T(8,128)} %get-tuple-element.215), channel_id=1, source_target_pairs={{0,8},{8,16},{16,24},{1,9},{9,17},{17,25},{2,10},{10,18},{18,26},{... | collective-permute-start | bytes 2456 | tf_op jit(solution)/shard_map/ppermute | solution.py:22
  746.3 20.6 %collective-permute-start.90 = (f32[1,16,16]{2,1,0:T(8,128)}, f32[1,16,16]{2,1,0:T(8,128)}, u32[]{:S(2)}, u32[]{:S(2)}) collective-permute-start(f32[1,16,16]{2,1,0:T(8,128)} %get-tuple-element.314), channel_id=1, source_target_pairs={{0,1},{2,3},{4,5},{6,7},{8,9},{10,11},{12,13},{14,15},{16,17},{18,... | collective-permute-start | bytes 3080 | tf_op jit(solution)/shard_map/ppermute | solution.py:22
  748.7 18.2 %collective-permute-start.91 = (f32[1,16,16]{2,1,0:T(8,128)}, f32[1,16,16]{2,1,0:T(8,128)}, u32[]{:S(2)}, u32[]{:S(2)}) collective-permute-start(f32[1,16,16]{2,1,0:T(8,128)} %get-tuple-element.315), channel_id=1, source_target_pairs={{1,0},{3,2},{5,4},{7,6},{9,8},{11,10},{13,12},{15,14},{17,16},{19,... | collective-permute-start | bytes 3080 | tf_op jit(solution)/shard_map/ppermute | solution.py:23
  783.4 13.3 collective-permute-start.88
  789.3 13.5 collective-permute-start.95
  1112.4 15.4 %collective-permute-start.179 = (f32[10,66,1]{2,1,0:T(8,128)S(1)}, f32[10,66,1]{2,1,0:T(8,128)S(1)}, u32[]{:S(2)}, u32[]{:S(2)}) collective-permute-start(f32[10,66,1]{2,1,0:T(8,128)S(1)} %get-tuple-element.139), channel_id=1, source_target_pairs={{8,0},{16,8},{24,16},{9,1},{17,9},{25,17},{10,2},{18,10},{26,18},{... | collective-permute-start | bytes 7928 | tf_op jit(solution)/shard_map/ppermute | solution.py:23
  1143.2 15.4 %collective-permute-start.185 = (f32[10,66,1]{2,1,0:T(8,128)S(1)}, f32[10,66,1]{2,1,0:T(8,128)S(1)}, u32[]{:S(2)}, u32[]{:S(2)}) collective-permute-start(f32[10,66,1]{2,1,0:T(8,128)S(1)} %get-tuple-element.137), channel_id=1, source_target_pairs={{8,0},{16,8},{24,16},{9,1},{17,9},{25,17},{10,2},{18,10},{26,18},{... | collective-permute-start | bytes 7928 | tf_op jit(solution)/shard_map/ppermute | solution.py:23
  1173.9 15.4 %collective-permute-start.191 = (f32[10,66,1]{2,1,0:T(8,128)S(1)}, f32[10,66,1]{2,1,0:T(8,128)S(1)}, u32[]{:S(2)}, u32[]{:S(2)}) collective-permute-start(f32[10,66,1]{2,1,0:T(8,128)S(1)} %get-tuple-element.135), channel_id=1, source_target_pairs={{8,0},{16,8},{24,16},{9,1},{17,9},{25,17},{10,2},{18,10},{26,18},{... | collective-permute-start | bytes 7928 | tf_op jit(solution)/shard_map/ppermute | solution.py:23
  1204.5 15.4 %collective-permute-start.197 = (f32[10,66,1]{2,1,0:T(8,128)S(1)}, f32[10,66,1]{2,1,0:T(8,128)S(1)}, u32[]{:S(2)}, u32[]{:S(2)}) collective-permute-start(f32[10,66,1]{2,1,0:T(8,128)S(1)} %get-tuple-element.133), channel_id=1, source_target_pairs={{8,0},{16,8},{24,16},{9,1},{17,9},{25,17},{10,2},{18,10},{26,18},{... | collective-permute-start | bytes 7928 | tf_op jit(solution)/shard_map/ppermute | solution.py:23
  1235.2 15.4 %collective-permute-start.203 = (f32[10,66,1]{2,1,0:T(8,128)S(1)}, f32[10,66,1]{2,1,0:T(8,128)S(1)}, u32[]{:S(2)}, u32[]{:S(2)}) collective-permute-start(f32[10,66,1]{2,1,0:T(8,128)S(1)} %get-tuple-element.131), channel_id=1, source_target_pairs={{8,0},{16,8},{24,16},{9,1},{17,9},{25,17},{10,2},{18,10},{26,18},{... | collective-permute-start | bytes 7928 | tf_op jit(solution)/shard_map/ppermute | solution.py:23
  (311 other events, 4296.7 us)
where the time goes:
time: 1440 us; the launch traced here: 1420 us
  starting transfers between devices  440 us (31%)
  local copies, waits for them, and re-layouts  369 us (26%)
  waiting for transfers between devices  362 us (25%)
  other arithmetic  246 us (17%)
    ppermute x114, waiting for transfers between devices, extended(): after = lax.ppermute(first, axis, down)  317 us
    ppermute x114, starting transfers between devices, extended(): before = lax.ppermute(last, axis, up)  291 us
    reshape x5, local copies, waits for them, and re-layouts, restrict(): field.reshape(s0 // 2, 2, s1 // 2, 2, s2 // 2, 2).mean(axis=(1, 3, 5))  221 us
    ppermute x114, starting transfers between devices, extended(): after = lax.ppermute(first, axis, down)  149 us
    add x28, other arithmetic, smooth(): field = field + update  103 us
    reduce_sum x9, other arithmetic, restrict(): field.reshape(s0 // 2, 2, s1 // 2, 2, s2 // 2, 2).mean(axis=(1, 3, 5))  83.8 us
    ppermute x114, waiting for transfers between devices, extended(): before = lax.ppermute(last, axis, up)  45.4 us
    slice x81, local copies, waits for them, and re-layouts, extended(): last = lax.slice_in_dim(array, length - width, length, axis=dim)  42.7 us
  transfers between devices with their start and end apart: 228, of which 117 were waited for; matrix products, arithmetic and copies ran while one was open for 30% of the time, Pallas kernels for 0%

commit v1 on v0

--- a/solution.py
+++ b/solution.py
@@ -1,11 +1,753 @@
 import jax
 import jax.numpy as jnp
 from jax import lax
+from jax.experimental import pallas as pl
+from jax.experimental.pallas import tpu as pltpu
 from jax.sharding import PartitionSpec as P
 
 LEVELS = 3
 DEG = 4
 CDEG = 8
+THETA = 1.2
+DELTA = 0.8
+F32 = jnp.float32
+LANES = 128
+
+
+def vmem(*shape):
+    return pltpu.VMEM(shape, F32)
+
+
+def shape(*dims):
+    return jax.ShapeDtypeStruct(dims, F32)
+
+
+def call(kernel, outs, scratch=(), ins=0, name=None):
+    spec = pl.BlockSpec(memory_space=pltpu.VMEM)
+    single = not isinstance(outs, (list, tuple))
+    return pl.pallas_call(
+        kernel,
+        out_shape=outs,
+        in_specs=[spec] * ins,
+        out_specs=spec if single else [spec] * len(outs),
+        scratch_shapes=list(scratch),
+        compiler_params=pltpu.CompilerParams(vmem_limit_bytes=60 * 1024 * 1024),
+        name=name,
+    )
+
+
+def dot(a, b):
+    return jnp.dot(a, b, precision=lax.Precision.HIGHEST, preferred_element_type=F32)
+
+
+def iota(rows, cols, axis):
+    return lax.broadcasted_iota(jnp.int32, (rows, cols), axis)
+
+
+def roll(value, amount):
+    amount = amount % LANES
+    return value if amount == 0 else pltpu.roll(value, amount, 1)
+
+
+def chebyshev(degree):
+    sigma = THETA / DELTA
+    rho = 1.0 / sigma
+    steps = [(0.0, 1.0 / THETA)]
+    for _ in range(degree - 1):
+        new = 1.0 / (2.0 * sigma - rho)
+        steps.append((new * rho, 2.0 * new / DELTA))
+        rho = new
+    return steps
+
+
+class Level:
+    def __init__(self, refs, wrap):
+        self.wx, self.wy, self.wz, self.f, self.dinv, self.u, self.v, self.d = refs
+        self.tiles = self.u.shape[2] // LANES
+        self.wrap = wrap
+
+    def get(self, ref, z, row):
+        return [ref[z, row : row + 8, LANES * t : LANES * (t + 1)] for t in range(self.tiles)]
+
+    def put(self, ref, z, row, values):
+        for t, value in enumerate(values):
+            ref[z, row : row + 8, LANES * t : LANES * (t + 1)] = value
+
+    def right(self, values):
+        lane = iota(8, LANES, 1)
+        rolled = [roll(v, -1) for v in values]
+        if self.tiles == 1:
+            return rolled
+        return [jnp.where(lane == LANES - 1, rolled[1 - t], rolled[t]) for t in range(2)]
+
+    def left(self, values):
+        lane = iota(8, LANES, 1)
+        rolled = [roll(v, 1) for v in values]
+        if self.tiles == 1:
+            return rolled
+        return [jnp.where(lane == 0, rolled[1 - t], rolled[t]) for t in range(2)]
+
+
+def each(fn, *lists):
+    return [fn(*items) for items in zip(*lists)]
+
+
+def setup(level, kappa, planes, first, last, coef):
+    lane = iota(8, LANES, 1)
+    half = 0.5 * kappa
+
+    def zface(z, row):
+        return each(lambda a, b: half * (a + b), level.get(coef, z, row), level.get(coef, z + 1, row))
+
+    for t in range(first, last):
+        level.put(level.wz, 0, 8 * t, zface(0, 8 * t))
+
+    for row in (8 * first - 8,):
+        def edge(z, carry):
+            a = level.get(coef, z, row)
+            b = level.get(coef, z, row + 1)
+            level.put(level.wy, z, row, each(lambda p, q: half * (p + q), a, b))
+            return carry
+        lax.fori_loop(1, planes + 1, edge, 0)
+
+    def body(z, carry):
+        for t in range(first, last):
+            row = 8 * t
+            a = level.get(coef, z, row)
+            ar = level.right(a)
+            if level.wrap:
+                ar = each(lambda v: jnp.where(lane == LANES - 1, 0.0, v), ar)
+            wx = each(lambda p, q: half * (p + q), a, ar)
+            wl = level.left(wx)
+            if level.wrap:
+                wl = each(lambda v, p: jnp.where(lane == 0, half * p, v), wl, a)
+            wy = each(lambda p, q: half * (p + q), a, level.get(coef, z, row + 1))
+            wd = each(lambda p, q: half * (p + q), a, level.get(coef, z, row - 1))
+            wz = zface(z, row)
+            wb = level.get(level.wz, z - 1, row)
+            c = level.get(level.dinv, z, row)
+            den = each(lambda p, q, r, s, t_, u_, v_: p + q + r + s + t_ + u_ + v_, wx, wl, wy, wd, wz, wb, c)
+            inside = each(lambda v: v > 0.0, c)
+            dinv = each(lambda m, v: jnp.where(m, 1.0 / jnp.where(m, v, 1.0), 0.0), inside, den)
+            f = each(lambda v, w: v * w, level.get(level.f, z, row), dinv)
+            if level.wrap:
+                wx = each(lambda v: jnp.where(lane == LANES - 1, 0.0, v), wx)
+            level.put(level.wx, z, row, wx)
+            level.put(level.wy, z, row, wy)
+            level.put(level.wz, z, row, wz)
+            level.put(level.dinv, z, row, dinv)
+            level.put(level.f, z, row, f)
+        return carry
+
+    lax.fori_loop(1, planes + 1, body, 0)
+
+
+def neighbours(level, src, z, row):
+    u = level.get(src, z, row)
+    wx = level.get(level.wx, z, row)
+    total = each(lambda w, v: w * v, wx, level.right(u))
+    total = each(lambda s, v: s + v, total, level.left(each(lambda w, v: w * v, wx, u)))
+    mac = lambda s, w, v: s + w * v
+    total = each(mac, total, level.get(level.wy, z, row), level.get(src, z, row + 1))
+    total = each(mac, total, level.get(level.wy, z, row - 1), level.get(src, z, row - 1))
+    total = each(mac, total, level.get(level.wz, z, row), level.get(src, z + 1, row))
+    total = each(mac, total, level.get(level.wz, z - 1, row), level.get(src, z - 1, row))
+    return u, total
+
+
+def scaled_residual(level, src, z, row):
+    u, total = neighbours(level, src, z, row)
+    f = level.get(level.f, z, row)
+    dinv = level.get(level.dinv, z, row)
+    return u, dinv, each(lambda f_, d_, s, v: f_ + d_ * s - v, f, dinv, total, u)
+
+
+def sweep(level, src, dst, planes, first, last, weights):
+    keep, gain = weights
+
+    def body(z, carry):
+        for t in range(first, last):
+            row = 8 * t
+            u, _, r = scaled_residual(level, src, z, row)
+            if keep == 0.0:
+                d = each(lambda v: gain * v, r)
+            else:
+                d = each(lambda p, v: keep * p + gain * v, level.get(level.d, z, row), r)
+            level.put(level.d, z, row, d)
+            level.put(dst, z, row, each(lambda p, v: p + v, u, d))
+        return carry
+
+    lax.fori_loop(1, planes + 1, body, 0)
+
+
+def start(level, planes, first, last):
+    def body(z, carry):
+        for t in range(first, last):
+            d = each(lambda v: v * (1.0 / THETA), level.get(level.f, z, 8 * t))
+            level.put(level.d, z, 8 * t, d)
+            level.put(level.u, z, 8 * t, d)
+        return carry
+
+    lax.fori_loop(1, planes + 1, body, 0)
+
+
+def presmooth(level, planes, first, last, degree):
+    start(level, planes(0), first, last)
+    src, dst = level.u, level.v
+    for step, weights in enumerate(chebyshev(degree)[1:], 1):
+        sweep(level, src, dst, planes(step), first, last, weights)
+        src, dst = dst, src
+    return src, dst
+
+
+def postsmooth(level, src, dst, planes, first, last, degree):
+    for step, weights in enumerate(chebyshev(degree)):
+        sweep(level, src, dst, planes(step), first, last, weights)
+        src, dst = dst, src
+    return src, dst
+
+
+def residual_pair(level, src, k, first, last, buf):
+    for t in range(first, last):
+        parts = []
+        for z in (2 * k + 1, 2 * k + 2):
+            one = Level((level.wx, level.wy, level.wz, level.f, level.dinv, level.u, level.v, level.d), level.wrap)
+            _, dinv, r = scaled_residual(one, src, z, 8 * t)
+            ok = dinv[0] > 0.0
+            parts.append(jnp.where(ok, r[0], 0.0) / jnp.where(ok, dinv[0], 1.0))
+        buf[8 * (t - first) : 8 * (t - first) + 8, :] = parts[0] + parts[1]
+
+
+def pair_rows(out_rows, in_rows, out_offset, in_offset, count):
+    r, c = iota(out_rows, in_rows, 0) - out_offset, iota(out_rows, in_rows, 1) - in_offset
+    hit = (r >= 0) & (r < count) & ((c == 2 * r) | (c == 2 * r + 1))
+    return jnp.where(hit, 1.0, 0.0).astype(F32)
+
+
+def pair_lanes(in_lanes, out_lanes, in_offset, out_offset, count, weight):
+    r, c = iota(in_lanes, out_lanes, 0) - in_offset, iota(in_lanes, out_lanes, 1) - out_offset
+    hit = (c >= 0) & (c < count) & ((r == 2 * c) | (r == 2 * c + 1))
+    return jnp.where(hit, weight, 0.0).astype(F32)
+
+
+def interp(fine, coarse):
+    own = jnp.right_shift(fine, 1)
+    other = own + 2 * (fine - 2 * own) - 1
+    return jnp.where(coarse == own, 0.75, 0.0) + jnp.where(coarse == other, 0.25, 0.0)
+
+
+def pack(entries, limit=LANES):
+    where, tile, offset = {}, 0, 0
+    for key, n in entries:
+        if n <= 0:
+            continue
+        if offset + n > limit:
+            tile, offset = tile + 1, 0
+        where[key] = (tile, offset, n)
+        offset += n
+    return where, tile + 1
+
+
+def rows_of(entries):
+    where, offset = {}, 16
+    for key, n in entries:
+        if n <= 0:
+            continue
+        where[key] = (offset, n)
+        offset += n
+    return where, -(-(offset + 16) // 8) * 8
+
+
+def before_rows(ref, place, height):
+    if place is None:
+        return jnp.zeros((height, LANES), F32)
+    offset, n = place
+    base = offset + n - height
+    value = ref[base : base + height, :]
+    return jnp.where(iota(height, LANES, 0) >= height - n, value, 0.0)
+
+
+def after_rows(ref, place, height):
+    if place is None:
+        return jnp.zeros((height, LANES), F32)
+    offset, n = place
+    value = ref[offset : offset + height, :]
+    return jnp.where(iota(height, LANES, 0) < n, value, 0.0)
+
+
+HALO = 4
+HALO1 = 10
+ROW0, ROW1, ROW2 = 16, 24, 8
+LANE1 = 16
+
+
+class Plan:
+    def __init__(self, z, y, x):
+        self.z, self.y, self.x = z, y, x
+        z1 = z // 2
+        self.z1, self.y1, self.x1 = z1, y // 2, x // 2
+        reach = lambda p, n: n if p < z else max(0, n - (p - z + 1))
+        self.a0 = [(("a", p), reach(p, HALO + 1)) for p in range(z + HALO + 1)]
+        self.c0 = [(("c", p), reach(p, HALO)) for p in range(z + HALO)]
+        self.f0 = [(("f", p), reach(p, HALO)) for p in range(z + HALO)]
+        self.u0 = [(("u", p), reach(p, HALO)) for p in range(z + HALO)]
+        far = lambda o, j, n: n if o == 0 else max(0, min(n, n + 2 - (z1 - j)))
+        sides = [(o, j) for o in (0, 1) for j in range(z1)]
+        self.sides = sides
+        self.ac1 = [(("ac", o, j), far(o, j, HALO1 + 1)) for o, j in sides]
+        self.a1 = [(("a1", o, j), far(o, j, HALO1 + 1)) for o, j in sides]
+        self.c1 = [(("c1", o, j), far(o, j, HALO1)) for o, j in sides]
+        self.f1 = [(("f1", o, j), far(o, j, HALO1)) for o, j in sides]
+        self.fp = [(("fp", j), HALO1) for j in range(z1)]
+        self.yrows, self.ycount = rows_of(self.a0 + self.c0 + self.f0 + self.ac1)
+        self.yrows2, self.ycount2 = rows_of(self.u0 + self.fp)
+        self.x0, t0 = pack(self.a0 + self.c0 + self.f0)
+        self.x1m, t1 = pack(self.a1 + self.c1)
+        self.xu, tu = pack(self.u0)
+        self.xf, tf = pack(self.f1)
+        self.e0, self.e1 = y + 16, y // 2 + 32
+        self.xcount = t0 * self.e0 + t1 * self.e1
+        self.xcount2 = tu * self.e0 + tf * self.e1
+        self.xbase1, self.xbase2 = t0 * self.e0, tu * self.e0
+        self.tiles = (t0, t1, tu, tf)
+        self.r0, self.r1 = y + 32, y // 2 + 48
+        self.t0, self.t1 = (1, self.r0 // 8 - 1), (1, self.r1 // 8 - 1)
+
+
+def plane_of(plan, key, core, coeff, rhs, shift, zrecv):
+    kind, p = key
+    own = {"a": coeff, "f": rhs, "c": shift}[kind]
+    if p < plan.z:
+        return lambda rows: own[p + core * (plan.z - 1 - 2 * p), rows, :]
+    base = {"a": 0, "c": HALO + 1, "f": 2 * HALO + 1}[kind]
+    return lambda rows: zrecv[base + p - plan.z, rows, :]
+
+
+def zpack(plan):
+    def kernel(coeff, rhs, shift, out):
+        core = lax.axis_index("pz")
+        i = 0
+        for ref, n in ((coeff, HALO + 1), (shift, HALO), (rhs, HALO)):
+            for j in range(n):
+                p = plan.z - 1 - j
+                out[i] = ref[p + core * (plan.z - 1 - 2 * p)]
+                i += 1
+
+    return call(kernel, shape(3 * HALO + 1, plan.y, plan.x), ins=3)
+
+
+def restrict_coefficients(plan):
+    def kernel(coeff, shift, out):
+        core = lax.axis_index("pz")
+        ry = pair_rows(plan.y1, plan.y, 0, 0, plan.y1)
+        ra = pair_lanes(LANES, LANES, 0, 0, plan.x1, 0.125)
+        rc = pair_lanes(LANES, LANES, 0, plan.x1, plan.x1, 0.125)
+        for k in range(plan.z1):
+            i = 2 * k + core * (plan.z - 2 - 4 * k)
+            a = dot(dot(ry, coeff[i] + coeff[i + 1]), ra)
+            c = dot(dot(ry, shift[i] + shift[i + 1]), rc)
+            out[k] = a + c
+
+    return call(kernel, shape(plan.z1, plan.y1, LANES), ins=2)
+
+
+def ypack(plan):
+    def kernel(coeff, rhs, shift, zrecv, ac, aco, up, down):
+        core = lax.axis_index("pz")
+        for key, (offset, n) in plan.yrows.items():
+            if key[0] == "ac":
+                ref = (ac, aco)[key[1]]
+                get, height = (lambda rows, ref=ref, j=key[2]: ref[j, rows, :]), plan.y1
+            else:
+                get, height = plane_of(plan, key, core, coeff, rhs, shift, zrecv), plan.y
+            up[offset : offset + n, :] = get(slice(height - n, height))
+            down[offset : offset + n, :] = get(slice(0, n))
+
+    out = shape(plan.ycount, LANES)
+    return call(kernel, [out, out], ins=6)
+
+
+def send_lanes(out, base, extent, tile, items, rows):
+    start_row = base + tile * extent
+    for height, part in rows:
+        lane = iota(height, LANES, 1)
+        total = jnp.zeros((height, LANES), F32)
+        for get, first, n, offset in items:
+            value = roll(get(part), offset - first)
+            total = jnp.where((lane >= offset) & (lane < offset + n), value, total)
+        out[start_row : start_row + height, :] = total
+        start_row += height
+
+
+def xpack(plan):
+    def kernel(coeff, rhs, shift, zrecv, ac, aco, before, after, up, down):
+        core = lax.axis_index("pz")
+
+        def get0(key):
+            plane = plane_of(plan, key, core, coeff, rhs, shift, zrecv)
+            place = plan.yrows.get(key)
+            return lambda part: (
+                before_rows(before, place, 8) if part == 0
+                else after_rows(after, place, 8) if part == 2
+                else plane(slice(0, plan.y))
+            )
+
+        def get1(key):
+            place = plan.yrows.get(("ac",) + key[1:])
+            ref = (ac, aco)[key[1]]
+            return lambda part: (
+                before_rows(before, place, 16) if part == 0
+                else after_rows(after, place, 16) if part == 2
+                else ref[key[2]]
+            )
+
+        for tile in range(plan.tiles[0]):
+            keys = [(k, o, n) for k, (t, o, n) in plan.x0.items() if t == tile]
+            rows = ((8, 0), (plan.y, 1), (8, 2))
+            send_lanes(up, 0, plan.e0, tile, [(get0(k), plan.x - n, n, o) for k, o, n in keys], rows)
+            send_lanes(down, 0, plan.e0, tile, [(get0(k), 0, n, o) for k, o, n in keys], rows)
+        for tile in range(plan.tiles[1]):
+            keys = [(k, o, n) for k, (t, o, n) in plan.x1m.items() if t == tile]
+            rows = ((16, 0), (plan.y1, 1), (16, 2))
+            side = lambda k: plan.x1 if k[0] == "c1" else 0
+            send_lanes(up, plan.xbase1, plan.e1, tile, [(get1(k), side(k) + plan.x1 - n, n, o) for k, o, n in keys], rows)
+            send_lanes(down, plan.xbase1, plan.e1, tile, [(get1(k), side(k), n, o) for k, o, n in keys], rows)
+
+    out = shape(plan.xcount, LANES)
+    return call(kernel, [out, out], ins=8)
+
+
+def ypack2(plan):
+    def kernel(u, zrecv, f, up, down, pair):
+        for j in range(plan.z1):
+            base = HALO * plan.y + j * plan.y1
+            pair[j] = f[j] + zrecv[base : base + plan.y1, :]
+        for key, (offset, n) in plan.yrows2.items():
+            if key[0] == "fp":
+                get, height = (lambda rows, j=key[1]: pair[j, rows, :]), plan.y1
+            elif key[1] < plan.z:
+                get, height = (lambda rows, p=key[1]: u[p, rows, :]), plan.y
+            else:
+                base = (key[1] - plan.z) * plan.y
+                get, height = (lambda rows, b=base: zrecv[b + rows.start : b + rows.stop, :]), plan.y
+            up[offset : offset + n, :] = get(slice(height - n, height))
+            down[offset : offset + n, :] = get(slice(0, n))
+
+    out = shape(plan.ycount2, LANES)
+    return call(kernel, [out, out, shape(plan.z1, plan.y1, LANES)], ins=3)
+
+
+def u_plane(plan, p, u, zrecv):
+    if p < plan.z:
+        return u[p]
+    return zrecv[(p - plan.z) * plan.y : (p - plan.z + 1) * plan.y, :]
+
+
+def xpack2(plan):
+    def kernel(u, zrecv, pair, before, after, up, down):
+        def get0(key):
+            place = plan.yrows2.get(key)
+            return lambda part: (
+                before_rows(before, place, 8) if part == 0
+                else after_rows(after, place, 8) if part == 2
+                else u_plane(plan, key[1], u, zrecv)
+            )
+
+        def get1(key):
+            place = plan.yrows2.get(("fp", key[2]))
+            return lambda part: (
+                before_rows(before, place, 16) if part == 0
+                else after_rows(after, place, 16) if part == 2
+                else pair[key[2]]
+            )
+
+        for tile in range(plan.tiles[2]):
+            keys = [(k, o, n) for k, (t, o, n) in plan.xu.items() if t == tile]
+            rows = ((8, 0), (plan.y, 1), (8, 2))
+            send_lanes(up, 0, plan.e0, tile, [(get0(k), plan.x - n, n, o) for k, o, n in keys], rows)
+            send_lanes(down, 0, plan.e0, tile, [(get0(k), 0, n, o) for k, o, n in keys], rows)
+        for tile in range(plan.tiles[3]):
+            keys = [(k, o, n) for k, (t, o, n) in plan.xf.items() if t == tile]
+            rows = ((16, 0), (plan.y1, 1), (16, 2))
+            send_lanes(up, plan.xbase2, plan.e1, tile, [(get1(k), k[1] * plan.x1 + plan.x1 - n, n, o) for k, o, n in keys], rows)
+            send_lanes(down, plan.xbase2, plan.e1, tile, [(get1(k), k[1] * plan.x1, n, o) for k, o, n in keys], rows)
+
+    out = shape(plan.xcount2, LANES)
+    return call(kernel, [out, out], ins=5)
+
+
+def zero(*refs):
+    for ref in refs:
+        def body(z, carry, ref=ref):
+            ref[z] = jnp.zeros(ref.shape[1:], F32)
+            return carry
+        lax.fori_loop(0, ref.shape[0], body, 0)
+
+
+def side_lanes(plan, place, before, after):
+    if place is None:
+        return jnp.zeros((plan.e0, LANES), F32)
+    tile, offset, n = place
+    rows = slice(tile * plan.e0, (tile + 1) * plan.e0)
+    lane = iota(plan.e0, LANES, 1)
+    value = jnp.where(lane < n, roll(after[rows, :], -offset), 0.0)
+    return jnp.where(lane >= LANES - n, roll(before[rows, :], -n - offset), value)
+
+
+def fill0(plan, dst, p, plane, yplace, yb, ya, xplace, xb, xa):
+    top, own = ROW0 - 8, plan.y
+    dst[p + 1, top:ROW0, 0:LANES] = before_rows(yb, yplace, 8)
+    dst[p + 1, ROW0 : ROW0 + own, 0:LANES] = plane
+    dst[p + 1, ROW0 + own : ROW0 + own + 8, 0:LANES] = after_rows(ya, yplace, 8)
+    dst[p + 1, top : top + plan.e0, LANES : 2 * LANES] = side_lanes(plan, xplace, xb, xa)
+
+
+def level0(plan, level, core, coeff, rhs, shift, zrecv, yb, ya, xb, xa):
+    zero(level.u, level.v)
+    for kind, dst, planes in (("a", level.v, plan.z + HALO + 1), ("c", level.dinv, plan.z + HALO), ("f", level.f, plan.z + HALO)):
+        for p in range(planes):
+            key = (kind, p)
+            plane = plane_of(plan, key, core, coeff, rhs, shift, zrecv)(slice(0, plan.y))
+            fill0(plan, dst, p, plane, plan.yrows.get(key), yb, ya, plan.x0.get(key), xb, xa)
+    setup(level, 1.0, plan.z + HALO, *plan.t0, level.v)
+
+
+def level0_scratch(plan):
+    return [vmem(plan.z + HALO + 2, plan.r0, 2 * LANES)] * 8
+
+
+def fill1(plan, dst, p, own, own_first, yplace, yb, ya, xplace, base, xb, xa):
+    tile, offset, n = xplace
+    row = ROW1 - 16
+    start_row = base + tile * plan.e1
+    for height, value in ((16, before_rows(yb, yplace, 16)), (plan.y1, own), (16, after_rows(ya, yplace, 16))):
+        lane = iota(height, LANES, 1)
+        total = jnp.where((lane >= LANE1) & (lane < LANE1 + plan.x1), roll(value, LANE1 - own_first), 0.0)
+        left = roll(xb[start_row : start_row + height, :], LANE1 - n - offset)
+        right = roll(xa[start_row : start_row + height, :], LANE1 + plan.x1 - offset)
+        total = jnp.where((lane >= LANE1 - n) & (lane < LANE1), left, total)
+        total = jnp.where((lane >= LANE1 + plan.x1) & (lane < LANE1 + plan.x1 + n), right, total)
+        dst[p + 1, row : row + height, :] = total
+        row, start_row = row + height, start_row + height
+
+
+def down0(plan):
+    def kernel(coeff, rhs, shift, zrecv, yb, ya, xb, xa, u_out, f_out, z_out, *scratch):
+        buf, scratch = scratch[0], scratch[1:]
+        core = lax.axis_index("pz")
+        level = Level(scratch, False)
+        level0(plan, level, core, coeff, rhs, shift, zrecv, yb, ya, xb, xa)
+        src, _ = presmooth(level, lambda s: plan.z + HALO - s, *plan.t0, DEG)
+
+        def keep(z, carry):
+            u_out[z] = src[z + 1, ROW0 : ROW0 + plan.y, 0:LANES]
+            return carry
+
+        lax.fori_loop(0, plan.z, keep, 0)
+        for j in range(HALO):
+            z_out[j * plan.y : (j + 1) * plan.y, :] = src[plan.z - j, ROW0 : ROW0 + plan.y, 0:LANES]
+        ry = pair_rows(plan.y1, plan.y, 0, 0, plan.y1)
+        rx = pair_lanes(LANES, LANES, 0, 0, plan.x1, 0.125)
+        ro = pair_lanes(LANES, LANES, 0, plan.x1, plan.x1, 0.125)
+
+        def residual(k, carry):
+            residual_pair(level, src, k, ROW0 // 8, (ROW0 + plan.y) // 8, buf)
+            part = dot(ry, buf[...])
+            f_out[k] = dot(part, rx)
+            row = pl.multiple_of(HALO * plan.y + k * plan.y1, 8)
+            z_out[pl.ds(row, plan.y1), :] = dot(part, ro)
+            return carry
+
+        lax.fori_loop(0, plan.z1, residual, 0)
+
+    outs = [
+        shape(plan.z, plan.y, LANES),
+        shape(plan.z1, plan.y1, LANES),
+        shape(HALO * plan.y + plan.z1 * plan.y1, LANES),
+    ]
+    return call(kernel, outs, [vmem(plan.y, LANES)] + level0_scratch(plan), ins=8)
+
+
+def down1(plan):
+    planes, z2, y2, x2 = 2 * plan.z1, plan.z1 // 2, plan.y1 // 2, plan.x1 // 2
+
+    def kernel(ac, aco, yb, ya, xb, xa, pair, yb2, ya2, xb2, xa2, wx, wy, wz, f, dinv, u_out, message, u, d, buf):
+        level = Level((wx, wy, wz, f, dinv, u, u_out, d), False)
+        zero(u, u_out)
+        for o, j in plan.sides:
+            p = j if o == 0 else planes - 1 - j
+            ref = (ac, aco)[o]
+            place = plan.yrows[("ac", o, j)]
+            fill1(plan, u_out, p, ref[j], 0, place, yb, ya, plan.x1m[("a1", o, j)], plan.xbase1, xb, xa)
+            wide = (place[0], place[1])
+            fill1c(plan, dinv, p, ref[j], wide, yb, ya, plan.x1m[("c1", o, j)], plan.xbase1, xb, xa)
+            fill1(plan, f, p, pair[j], o * plan.x1, plan.yrows2[("fp", j)], yb2, ya2, plan.xf[("f1", o, j)], plan.xbase2, xb2, xa2)
+        setup(level, 0.25, planes, *plan.t1, u_out)
+        src, _ = presmooth(level, lambda s: planes, *plan.t1, DEG)
+        assert src is u_out
+        ry = pair_rows(y2, plan.y1, 0, 0, y2)
+        totals = [jnp.zeros((y2, LANES), F32) for _ in range(3)]
+        for k in range(z2):
+            residual_pair(level, src, k, ROW1 // 8, (ROW1 + plan.y1) // 8, buf)
+            own = dot(ry, ac[2 * k] + ac[2 * k + 1])
+            for i, (part, first) in enumerate(((dot(ry, buf[...]), LANE1), (own, 0), (own, plan.x1))):
+                totals[i] += dot(part, pair_lanes(LANES, LANES, first, k * x2, x2, 0.125))
+        for i in range(3):
+            message[i * y2 : (i + 1) * y2, :] = totals[i]
+
+    big = (planes + 2, plan.r1, LANES)
+    outs = [shape(*big)] * 6 + [shape(3 * y2, LANES)]
+    return call(kernel, outs, [vmem(*big)] * 2 + [vmem(plan.y1, LANES)], ins=11)
+
+
+def fill1c(plan, dst, p, own, yplace, yb, ya, xplace, base, xb, xa):
+    fill1(plan, dst, p, own, plan.x1, yplace, yb, ya, xplace, base, xb, xa)
+
+
+def prolong(level, base, out, tmp, planes, py, px):
+    def body(z, carry):
+        tmp[z] = dot(dot(py, base[z]), px)
+        return carry
+
+    lax.fori_loop(1, planes + 1, body, 0)
+
+
+def correct(level, src, dst, tmp, fine_planes, first, last):
+    for odd in (0, 1):
+        def body(k, carry, odd=odd):
+            z = 2 * k + 1 + odd
+            for t in range(first, last):
+                row = 8 * t
+                near, far = level.get(tmp, k + 1, row), level.get(tmp, k + 2 * odd, row)
+                dinv, u = level.get(level.dinv, z, row), level.get(src, z, row)
+                new = each(lambda n, f, m, v: v + jnp.where(m > 0.0, 0.75 * n + 0.25 * f, 0.0), near, far, dinv, u)
+                level.put(dst, z, row, new)
+            return carry
+
+        lax.fori_loop(0, fine_planes // 2, body, 0)
+
+
+def coarse(plan, devices_y, devices_x):
+    planes1 = 2 * plan.z1
+    z2, y2, x2 = plan.z1 // 2, plan.y1 // 2, plan.x1 // 2
+    planes2, rows2, lanes2 = 2 * z2, devices_y * y2, devices_x * x2
+    planes3, rows3, lanes3 = planes2 // 2, rows2 // 2, lanes2 // 2
+    h2, h3 = rows2 + 16, rows3 + 16
+    t2, t3 = (1, h2 // 8 - 1), (1, h3 // 8 - 1)
+
+    def kernel(mine, other, wx, wy, wz, f, dinv, u_in, e1, *scratch):
+        l2, l3, (u1, d1, buf, tmp3, tmp2) = scratch[:8], scratch[8:16], scratch[16:]
+        two, three = Level(l2, True), Level(l3, False)
+        zero(two.u, two.v, *l3)
+        lane = iota(y2, LANES, 1)
+        for i, dst in enumerate((two.f, two.v, two.dinv)):
+            for ref, plane in ((mine, lambda k: k), (other, lambda k: planes2 - 1 - k)):
+                for k in range(z2):
+                    for qy in range(devices_y):
+                        total = jnp.zeros((y2, LANES), F32)
+                        for qx in range(devices_x):
+                            value = ref[qy * devices_x + qx, i * y2 : (i + 1) * y2, :]
+                            value = roll(value, x2 * (qx - k))
+                            total = jnp.where((lane >= x2 * qx) & (lane < x2 * qx + x2), value, total)
+                        row = ROW2 + qy * y2
+                        dst[plane(k) + 1, row : row + y2, :] = total
+        ry = pair_rows(h3, rows2, ROW2, 0, rows3)
+        rx = pair_lanes(LANES, LANES, 0, 0, lanes3, 0.125)
+        for k in range(planes3):
+            for src, dst in ((two.v, three.v), (two.dinv, three.dinv)):
+                value = src[2 * k + 1, ROW2 : ROW2 + rows2, :] + src[2 * k + 2, ROW2 : ROW2 + rows2, :]
+                dst[k + 1] = dot(dot(ry, value), rx)
+        setup(two, 0.25**2, planes2, *t2, two.v)
+        src2, dst2 = presmooth(two, lambda s: planes2, *t2, DEG)
+
+        def residual(k, carry):
+            residual_pair(two, src2, k, *t2, buf)
+            three.f[k + 1] = dot(dot(ry, buf[...]), rx)
+            return carry
+
+        lax.fori_loop(0, planes3, residual, 0)
+        setup(three, 0.25**3, planes3, *t3, three.v)
+        src3, _ = presmooth(three, lambda s: planes3, *t3, CDEG)
+
+        zero(tmp3, tmp2)
+        py = interp(iota(h2, h3, 0) - ROW2, iota(h2, h3, 1) - ROW2)
+        px = interp(iota(LANES, LANES, 1), iota(LANES, LANES, 0))
+        prolong(two, src3, None, tmp3, planes3, py, px)
+        correct(two, src2, src2, tmp3, planes2, *t2)
+        src2, _ = postsmooth(two, src2, dst2, lambda s: planes2, *t2, DEG)
+
+        me_y, me_x = lax.axis_index("py"), lax.axis_index("px")
+        py = interp(iota(plan.r1, h2, 0) - ROW1 + me_y * plan.y1, iota(plan.r1, h2, 1) - ROW2)
+        px = interp(iota(LANES, LANES, 1) - LANE1 + me_x * plan.x1, iota(LANES, LANES, 0))
+        one = Level((wx, wy, wz, f, dinv, u1, e1, d1), False)
+        zero(u1, e1)
+        prolong(one, src2, None, tmp2, planes2, py, px)
+        correct(one, u_in, e1, tmp2, planes1, *plan.t1)
+        src1, _ = postsmooth(one, e1, u1, lambda s: min(planes1, plan.z1 + 6 - s), *plan.t1, DEG)
+        assert src1 is e1
+
+    big1 = (planes1 + 2, plan.r1, LANES)
+    scratch = [vmem(planes2 + 2, h2, LANES)] * 8 + [vmem(planes3 + 2, h3, LANES)] * 8
+    scratch += [vmem(*big1)] * 2 + [vmem(rows2, LANES), vmem(planes3 + 2, h2, LANES), vmem(planes2 + 2, plan.r1, LANES)]
+    return call(kernel, shape(*big1), scratch, ins=8)
+
+
+def up0(plan):
+    planes = plan.z + HALO
+    few = HALO // 2 + plan.z1 + 1
+
+    def kernel(coeff, rhs, shift, zrecv, yb, ya, xb, xa, u_in, zrecv2, yb2, ya2, xb2, xa2, e1, out, tmp, *scratch):
+        core = lax.axis_index("pz")
+        level = Level(scratch, False)
+        level0(plan, level, core, coeff, rhs, shift, zrecv, yb, ya, xb, xa)
+        for p in range(planes):
+            key = ("u", p)
+            fill0(plan, level.u, p, u_plane(plan, p, u_in, zrecv2), plan.yrows2.get(key), yb2, ya2, plan.xu.get(key), xb2, xa2)
+        tmp[0] = jnp.zeros(tmp.shape[1:], F32)
+        fine = iota(plan.r0, plan.r1, 0) - ROW0
+        py = interp(fine, iota(plan.r0, plan.r1, 1) - ROW1)
+        lane = iota(LANES, 2 * LANES, 1)
+        lane = jnp.where(lane < LANES + LANES // 2, lane, lane - 2 * LANES)
+        px = interp(lane, iota(LANES, 2 * LANES, 0) - LANE1)
+        prolong(level, e1, None, tmp, few, py, px)
+        correct(level, level.u, level.u, tmp, planes, *plan.t0)
+        src, _ = postsmooth(level, level.u, level.v, lambda s: planes - 1 - s, *plan.t0, DEG)
+        for p in range(plan.z):
+            out[p + core * (plan.z - 1 - 2 * p)] = src[p + 1, ROW0 : ROW0 + plan.y, 0:LANES]
+
+    return call(kernel, shape(plan.z, plan.y, LANES), [vmem(few + 2, plan.r0, 2 * LANES)] + level0_scratch(plan), ins=15)
+
+
+def swap(value, axis):
+    return lax.ppermute(value, axis, [(0, 1), (1, 0)])
+
+
+def shifted(up, down, axis):
+    n = lax.axis_size(axis)
+    before = lax.ppermute(up, axis, [(i, i + 1) for i in range(n - 1)])
+    after = lax.ppermute(down, axis, [(i + 1, i) for i in range(n - 1)])
+    return before, after
+
+
+def local(rhs, coeff, shift):
+    plan = Plan(*rhs.shape)
+    zrecv = swap(zpack(plan)(coeff, rhs, shift), "pz")
+    ac = restrict_coefficients(plan)(coeff, shift)
+    aco = swap(ac, "pz")
+    yb, ya = shifted(*ypack(plan)(coeff, rhs, shift, zrecv, ac, aco), "py")
+    xb, xa = shifted(*xpack(plan)(coeff, rhs, shift, zrecv, ac, aco, yb, ya), "px")
+    fine = (coeff, rhs, shift, zrecv, yb, ya, xb, xa)
+    u, f, z_out = down0(plan)(*fine)
+    zrecv2 = swap(z_out, "pz")
+    up, down, pair = ypack2(plan)(u, zrecv2, f)
+    yb2, ya2 = shifted(up, down, "py")
+    xb2, xa2 = shifted(*xpack2(plan)(u, zrecv2, pair, yb2, ya2), "px")
+    *one, message = down1(plan)(ac, aco, yb, ya, xb, xa, pair, yb2, ya2, xb2, xa2)
+    ny, nx = lax.axis_size("py"), lax.axis_size("px")
+    mine = lax.all_to_all(jnp.broadcast_to(message[None], (ny * nx,) + message.shape), ("py", "px"), 0, 0)
+    other = swap(mine, "pz")
+    e1 = coarse(plan, ny, nx)(mine, other, *one)
+    return up0(plan)(*fine, u, zrecv2, yb2, ya2, xb2, xa2, e1)
 
 
 lower_bound = 0.4
@@ -95,7 +837,7 @@
     return stacked.reshape(shape)
 
 
-def prolong(padded):
+def prolong_all(padded):
     for axis_index in range(3):
         padded = refine_axis(padded, axis_index)
     return padded
@@ -113,7 +855,7 @@
     return extended(field, (("pz", 0), ("py", 1), ("px", 2)), 1)
 
 
-def local(rhs, coeff, shift):
+def general(rhs, coeff, shift):
     coeff_pad_zero = extended(coeff, (("pz", 0), ("py", 1), ("px", 2)), 1)
     level_zero = make_level(coeff_pad_zero, shift, 1.0)
     field = smooth(None, rhs, level_zero, DEG, fine_pad)
@@ -139,15 +881,16 @@
     coarse_field = smooth(None, coarse_source, coarse_level, CDEG, coarse_face_pad)
     padded = extended(coarse_field, (("pz", 0), ("py", 1), ("px", 2)), 1)
     for depth in range(LEVELS - 1, 0, -1):
-        field = fields[depth] + prolong(padded)
+        field = fields[depth] + prolong_all(padded)
         field = smooth(field, sources[depth], levels_list[depth], DEG, face_pad)
         padded = extended(field, (("pz", 0), ("py", 1), ("px", 2)), 1)
-    field = fields[0] + prolong(padded)
+    field = fields[0] + prolong_all(padded)
     field = smooth(field, rhs, level_zero, DEG, fine_pad)
     return field
 
 
 def solution(mesh):
-    in_specs = (P("pz", "py", "px"), P("pz", "py", "px"), P("pz", "py", "px"))
-    out_specs = P("pz", "py", "px")
-    return jax.shard_map(local, mesh=mesh, in_specs=in_specs, out_specs=out_specs, check_vma=False)
+    spec = P("pz", "py", "px")
+    body = local if mesh.shape["pz"] == 2 else general
+
+    return jax.shard_map(body, mesh=mesh, in_specs=(spec,) * 3, out_specs=spec, check_vma=False)

time: 1440 us -> 219 us (0.15); the launches traced: 1420 us -> 218 us
  starting transfers between devices: 440 us -> 20.7 us
  local copies, waits for them, and re-layouts: 369 us -> 6.95 us
  waiting for transfers between devices: 362 us -> 38.5 us
  other arithmetic: 246 us -> 0 us
  Pallas kernels: 0 us -> 129 us
  blocking collectives: 0 us -> 22.8 us
    ppermute x228 -> x12, starting transfers between devices: 440 us -> 20.7 us  [the longest x4 14.9 us: shifted(): before = lax.ppermute(up, axis, [(i, i + 1) for i in range(n - 1)])]
    ppermute x228 -> x12, waiting for transfers between devices: 362 us -> 38.5 us  [the longest x4 20.6 us: shifted(): after = lax.ppermute(down, axis, [(i + 1, i) for i in range(n - 1)])]
    reshape x7 -> x0, local copies, waits for them, and re-layouts: 224 us -> none  [the longest x5 221 us: restrict(): field.reshape(s0 // 2, 2, s1 // 2, 2, s2 // 2, 2).mean(axis=(1, 3, 5))]
    pallas_call x0 -> x10, Pallas kernels: none -> 129 us  [the longest x1 33.7 us: local(): return up0(plan)(*fine, u, zrecv2, yb2, ya2, xb2, xa2, e1)]
    add x31 -> x0, other arithmetic: 107 us -> none  [the longest x28 103 us: smooth(): field = field + update]
    reduce_sum x9 -> x0, other arithmetic: 83.8 us -> none  [restrict(): field.reshape(s0 // 2, 2, s1 // 2, 2, s2 // 2, 2).mean(axis=(1, 3, 5))]
    slice x94 -> x0, local copies, waits for them, and re-layouts: 62 us -> none  [the longest x81 42.7 us: extended(): last = lax.slice_in_dim(array, length - width, length, axis=dim)]
    ppermute x18 -> x0, local copies, waits for them, and re-layouts: 30.3 us -> none  [the longest x9 15.3 us: extended(): after = lax.ppermute(first, axis, down)]
  transfers between devices with their start and end apart: 228 -> 12, of which waited for: 117 -> 11; matrix products, arithmetic and copies ran while one was open for 30% -> 0% of each run, Pallas kernels for 0% -> 2%
where the time goes in v1:
time: 219 us; the launch traced here: 218 us
  Pallas kernels  129 us (59%)
  waiting for transfers between devices  38.5 us (18%)
  blocking collectives  22.8 us (10%)
  starting transfers between devices  20.7 us (9%)
  local copies, waits for them, and re-layouts  6.95 us (3%)
    pallas_call x1, Pallas kernels, local(): return up0(plan)(*fine, u, zrecv2, yb2, ya2, xb2, xa2, e1)  33.7 us
    pallas_call x1, Pallas kernels, local(): e1 = coarse(plan, ny, nx)(mine, other, *one)  32.3 us
    pallas_call x1, Pallas kernels, local(): u, f, z_out = down0(plan)(*fine)  26.6 us
    all_to_all x1, blocking collectives, local(): lax.all_to_all(jnp.broadcast_to(message[None], (ny * nx,) + message.shape...  22.8 us
    ppermute x4, waiting for transfers between devices, shifted(): after = lax.ppermute(down, axis, [(i + 1, i) for i in range(n - 1)])  20.6 us
    ppermute x4, starting transfers between devices, shifted(): before = lax.ppermute(up, axis, [(i, i + 1) for i in range(n - 1)])  14.9 us
    pallas_call x1, Pallas kernels, local(): down1(plan)(ac, aco, yb, ya, xb, xa, pair, yb2, ya2, xb2, xa2)  14.7 us
    ppermute x4, waiting for transfers between devices, shifted(): before = lax.ppermute(up, axis, [(i, i + 1) for i in range(n - 1)])  11.8 us
  transfers between devices with their start and end apart: 12, of which 11 were waited for; matrix products, arithmetic and copies ran while one was open for 0% of the time, Pallas kernels for 2%

profile of v1, /device:TPU:0, one launch (start us, length us, event | category | flops | bytes accessed | tf_op | source)
XLA Modules:
  0.0 218.3 jit_solution(6082875841163421171)
XLA Ops:
  0.0 2.8 %shard_map.37 = f32[13,128,128]{2,1,0:T(8,128)} custom-call(f32[16,128,128]{2,1,0:T(8,128)} %coeff.11, f32[16,128,128]{2,1,0:T(8,128)} %rhs.9, f32[16,128,128]{2,1,0:T(8,128)} %shift.11), custom_call_target="tpu_custom_call" | custom-call | tf_op jit(solution)/shard_map/pallas_call | solution.py:734
  3.3 4.3 %shard_map.38.ac = f32[8,64,128]{2,1,0:T(8,128)} custom-call(f32[16,128,128]{2,1,0:T(8,128)} %coeff.11, f32[16,128,128]{2,1,0:T(8,128)} %shift.11), custom_call_target="tpu_custom_call" | custom-call | tf_op jit(solution)/shard_map/pallas_call | solution.py:735
  7.7 1.7 collective-permute-done.1.aco
  10.1 1.0 copy-done
  11.1 3.0 %shard_map.39 = (f32[424,128]{1,0:T(8,128)}, f32[424,128]{1,0:T(8,128)}) custom-call(f32[16,128,128]{2,1,0:T(8,128)} %coeff.11, f32[16,128,128]{2,1,0:T(8,128)} %rhs.9, f32[16,128,128]{2,1,0:T(8,128)} %shift.11, f32[13,128,128]{2,1,0:T(8,128)} %copy-done, f32[8,64,128]{2,1,0:T(8,128)} %shard_map.38.ac, f32[8,64,128]{2,1,0:T(8,128)} %copy-done.7), custom_call_target="tpu_custom_call" | custom-call | tf_op jit(solution)/shard_map/pallas_call | solution.py:737
  14.1 4.6 %collective-permute-start.2 = (f32[424,128]{1,0:T(8,128)}, f32[424,128]{1,0:T(8,128)S(1)}, u32[]{:S(2)}, u32[]{:S(2)}) collective-permute-start(f32[424,128]{1,0:T(8,128)} %get-tuple-element.24), channel_id=1, source_target_pairs={{0,2},{2,4},{4,6},{1,3},{3,5},{5,7},{8,10},{10,12},{12,14},{9,11},... | collective-permute-start | bytes 651272 | tf_op jit(solution)/shard_map/ppermute | solution.py:727
  18.7 1.3 collective-permute-start.3
  20.0 4.1 %collective-permute-done.2.before.yb = f32[424,128]{1,0:T(8,128)S(1)} collective-permute-done((f32[424,128]{1,0:T(8,128)}, f32[424,128]{1,0:T(8,128)S(1)}, u32[]{:S(2)}, u32[]{:S(2)}) %collective-permute-start.2) | collective-permute-done | bytes 217120 | tf_op jit(solution)/shard_map/ppermute | solution.py:727
  24.1 4.0 %collective-permute-done.3.after.ya = f32[424,128]{1,0:T(8,128)S(1)} collective-permute-done((f32[424,128]{1,0:T(8,128)}, f32[424,128]{1,0:T(8,128)S(1)}, u32[]{:S(2)}, u32[]{:S(2)}) %collective-permute-start.3) | collective-permute-done | bytes 217120 | tf_op jit(solution)/shard_map/ppermute | solution.py:728
  28.8 6.2 %shard_map.40 = (f32[576,128]{1,0:T(8,128)}, f32[576,128]{1,0:T(8,128)}) custom-call(f32[16,128,128]{2,1,0:T(8,128)} %coeff.11, f32[16,128,128]{2,1,0:T(8,128)} %rhs.9, f32[16,128,128]{2,1,0:T(8,128)} %shift.11, f32[13,128,128]{2,1,0:T(8,128)} %copy-done, f32[8,64,128]{2,1,0:T(8,128)} %shard_map.38.ac, f32[8,64,128]{2,1,0:T(8,128)} %copy-done.7, ...), custom_call_target="tpu_custom_call" | custom-call | tf_op jit(solution)/shard_map/pallas_call | solution.py:738
  35.0 3.4 %collective-permute-start.4 = (f32[576,128]{1,0:T(8,128)}, f32[576,128]{1,0:T(8,128)S(1)}, u32[]{:S(2)}, u32[]{:S(2)}) collective-permute-start(f32[576,128]{1,0:T(8,128)} %get-tuple-element.26), channel_id=1, source_target_pairs={{0,8},{8,16},{16,24},{1,9},{9,17},{17,25},{2,10},{10,18},{18,26},{... | collective-permute-start | bytes 884744 | tf_op jit(solution)/shard_map/ppermute | solution.py:727
  38.4 1.3 collective-permute-start.5
  39.7 4.6 %collective-permute-done.4.xb = f32[576,128]{1,0:T(8,128)S(1)} collective-permute-done((f32[576,128]{1,0:T(8,128)}, f32[576,128]{1,0:T(8,128)S(1)}, u32[]{:S(2)}, u32[]{:S(2)}) %collective-permute-start.4) | collective-permute-done | bytes 294944 | tf_op jit(solution)/shard_map/ppermute | solution.py:727
  44.4 8.2 %collective-permute-done.5.xa = f32[576,128]{1,0:T(8,128)S(1)} collective-permute-done((f32[576,128]{1,0:T(8,128)}, f32[576,128]{1,0:T(8,128)S(1)}, u32[]{:S(2)}, u32[]{:S(2)}) %collective-permute-start.5) | collective-permute-done | bytes 294944 | tf_op jit(solution)/shard_map/ppermute | solution.py:728
  53.3 26.6 %shard_map.41 = (f32[16,128,128]{2,1,0:T(8,128)}, f32[8,64,128]{2,1,0:T(8,128)}, f32[1024,128]{1,0:T(8,128)}) custom-call(f32[16,128,128]{2,1,0:T(8,128)} %coeff.11, f32[16,128,128]{2,1,0:T(8,128)} %rhs.9, f32[16,128,128]{2,1,0:T(8,128)} %shift.11, f32[13,128,128]{2,1,0:T(8,128)} %copy-done, f32[424,128]{1,0:T(8,128)} %copy-done.2, f32[424,128]{1,0:T(8,128)} %copy-done.3, ...), custom_call_target="tpu_custom_call" | custom-call | tf_op jit(solution)/shard_map/pallas_call | solution.py:740
  79.9 2.1 collective-permute-done.6.zrecv.zrecv2
  82.8 2.2 %shard_map.42 = (f32[184,128]{1,0:T(8,128)}, f32[184,128]{1,0:T(8,128)}, f32[8,64,128]{2,1,0:T(8,128)}) custom-call(f32[16,128,128]{2,1,0:T(8,128)} %get-tuple-element.28.u.u_in, f32[1024,128]{1,0:T(8,128)} %copy-done.1, f32[8,64,128]{2,1,0:T(8,128)} %get-tuple-element.30.f), custom_call_target="tpu_custom_call" | custom-call | tf_op jit(solution)/shard_map/pallas_call | solution.py:742
  85.1 3.5 %collective-permute-start.7 = (f32[184,128]{1,0:T(8,128)}, f32[184,128]{1,0:T(8,128)S(1)}, u32[]{:S(2)}, u32[]{:S(2)}) collective-permute-start(f32[184,128]{1,0:T(8,128)} %get-tuple-element.31), channel_id=1, source_target_pairs={{0,2},{2,4},{4,6},{1,3},{3,5},{5,7},{8,10},{10,12},{12,14},{9,11},... | collective-permute-start | bytes 282632 | tf_op jit(solution)/shard_map/ppermute | solution.py:727
  88.5 1.3 collective-permute-start.8
  89.8 1.3 collective-permute-done.7.before.yb2
  91.1 4.1 %collective-permute-done.8.after.ya2 = f32[184,128]{1,0:T(8,128)S(1)} collective-permute-done((f32[184,128]{1,0:T(8,128)}, f32[184,128]{1,0:T(8,128)S(1)}, u32[]{:S(2)}, u32[]{:S(2)}) %collective-permute-start.8) | collective-permute-done | bytes 94240 | tf_op jit(solution)/shard_map/ppermute | solution.py:728
  95.8 3.4 %shard_map.43 = (f32[336,128]{1,0:T(8,128)}, f32[336,128]{1,0:T(8,128)}) custom-call(f32[16,128,128]{2,1,0:T(8,128)} %get-tuple-element.28.u.u_in, f32[1024,128]{1,0:T(8,128)} %copy-done.1, f32[8,64,128]{2,1,0:T(8,128)} %get-tuple-element.33.pair, f32[184,128]{1,0:T(8,128)} %copy-done.8, f32[184,128]{1,0:T(8,128)} %copy-done.9), custom_call_target="tpu_custom_call" | custom-call | tf_op jit(solution)/shard_map/pallas_call | solution.py:744
  99.2 3.4 %collective-permute-start.9 = (f32[336,128]{1,0:T(8,128)}, f32[336,128]{1,0:T(8,128)S(1)}, u32[]{:S(2)}, u32[]{:S(2)}) collective-permute-start(f32[336,128]{1,0:T(8,128)} %get-tuple-element.34), channel_id=1, source_target_pairs={{0,8},{8,16},{16,24},{1,9},{9,17},{17,25},{2,10},{10,18},{18,26},{... | collective-permute-start | bytes 516104 | tf_op jit(solution)/shard_map/ppermute | solution.py:727
  102.6 1.5 collective-permute-start.10
  104.1 1.7 collective-permute-done.9.xb2
  105.8 4.3 %collective-permute-done.10.xa2 = f32[336,128]{1,0:T(8,128)S(1)} collective-permute-done((f32[336,128]{1,0:T(8,128)}, f32[336,128]{1,0:T(8,128)S(1)}, u32[]{:S(2)}, u32[]{:S(2)}) %collective-permute-start.10) | collective-permute-done | bytes 172064 | tf_op jit(solution)/shard_map/ppermute | solution.py:728
  110.8 14.7 %shard_map.44 = (f32[18,112,128]{2,1,0:T(8,128)}, f32[18,112,128]{2,1,0:T(8,128)}, f32[18,112,128]{2,1,0:T(8,128)}, f32[18,112,128]{2,1,0:T(8,128)}, f32[18,112,...) custom-call(f32[8,64,128]{2,1,0:T(8,128)} %shard_map.38.ac, f32[8,64,128]{2,1,0:T(8,128)} %copy-done.7, ...), custom_call_target="tpu_custom_call" | custom-call | tf_op jit(solution)/shard_map/pallas_call | solution.py:745
  126.3 22.8 %all_to_all.5.mine = f32[16,96,128]{2,1,0:T(8,128)S(1)} all-to-all(f32[16,96,128]{2,1,0:T(8,128)S(1)} %broadcast_in_dim.2), channel_id=1, replica_groups=mesh['px'=4,'py'=4,'pz'=2] {'py','px'}, dimensions={0} | all-to-all | bytes 1572864 | tf_op jit(solution)/shard_map/all_to_all | solution.py:747
  149.2 2.3 %collective-permute-done.11.other = f32[16,96,128]{2,1,0:T(8,128)S(1)} collective-permute-done((f32[16,96,128]{2,1,0:T(8,128)S(1)}, f32[16,96,128]{2,1,0:T(8,128)S(1)}, u32[]{:S(2)}, u32[]{:S(2)}) %collective-permute-start.11) | collective-permute-done | bytes 786464 | tf_op jit(solution)/shard_map/ppermute | solution.py:722
  151.4 0.9 copy-done.10
  152.3 32.3 %shard_map.45.e1 = f32[18,112,128]{2,1,0:T(8,128)} custom-call(f32[16,96,128]{2,1,0:T(8,128)} %copy-done.4, f32[16,96,128]{2,1,0:T(8,128)} %copy-done.10, f32[18,112,128]{2,1,0:T(8,128)} %get-tuple-element.37.wx, f32[18,112,128]{2,1,0:T(8,128)} %get-tuple-element.38.wy, f32[18,112,128]{2,1,0:T(8,128)} %get-tuple-element.39.wz, ...), custom_call_target="tpu_custom_call" | custom-call | tf_op jit(solution)/shard_map/pallas_call | solution.py:749
  184.7 33.7 %shard_map.46 = f32[16,128,128]{2,1,0:T(8,128)} custom-call(f32[16,128,128]{2,1,0:T(8,128)} %coeff.11, f32[16,128,128]{2,1,0:T(8,128)} %rhs.9, f32[16,128,128]{2,1,0:T(8,128)} %shift.11, f32[13,128,128]{2,1,0:T(8,128)} %copy-done, f32[424,128]{1,0:T(8,128)} %copy-done.2, f32[424,128]{1,0:T(8,128)} %copy-done.3, f32[576,128]{1,0:T(8,128)} %copy-done.5, ...), custom_call_target="tpu_custom_call" | custom-call | tf_op jit(solution)/shard_map/pallas_call | solution.py:750
  (30 shorter events, 5.6 us)
Async XLA Ops:
  2.8 6.6 %collective-permute-start = (f32[13,128,128]{2,1,0:T(8,128)}, f32[13,128,128]{2,1,0:T(8,128)S(1)}, u32[]{:S(2)}, u32[]{:S(2)}) collective-permute-start(f32[13,128,128]{2,1,0:T(8,128)} %shard_map.37), channel_id=1, source_target_pairs={{0,1},{1,0},{2,3},{3,2},{4,5},{5,4},{6,7},{7,6},{8,9},{9,8},{10,11... | collective-permute-start | bytes 2555912 | tf_op jit(solution)/shard_map/ppermute | solution.py:722
  7.6 1.7 collective-permute-start.1
  9.4 0.7 copy-start.7
  10.1 1.0 copy-start
  14.1 10.0 %collective-permute-start.2 = (f32[424,128]{1,0:T(8,128)}, f32[424,128]{1,0:T(8,128)S(1)}, u32[]{:S(2)}, u32[]{:S(2)}) collective-permute-start(f32[424,128]{1,0:T(8,128)} %get-tuple-element.24), channel_id=1, source_target_pairs={{0,2},{2,4},{4,6},{1,3},{3,5},{5,7},{8,10},{10,12},{12,14},{9,11},... | collective-permute-start | bytes 651272 | tf_op jit(solution)/shard_map/ppermute | solution.py:727
  18.7 9.4 %collective-permute-start.3 = (f32[424,128]{1,0:T(8,128)}, f32[424,128]{1,0:T(8,128)S(1)}, u32[]{:S(2)}, u32[]{:S(2)}) collective-permute-start(f32[424,128]{1,0:T(8,128)} %get-tuple-element.25), channel_id=1, source_target_pairs={{2,0},{4,2},{6,4},{3,1},{5,3},{7,5},{10,8},{12,10},{14,12},{11,9},... | collective-permute-start | bytes 651272 | tf_op jit(solution)/shard_map/ppermute | solution.py:728
  24.1 4.0 %copy-start.2 = (f32[424,128]{1,0:T(8,128)}, f32[424,128]{1,0:T(8,128)S(1)}, u32[]{:S(2)}) copy-start(f32[424,128]{1,0:T(8,128)S(1)} %collective-permute-done.2.before.yb) | copy-start | bytes 651268
  28.2 0.7 copy-start.3
  35.0 9.4 %collective-permute-start.4 = (f32[576,128]{1,0:T(8,128)}, f32[576,128]{1,0:T(8,128)S(1)}, u32[]{:S(2)}, u32[]{:S(2)}) collective-permute-start(f32[576,128]{1,0:T(8,128)} %get-tuple-element.26), channel_id=1, source_target_pairs={{0,8},{8,16},{16,24},{1,9},{9,17},{17,25},{2,10},{10,18},{18,26},{... | collective-permute-start | bytes 884744 | tf_op jit(solution)/shard_map/ppermute | solution.py:727
  38.4 14.1 %collective-permute-start.5 = (f32[576,128]{1,0:T(8,128)}, f32[576,128]{1,0:T(8,128)S(1)}, u32[]{:S(2)}, u32[]{:S(2)}) collective-permute-start(f32[576,128]{1,0:T(8,128)} %get-tuple-element.27), channel_id=1, source_target_pairs={{8,0},{16,8},{24,16},{9,1},{17,9},{25,17},{10,2},{18,10},{26,18},{... | collective-permute-start | bytes 884744 | tf_op jit(solution)/shard_map/ppermute | solution.py:728
  44.4 8.2 %copy-start.5 = (f32[576,128]{1,0:T(8,128)}, f32[576,128]{1,0:T(8,128)S(1)}, u32[]{:S(2)}) copy-start(f32[576,128]{1,0:T(8,128)S(1)} %collective-permute-done.4.xb) | copy-start | bytes 884740
  52.6 0.7 copy-start.6
  79.9 2.1 collective-permute-start.6
  82.0 0.8 copy-start.1
  85.1 6.0 %collective-permute-start.7 = (f32[184,128]{1,0:T(8,128)}, f32[184,128]{1,0:T(8,128)S(1)}, u32[]{:S(2)}, u32[]{:S(2)}) collective-permute-start(f32[184,128]{1,0:T(8,128)} %get-tuple-element.31), channel_id=1, source_target_pairs={{0,2},{2,4},{4,6},{1,3},{3,5},{5,7},{8,10},{10,12},{12,14},{9,11},... | collective-permute-start | bytes 282632 | tf_op jit(solution)/shard_map/ppermute | solution.py:727
  88.5 6.7 %collective-permute-start.8 = (f32[184,128]{1,0:T(8,128)}, f32[184,128]{1,0:T(8,128)S(1)}, u32[]{:S(2)}, u32[]{:S(2)}) collective-permute-start(f32[184,128]{1,0:T(8,128)} %get-tuple-element.32), channel_id=1, source_target_pairs={{2,0},{4,2},{6,4},{3,1},{5,3},{7,5},{10,8},{12,10},{14,12},{11,9},... | collective-permute-start | bytes 282632 | tf_op jit(solution)/shard_map/ppermute | solution.py:728
  91.1 4.1 %copy-start.8 = (f32[184,128]{1,0:T(8,128)}, f32[184,128]{1,0:T(8,128)S(1)}, u32[]{:S(2)}) copy-start(f32[184,128]{1,0:T(8,128)S(1)} %collective-permute-done.7.before.yb2) | copy-start | bytes 282628
  95.2 0.6 copy-start.9
  99.2 6.6 %collective-permute-start.9 = (f32[336,128]{1,0:T(8,128)}, f32[336,128]{1,0:T(8,128)S(1)}, u32[]{:S(2)}, u32[]{:S(2)}) collective-permute-start(f32[336,128]{1,0:T(8,128)} %get-tuple-element.34), channel_id=1, source_target_pairs={{0,8},{8,16},{16,24},{1,9},{9,17},{17,25},{2,10},{10,18},{18,26},{... | collective-permute-start | bytes 516104 | tf_op jit(solution)/shard_map/ppermute | solution.py:727
  102.6 7.5 %collective-permute-start.10 = (f32[336,128]{1,0:T(8,128)}, f32[336,128]{1,0:T(8,128)S(1)}, u32[]{:S(2)}, u32[]{:S(2)}) collective-permute-start(f32[336,128]{1,0:T(8,128)} %get-tuple-element.35), channel_id=1, source_target_pairs={{8,0},{16,8},{24,16},{9,1},{17,9},{25,17},{10,2},{18,10},{26,18},{... | collective-permute-start | bytes 516104 | tf_op jit(solution)/shard_map/ppermute | solution.py:728
  105.8 4.3 %copy-start.11 = (f32[336,128]{1,0:T(8,128)}, f32[336,128]{1,0:T(8,128)S(1)}, u32[]{:S(2)}) copy-start(f32[336,128]{1,0:T(8,128)S(1)} %collective-permute-done.9.xb2) | copy-start | bytes 516100
  110.1 0.7 copy-start.12
  149.1 2.3 %copy-start.4 = (f32[16,96,128]{2,1,0:T(8,128)}, f32[16,96,128]{2,1,0:T(8,128)S(1)}, u32[]{:S(2)}) copy-start(f32[16,96,128]{2,1,0:T(8,128)S(1)} %all_to_all.5.mine) | copy-start | bytes 2359300
  149.1 2.3 %collective-permute-start.11 = (f32[16,96,128]{2,1,0:T(8,128)S(1)}, f32[16,96,128]{2,1,0:T(8,128)S(1)}, u32[]{:S(2)}, u32[]{:S(2)}) collective-permute-start(f32[16,96,128]{2,1,0:T(8,128)S(1)} %all_to_all.5.mine), channel_id=1, source_target_pairs={{0,1},{1,0},{2,3},{3,2},{4,5},{5,4},{6,7},{7,6},{8,9},{9,8},{10,11... | collective-permute-start | bytes 2359304 | tf_op jit(solution)/shard_map/ppermute | solution.py:722
  151.4 0.9 copy-start.10

commit v2 on v0

--- a/solution.py
+++ b/solution.py
@@ -1,11 +1,818 @@
 import jax
 import jax.numpy as jnp
 from jax import lax
+from jax.experimental import pallas as pl
+from jax.experimental.pallas import tpu as pltpu
 from jax.sharding import PartitionSpec as P
 
 LEVELS = 3
 DEG = 4
 CDEG = 8
+THETA = 1.2
+DELTA = 0.8
+F32 = jnp.float32
+LANES = 128
+
+
+def vmem(*shape):
+    return pltpu.VMEM(shape, F32)
+
+
+def shape(*dims):
+    return jax.ShapeDtypeStruct(dims, F32)
+
+
+def size(shape):
+    total = 4
+    for n in shape:
+        total *= n
+    return total
+
+
+def call(kernel, outs, scratch=(), name=None):
+    spec = pl.BlockSpec(memory_space=pltpu.VMEM)
+    single = not isinstance(outs, (list, tuple))
+    held = sum(size(o.shape) for o in ([outs] if single else outs)) + sum(size(r.shape) for r in scratch)
+
+    def run(*args):
+        grant = held + sum(size(a.shape) for a in args) + 4 * 1024 * 1024
+        return pl.pallas_call(
+            kernel,
+            out_shape=outs,
+            in_specs=[spec] * len(args),
+            out_specs=spec if single else [spec] * len(outs),
+            scratch_shapes=list(scratch),
+            compiler_params=pltpu.CompilerParams(vmem_limit_bytes=min(grant, 62 * 1024 * 1024)),
+            name=name,
+        )(*args)
+
+    return run
+
+
+def split(value):
+    high = value.astype(jnp.bfloat16)
+    return high, (value - high.astype(F32)).astype(jnp.bfloat16)
+
+
+def twice(matrix, axis):
+    matrix = matrix.astype(jnp.bfloat16)
+    return jnp.concatenate([matrix, matrix], axis=axis)
+
+
+def rows_dot(matrix, value):
+    return jnp.dot(matrix, jnp.concatenate(split(value), axis=0), preferred_element_type=F32)
+
+
+def lanes_dot(value, matrix):
+    return jnp.dot(jnp.concatenate(split(value), axis=1), matrix, preferred_element_type=F32)
+
+
+def loop(count, body, unroll=1):
+    if count <= unroll:
+        for z in range(1, count + 1):
+            body(z)
+        return
+
+    def step(i, carry):
+        for j in range(unroll):
+            body(i * unroll + 1 + j)
+        return carry
+
+    lax.fori_loop(0, count // unroll, step, 0)
+    for z in range(count - count % unroll + 1, count + 1):
+        body(z)
+
+
+def iota(rows, cols, axis):
+    return lax.broadcasted_iota(jnp.int32, (rows, cols), axis)
+
+
+def roll(value, amount):
+    amount = amount % LANES
+    return value if amount == 0 else pltpu.roll(value, amount, 1)
+
+
+def chebyshev(degree):
+    sigma = THETA / DELTA
+    rho = 1.0 / sigma
+    steps = [(0.0, 1.0 / THETA)]
+    for _ in range(degree - 1):
+        new = 1.0 / (2.0 * sigma - rho)
+        steps.append((new * rho, 2.0 * new / DELTA))
+        rho = new
+    return steps
+
+
+class Level:
+    def __init__(self, refs, tiles=1, unroll=1):
+        groups = [list(refs[i : i + tiles]) for i in range(0, len(refs), tiles)]
+        self.wx, self.wy, self.wz, self.f, self.dinv, self.u, self.v, self.d = groups
+        self.tiles, self.unroll = tiles, unroll
+
+    def right(self, values):
+        rolled = [roll(v, -1) for v in values]
+        if self.tiles == 1:
+            return rolled
+        lane = iota(8, LANES, 1)
+        return [jnp.where(lane == LANES - 1, rolled[1 - t], rolled[t]) for t in range(2)]
+
+    def left(self, values):
+        rolled = [roll(v, 1) for v in values]
+        if self.tiles == 1:
+            return rolled
+        lane = iota(8, LANES, 1)
+        return [jnp.where(lane == 0, rolled[1 - t], rolled[t]) for t in range(2)]
+
+
+def get(refs, z, row):
+    return [ref[z, row : row + 8, :] for ref in refs]
+
+
+def put(refs, z, row, values):
+    for ref, value in zip(refs, values):
+        ref[z, row : row + 8, :] = value
+
+
+def each(fn, *lists):
+    return [fn(*items) for items in zip(*lists)]
+
+
+def setup(level, kappa, planes, rows, coef):
+    half = 0.5 * kappa
+    mean = lambda p, q: half * (p + q)
+
+    for row in rows:
+        put(level.wz, 0, row, each(mean, get(coef, 0, row), get(coef, 1, row)))
+
+    def edge(z):
+        row = rows[0] - 8
+        put(level.wy, z, row, each(mean, get(coef, z, row), get(coef, z, row + 1)))
+
+    loop(planes, edge, level.unroll)
+
+    def body(z):
+        for row in rows:
+            a = get(coef, z, row)
+            wx = each(mean, a, level.right(a))
+            wy = each(mean, a, get(coef, z, row + 1))
+            wz = each(mean, a, get(coef, z + 1, row))
+            den = each(lambda p, q: p + q, wx, level.left(wx))
+            for more in (wy, each(mean, a, get(coef, z, row - 1)), wz, each(mean, a, get(coef, z - 1, row))):
+                den = each(lambda p, q: p + q, den, more)
+            c = get(level.dinv, z, row)
+            den = each(lambda p, q: p + q, den, c)
+            dinv = each(lambda m, v: jnp.where(m > 0.0, 1.0 / jnp.where(m > 0.0, v, 1.0), 0.0), c, den)
+            put(level.f, z, row, each(lambda v, w: v * w, get(level.f, z, row), dinv))
+            put(level.wx, z, row, wx)
+            put(level.wy, z, row, wy)
+            put(level.wz, z, row, wz)
+            put(level.dinv, z, row, dinv)
+
+    loop(planes, body, level.unroll)
+
+
+def scaled_residual(level, src, z, row):
+    u = get(src, z, row)
+    wx = get(level.wx, z, row)
+    total = each(lambda w, v: w * v, wx, level.right(u))
+    total = each(lambda s, v: s + v, total, level.left(each(lambda w, v: w * v, wx, u)))
+    mac = lambda s, w, v: s + w * v
+    total = each(mac, total, get(level.wy, z, row), get(src, z, row + 1))
+    total = each(mac, total, get(level.wy, z, row - 1), get(src, z, row - 1))
+    total = each(mac, total, get(level.wz, z, row), get(src, z + 1, row))
+    total = each(mac, total, get(level.wz, z - 1, row), get(src, z - 1, row))
+    f = get(level.f, z, row)
+    dinv = get(level.dinv, z, row)
+    return u, dinv, each(lambda f_, d_, s, v: f_ + d_ * s - v, f, dinv, total, u)
+
+
+def sweep(level, src, dst, planes, rows, weights, last=False):
+    keep, gain = weights
+
+    def body(z):
+        for row in rows:
+            u, _, r = scaled_residual(level, src, z, row)
+            if keep == 0.0:
+                d = each(lambda v: gain * v, r)
+            else:
+                d = each(lambda p, v: keep * p + gain * v, get(level.d, z, row), r)
+            if last:
+                put(dst[:1], z, row, [u[0] + d[0]])
+                continue
+            put(level.d, z, row, d)
+            put(dst, z, row, each(lambda p, v: p + v, u, d))
+
+    loop(planes, body, level.unroll)
+
+
+def presmooth(level, planes, rows, degree):
+    def start(z):
+        for row in rows:
+            d = each(lambda v: v * (1.0 / THETA), get(level.f, z, row))
+            put(level.d, z, row, d)
+            put(level.u, z, row, d)
+
+    loop(planes(0), start, level.unroll)
+    src, dst = level.u, level.v
+    for step, weights in enumerate(chebyshev(degree)[1:], 1):
+        sweep(level, src, dst, planes(step), rows, weights)
+        src, dst = dst, src
+    return src, dst
+
+
+def postsmooth(level, src, dst, planes, rows, degree, own=None):
+    for step, weights in enumerate(chebyshev(degree)):
+        final = step == degree - 1
+        sweep(level, src, dst, planes(step), own if final and own else rows, weights, final)
+        src, dst = dst, src
+    return src, dst
+
+
+def residual_pair(level, src, k, rows, buf):
+    for i, row in enumerate(rows):
+        parts = []
+        for z in (2 * k + 1, 2 * k + 2):
+            _, dinv, r = scaled_residual(level, src, z, row)
+            ok = dinv[0] > 0.0
+            parts.append(jnp.where(ok, r[0], 0.0) / jnp.where(ok, dinv[0], 1.0))
+        buf[8 * i : 8 * i + 8, :] = parts[0] + parts[1]
+
+
+def pair_rows(out_rows, in_rows, out_offset, in_offset, count):
+    r, c = iota(out_rows, in_rows, 0) - out_offset, iota(out_rows, in_rows, 1) - in_offset
+    hit = (r >= 0) & (r < count) & ((c == 2 * r) | (c == 2 * r + 1))
+    return jnp.where(hit, 1.0, 0.0).astype(F32)
+
+
+def pair_lanes(in_lanes, out_lanes, in_offset, out_offset, count, weight):
+    r, c = iota(in_lanes, out_lanes, 0) - in_offset, iota(in_lanes, out_lanes, 1) - out_offset
+    hit = (c >= 0) & (c < count) & ((r == 2 * c) | (r == 2 * c + 1))
+    return jnp.where(hit, weight, 0.0).astype(F32)
+
+
+def interp(fine, coarse):
+    own = jnp.right_shift(fine, 1)
+    other = own + 2 * (fine - 2 * own) - 1
+    return jnp.where(coarse == own, 0.75, 0.0) + jnp.where(coarse == other, 0.25, 0.0)
+
+
+def pack(entries, limit=LANES):
+    where, tile, offset = {}, 0, 0
+    for key, n in entries:
+        if n <= 0:
+            continue
+        if offset + n > limit:
+            tile, offset = tile + 1, 0
+        where[key] = (tile, offset, n)
+        offset += n
+    return where, tile + 1
+
+
+def rows_of(entries):
+    where, offset = {}, 16
+    for key, n in entries:
+        if n <= 0:
+            continue
+        where[key] = (offset, n)
+        offset += n
+    return where, -(-(offset + 16) // 8) * 8
+
+
+def before_rows(ref, place, height):
+    if place is None:
+        return jnp.zeros((height, LANES), F32)
+    offset, n = place
+    base = offset + n - height
+    value = ref[base : base + height, :]
+    return jnp.where(iota(height, LANES, 0) >= height - n, value, 0.0)
+
+
+def after_rows(ref, place, height):
+    if place is None:
+        return jnp.zeros((height, LANES), F32)
+    offset, n = place
+    value = ref[offset : offset + height, :]
+    return jnp.where(iota(height, LANES, 0) < n, value, 0.0)
+
+
+HALO = 4
+HALO1 = 10
+ROW0, ROW1, ROW2 = 16, 24, 8
+
+
+class Plan:
+    def __init__(self, z, y, x):
+        self.z, self.y, self.x = z, y, x
+        z1 = z // 2
+        self.z1, self.y1, self.x1 = z1, y // 2, x // 2
+        reach = lambda p, n: n if p < z else max(0, n - (p - z + 1))
+        self.a0 = [(("a", p), reach(p, HALO + 1)) for p in range(z + HALO + 1)]
+        self.c0 = [(("c", p), reach(p, HALO)) for p in range(z + HALO)]
+        self.f0 = [(("f", p), reach(p, HALO)) for p in range(z + HALO)]
+        self.u0 = [(("u", p), reach(p, HALO)) for p in range(z + HALO)]
+        far = lambda o, j, n: n if o == 0 else max(0, min(n, n + 2 - (z1 - j)))
+        sides = [(o, j) for o in (0, 1) for j in range(z1)]
+        self.sides = sides
+        self.ac1 = [(("ac", o, j), far(o, j, HALO1 + 1)) for o, j in sides]
+        self.a1 = [(("a1", o, j), far(o, j, HALO1 + 1)) for o, j in sides]
+        self.c1 = [(("c1", o, j), far(o, j, HALO1)) for o, j in sides]
+        self.f1 = [(("f1", o, j), far(o, j, HALO1)) for o, j in sides]
+        self.fp = [(("fp", j), HALO1) for j in range(z1)]
+        self.yrows, self.ycount = rows_of(self.a0 + self.c0 + self.f0 + self.ac1)
+        self.yrows2, self.ycount2 = rows_of(self.u0 + self.fp)
+        self.x0, t0 = pack(self.a0 + self.c0 + self.f0)
+        self.x1m, t1 = pack(self.a1 + self.c1)
+        self.xu, tu = pack(self.u0)
+        self.xf, tf = pack(self.f1)
+        self.e0, self.e1 = y + 16, y // 2 + 32
+        self.xcount = t0 * self.e0 + t1 * self.e1
+        self.xcount2 = tu * self.e0 + tf * self.e1
+        self.xbase1, self.xbase2 = t0 * self.e0, tu * self.e0
+        self.tiles = (t0, t1, tu, tf)
+        self.r0, self.r1 = y + 32, y // 2 + 48
+        self.own0, self.own1 = list(range(ROW0, ROW0 + y, 8)), list(range(ROW1, ROW1 + y // 2, 8))
+        self.wide0 = list(range(ROW0 - HALO, ROW0 + y + HALO, 8))
+        self.wide1 = list(range(ROW1 - HALO1, ROW1 + y // 2 + HALO1, 8))
+
+
+def plane_of(plan, key, core, coeff, rhs, shift, zrecv):
+    kind, p = key
+    own = {"a": coeff, "f": rhs, "c": shift}[kind]
+    if p < plan.z:
+        return lambda rows: own[p + core * (plan.z - 1 - 2 * p), rows, :]
+    base = {"a": 0, "c": HALO + 1, "f": 2 * HALO + 1}[kind]
+    return lambda rows: zrecv[base + p - plan.z, rows, :]
+
+
+def zpack(plan):
+    def kernel(coeff, rhs, shift, out):
+        core = lax.axis_index("pz")
+        i = 0
+        for ref, n in ((coeff, HALO + 1), (shift, HALO), (rhs, HALO)):
+            for j in range(n):
+                p = plan.z - 1 - j
+                out[i] = ref[p + core * (plan.z - 1 - 2 * p)]
+                i += 1
+
+    return call(kernel, shape(3 * HALO + 1, plan.y, plan.x))
+
+
+def restrict_coefficients(plan):
+    def kernel(coeff, shift, out):
+        core = lax.axis_index("pz")
+        ry = twice(pair_rows(plan.y1, plan.y, 0, 0, plan.y1), 1)
+        ra = twice(pair_lanes(LANES, LANES, 0, 0, plan.x1, 0.125), 0)
+        rc = twice(pair_lanes(LANES, LANES, 0, plan.x1, plan.x1, 0.125), 0)
+        for k in range(plan.z1):
+            i = 2 * k + core * (plan.z - 2 - 4 * k)
+            a = lanes_dot(rows_dot(ry, coeff[i] + coeff[i + 1]), ra)
+            c = lanes_dot(rows_dot(ry, shift[i] + shift[i + 1]), rc)
+            out[k] = a + c
+
+    return call(kernel, shape(plan.z1, plan.y1, LANES))
+
+
+def ypack(plan):
+    def kernel(coeff, rhs, shift, zrecv, ac, aco, first, second, both):
+        core = lax.axis_index("pz")
+        up, down = stage_out(both, "py")
+        for key, (offset, n) in plan.yrows.items():
+            if key[0] == "ac":
+                ref = (ac, aco)[key[1]]
+                take, height = (lambda rows, ref=ref, j=key[2]: ref[j, rows, :]), plan.y1
+            else:
+                take, height = plane_of(plan, key, core, coeff, rhs, shift, zrecv), plan.y
+            up[offset : offset + n, :] = take(slice(height - n, height))
+            down[offset : offset + n, :] = take(slice(0, n))
+        first[...], second[...] = both[0], both[1]
+
+    out = shape(plan.ycount, LANES)
+    return call(kernel, [out, out], [vmem(2, plan.ycount, LANES)])
+
+
+def between(lane, first, n):
+    return ((lane - first) & (LANES - 1)) < n
+
+
+def send_lanes(outs, base, extent, tile, items, rows, width):
+    start_row = base + tile * extent
+    for height, part in rows:
+        lane = iota(height, LANES, 1)
+        totals = [jnp.zeros((height, LANES), F32)] * 2
+        for get_part, first, n, offset in items:
+            value = roll(get_part(part), offset - first)
+            totals[0] = jnp.where(between(lane, offset, n), value, totals[0])
+            totals[1] = jnp.where(between(lane, offset + n - width, n), value, totals[1])
+        for out, total in zip(outs, totals):
+            out[start_row : start_row + height, :] = total
+        start_row += height
+
+
+def take_lanes(before, after, rows, offset, n, last):
+    lane = iota(rows.stop - rows.start, LANES, 1)
+    value = jnp.where(between(lane, offset, n), before[rows, :], after[rows, :])
+    return roll(value, last + 1 - n - offset)
+
+
+def stage_out(both, axis):
+    odd = lax.axis_index(axis) & 1
+    return both.at[odd], both.at[1 - odd]
+
+
+def stage_in(both, first, second, axis):
+    here = lax.axis_index(axis)
+    odd, size_ = here & 1, lax.axis_size(axis)
+    valid = (here > 0) & (here < size_ - 1)
+    both[1 - odd] = first[...]
+    both[odd] = jnp.where(valid, second[...], 0.0)
+    return both.at[0], both.at[1]
+
+
+def xpack(plan):
+    def kernel(coeff, rhs, shift, zrecv, ac, aco, ya, yb, first, second, seen, both):
+        core = lax.axis_index("pz")
+        before, after = stage_in(seen, ya, yb, "py")
+        outs = stage_out(both, "px")
+
+        def get0(key):
+            plane = plane_of(plan, key, core, coeff, rhs, shift, zrecv)
+            place = plan.yrows.get(key)
+            return lambda part: (
+                before_rows(before, place, 8) if part == 0
+                else after_rows(after, place, 8) if part == 2
+                else plane(slice(0, plan.y))
+            )
+
+        def get1(key):
+            place = plan.yrows.get(("ac",) + key[1:])
+            ref = (ac, aco)[key[1]]
+            return lambda part: (
+                before_rows(before, place, 16) if part == 0
+                else after_rows(after, place, 16) if part == 2
+                else ref[key[2]]
+            )
+
+        for tile in range(plan.tiles[0]):
+            items = [(get0(k), plan.x - n, n, o) for k, (t, o, n) in plan.x0.items() if t == tile]
+            send_lanes(outs, 0, plan.e0, tile, items, ((8, 0), (plan.y, 1), (8, 2)), plan.x)
+        side = lambda k: plan.x1 if k[0] == "c1" else 0
+        for tile in range(plan.tiles[1]):
+            items = [(get1(k), side(k) + plan.x1 - n, n, o) for k, (t, o, n) in plan.x1m.items() if t == tile]
+            send_lanes(outs, plan.xbase1, plan.e1, tile, items, ((16, 0), (plan.y1, 1), (16, 2)), plan.x1)
+        first[...], second[...] = both[0], both[1]
+
+    out = shape(plan.xcount, LANES)
+    return call(kernel, [out, out], [vmem(2, plan.ycount, LANES), vmem(2, plan.xcount, LANES)])
+
+
+def u_plane(plan, p, u, zrecv):
+    if p < plan.z:
+        return lambda rows: u[p, rows, :]
+    base = (p - plan.z) * plan.y
+    return lambda rows: zrecv[base + rows.start : base + rows.stop, :]
+
+
+def ypack2(plan):
+    def kernel(u, zrecv, f, first, second, pair, both):
+        up, down = stage_out(both, "py")
+        for j in range(plan.z1):
+            base = HALO * plan.y + j * plan.y1
+            pair[j] = f[j] + zrecv[base : base + plan.y1, :]
+        for key, (offset, n) in plan.yrows2.items():
+            if key[0] == "fp":
+                take, height = (lambda rows, j=key[1]: pair[j, rows, :]), plan.y1
+            else:
+                take, height = u_plane(plan, key[1], u, zrecv), plan.y
+            up[offset : offset + n, :] = take(slice(height - n, height))
+            down[offset : offset + n, :] = take(slice(0, n))
+        first[...], second[...] = both[0], both[1]
+
+    out = shape(plan.ycount2, LANES)
+    return call(kernel, [out, out, shape(plan.z1, plan.y1, LANES)], [vmem(2, plan.ycount2, LANES)])
+
+
+def xpack2(plan):
+    def kernel(u, zrecv, pair, ya, yb, first, second, seen, both):
+        before, after = stage_in(seen, ya, yb, "py")
+        outs = stage_out(both, "px")
+
+        def get0(key):
+            place = plan.yrows2.get(key)
+            plane = u_plane(plan, key[1], u, zrecv)
+            return lambda part: (
+                before_rows(before, place, 8) if part == 0
+                else after_rows(after, place, 8) if part == 2
+                else plane(slice(0, plan.y))
+            )
+
+        def get1(key):
+            place = plan.yrows2.get(("fp", key[2]))
+            return lambda part: (
+                before_rows(before, place, 16) if part == 0
+                else after_rows(after, place, 16) if part == 2
+                else pair[key[2]]
+            )
+
+        for tile in range(plan.tiles[2]):
+            items = [(get0(k), plan.x - n, n, o) for k, (t, o, n) in plan.xu.items() if t == tile]
+            send_lanes(outs, 0, plan.e0, tile, items, ((8, 0), (plan.y, 1), (8, 2)), plan.x)
+        for tile in range(plan.tiles[3]):
+            items = [(get1(k), k[1] * plan.x1 + plan.x1 - n, n, o) for k, (t, o, n) in plan.xf.items() if t == tile]
+            send_lanes(outs, plan.xbase2, plan.e1, tile, items, ((16, 0), (plan.y1, 1), (16, 2)), plan.x1)
+        first[...], second[...] = both[0], both[1]
+
+    out = shape(plan.xcount2, LANES)
+    return call(kernel, [out, out], [vmem(2, plan.ycount2, LANES), vmem(2, plan.xcount2, LANES)])
+
+
+def zero(*groups):
+    for ref in [ref for group in groups for ref in group]:
+        def body(z, ref=ref):
+            ref[z - 1] = jnp.zeros(ref.shape[1:], F32)
+        loop(ref.shape[0], body)
+
+
+def fill0(plan, dst, p, plane, yplace, before, after, xplace, left, right):
+    main, side = dst
+    top, own = ROW0 - 8, plan.y
+    main[p + 1, top:ROW0, :] = before_rows(before, yplace, 8)
+    main[p + 1, ROW0 : ROW0 + own, :] = plane(slice(0, own))
+    main[p + 1, ROW0 + own : ROW0 + own + 8, :] = after_rows(after, yplace, 8)
+    value = jnp.zeros((plan.e0, LANES), F32)
+    if xplace is not None:
+        tile, offset, n = xplace
+        rows = slice(tile * plan.e0, (tile + 1) * plan.e0)
+        value = take_lanes(left, right, rows, offset, n, LANES - 1)
+        value = jnp.where(between(iota(plan.e0, LANES, 1), -n, 2 * n), value, 0.0)
+    side[p + 1, top : top + plan.e0, :] = value
+
+
+def level0(plan, level, core, coeff, rhs, shift, zrecv, before, after, left, right):
+    zero(level.u, level.v)
+    for kind, dst, planes in (("a", level.v, plan.z + HALO + 1), ("c", level.dinv, plan.z + HALO), ("f", level.f, plan.z + HALO)):
+        for p in range(planes):
+            key = (kind, p)
+            plane = plane_of(plan, key, core, coeff, rhs, shift, zrecv)
+            fill0(plan, dst, p, plane, plan.yrows.get(key), before, after, plan.x0.get(key), left, right)
+    setup(level, 1.0, plan.z + HALO, plan.wide0, level.v)
+
+
+def level0_scratch(plan):
+    return [vmem(plan.z + HALO + 2, plan.r0, LANES)] * 16
+
+
+def fill1(plan, dst, p, own, own_first, yplace, before, after, xplace, base, left, right):
+    tile, offset, n = xplace
+    row = ROW1 - 16
+    start_row = base + tile * plan.e1
+    for height, value in ((16, before_rows(before, yplace, 16)), (plan.y1, own), (16, after_rows(after, yplace, 16))):
+        lane = iota(height, LANES, 1)
+        halo = take_lanes(left, right, slice(start_row, start_row + height), offset, n, LANES - 1)
+        halo = jnp.where(between(lane, -n, n) | between(lane, plan.x1, n), halo, 0.0)
+        dst[p + 1, row : row + height, :] = jnp.where(lane < plan.x1, roll(value, -own_first), halo)
+        row, start_row = row + height, start_row + height
+
+
+def down0(plan):
+    def kernel(coeff, rhs, shift, zrecv, ya, yb, xa, xb, u_out, f_out, z_out, seen_y, seen_x, buf, *scratch):
+        core = lax.axis_index("pz")
+        ends = stage_in(seen_y, ya, yb, "py") + stage_in(seen_x, xa, xb, "px")
+        level = Level(scratch, 2)
+        level0(plan, level, core, coeff, rhs, shift, zrecv, *ends)
+        src, _ = presmooth(level, lambda s: plan.z + HALO - s, plan.wide0, DEG)
+        main = src[0]
+
+        def keep(z):
+            u_out[z - 1] = main[z, ROW0 : ROW0 + plan.y, :]
+
+        loop(plan.z, keep)
+        for j in range(HALO):
+            z_out[j * plan.y : (j + 1) * plan.y, :] = main[plan.z - j, ROW0 : ROW0 + plan.y, :]
+        ry = twice(pair_rows(plan.y1, plan.y, 0, 0, plan.y1), 1)
+        rx = twice(pair_lanes(LANES, LANES, 0, 0, plan.x1, 0.125), 0)
+        ro = twice(pair_lanes(LANES, LANES, 0, plan.x1, plan.x1, 0.125), 0)
+
+        def residual(z):
+            residual_pair(level, src, z - 1, plan.own0, buf)
+            part = rows_dot(ry, buf[...])
+            f_out[z - 1] = lanes_dot(part, rx)
+            row = HALO * plan.y + (z - 1) * plan.y1
+            z_out[pl.ds(pl.multiple_of(row, 8), plan.y1), :] = lanes_dot(part, ro)
+
+        loop(plan.z1, residual)
+
+    outs = [
+        shape(plan.z, plan.y, LANES),
+        shape(plan.z1, plan.y1, LANES),
+        shape(HALO * plan.y + plan.z1 * plan.y1, LANES),
+    ]
+    seen = [vmem(2, plan.ycount, LANES), vmem(2, plan.xcount, LANES)]
+    return call(kernel, outs, seen + [vmem(plan.y, LANES)] + level0_scratch(plan))
+
+
+def down1(plan):
+    planes, z2, y2, x2 = 2 * plan.z1, plan.z1 // 2, plan.y1 // 2, plan.x1 // 2
+
+    def kernel(ac, aco, ya, yb, xa, xb, pair, ya2, yb2, xa2, xb2, wx, wy, wz, f, dinv, u_out, message, *scratch):
+        seen_y, seen_x, seen_y2, seen_x2, u, d, buf = scratch
+        yends, xends = stage_in(seen_y, ya, yb, "py"), stage_in(seen_x, xa, xb, "px")
+        yends2, xends2 = stage_in(seen_y2, ya2, yb2, "py"), stage_in(seen_x2, xa2, xb2, "px")
+        level = Level((wx, wy, wz, f, dinv, u, u_out, d), 1, 2)
+        zero(level.u, level.v)
+        for o, j in plan.sides:
+            p = j if o == 0 else planes - 1 - j
+            own, place = (ac, aco)[o][j], plan.yrows[("ac", o, j)]
+            fill1(plan, u_out, p, own, 0, place, *yends, plan.x1m[("a1", o, j)], plan.xbase1, *xends)
+            fill1(plan, dinv, p, own, plan.x1, place, *yends, plan.x1m[("c1", o, j)], plan.xbase1, *xends)
+            fill1(plan, f, p, pair[j], o * plan.x1, plan.yrows2[("fp", j)], *yends2, plan.xf[("f1", o, j)], plan.xbase2, *xends2)
+        setup(level, 0.25, planes, plan.wide1, level.v)
+        src, _ = presmooth(level, lambda s: planes, plan.wide1, DEG)
+        assert src[0] is u_out
+        ry = twice(pair_rows(y2, plan.y1, 0, 0, y2), 1)
+        totals = [jnp.zeros((y2, LANES), F32) for _ in range(3)]
+        for k in range(z2):
+            residual_pair(level, src, k, plan.own1, buf)
+            own = rows_dot(ry, ac[2 * k] + ac[2 * k + 1])
+            for i, (part, first) in enumerate(((rows_dot(ry, buf[...]), 0), (own, 0), (own, plan.x1))):
+                totals[i] += lanes_dot(part, twice(pair_lanes(LANES, LANES, first, k * x2, x2, 0.125), 0))
+        for i in range(3):
+            message[i * y2 : (i + 1) * y2, :] = totals[i]
+
+    big = (planes + 2, plan.r1, LANES)
+    outs = [shape(*big)] * 6 + [shape(3 * y2, LANES)]
+    seen = [vmem(2, n, LANES) for n in (plan.ycount, plan.xcount, plan.ycount2, plan.xcount2)]
+    return call(kernel, outs, seen + [vmem(*big)] * 2 + [vmem(plan.y1, LANES)])
+
+
+def prolong(src, tmp, planes, py, px, rows, unroll=1):
+    def body(z):
+        for out, matrix in zip(tmp, px):
+            out[z, rows, :] = rows_dot(py, lanes_dot(src[z], matrix))
+
+    loop(planes, body, unroll)
+
+
+def correct(level, src, dst, tmp, fine_planes, rows):
+    def body(k):
+        for row in rows:
+            own = each(lambda v: 0.75 * v, get(tmp, k, row))
+            for z, far in ((2 * k - 1, k - 1), (2 * k, k + 1)):
+                new = each(
+                    lambda n, f, m, v: v + jnp.where(m > 0.0, n + 0.25 * f, 0.0),
+                    own, get(tmp, far, row), get(level.dinv, z, row), get(src, z, row),
+                )
+                put(dst, z, row, new)
+
+    loop(fine_planes // 2, body, level.unroll)
+
+
+def coarse(plan):
+    planes1 = 2 * plan.z1
+    z2, y2, x2 = plan.z1 // 2, plan.y1 // 2, plan.x1 // 2
+    planes2, rows2, lanes2 = 2 * z2, 3 * y2, 3 * x2
+    planes3, rows3, lanes3 = planes2 // 2, rows2 // 2, lanes2 // 2
+    h2, h3 = rows2 + 16, rows3 + 16
+    wide2, wide3 = list(range(ROW2, ROW2 + rows2, 8)), list(range(ROW2, ROW2 + rows3, 8))
+    block = 3 * y2
+
+    def kernel(own, xa, xb, owno, xao, xbo, wx, wy, wz, f, dinv, u_in, e1, *scratch):
+        l2, l3, (u1, d1, buf, tmp3, tmp2, seen) = scratch[:8], scratch[8:16], scratch[16:]
+        two, three = Level(l2, 1, 4), Level(l3, 1, 8)
+        zero(two.u, two.v, [*l3])
+        odd = lax.axis_index("py") & 1
+        here = lax.axis_index("py")
+        parts = ((1 - odd) * 2, 1, odd * 2)
+        edge = (here > 0) & (here < lax.axis_size("py") - 1)
+        ok = (jnp.where(odd == 1, True, edge), None, jnp.where(odd == 0, True, edge))
+        lane = iota(y2, LANES, 1)
+        group = [between(lane, x2 * g, x2) for g in range(4)]
+        for side, (mid, first, second) in enumerate(((own, xa, xb), (owno, xao, xbo))):
+            left, right = stage_in(seen, first, second, "px")
+            for i, dst in enumerate((two.f[0], two.v[0], two.dinv[0])):
+                for b in range(3):
+                    base = pl.multiple_of(parts[b] * block + i * y2, 8)
+                    blocks = [ref[pl.ds(base, y2), :] for ref in (left, mid, right)]
+                    if ok[b] is not None:
+                        blocks = [jnp.where(ok[b], v, 0.0) for v in blocks]
+                    turned = []
+                    for s in range(4):
+                        value = jnp.zeros((y2, LANES), F32)
+                        for k in range(z2):
+                            if (k + s) % 4 < 3:
+                                value = jnp.where(group[k], blocks[(k + s) % 4], value)
+                        turned.append(roll(value, x2 * s))
+                    for k in range(z2):
+                        value = jnp.zeros((y2, LANES), F32)
+                        for g in range(3):
+                            value = jnp.where(group[g], turned[(g - k) % 4], value)
+                        p = k if side == 0 else planes2 - 1 - k
+                        dst[p + 1, ROW2 + b * y2 : ROW2 + (b + 1) * y2, :] = value
+        ry = twice(pair_rows(h3, rows2, ROW2, 0, rows3), 1)
+        rx = twice(pair_lanes(LANES, LANES, 0, 0, lanes3, 0.125), 0)
+        for k in range(planes3):
+            for src, dst in ((two.v[0], three.v[0]), (two.dinv[0], three.dinv[0])):
+                value = src[2 * k + 1, ROW2 : ROW2 + rows2, :] + src[2 * k + 2, ROW2 : ROW2 + rows2, :]
+                dst[k + 1] = lanes_dot(rows_dot(ry, value), rx)
+        setup(two, 0.25**2, planes2, wide2, two.v)
+        src2, dst2 = presmooth(two, lambda s: planes2, wide2, DEG)
+        for k in range(planes3):
+            residual_pair(two, src2, k, wide2, buf.at[k])
+        for k in range(planes3):
+            three.f[0][k + 1] = lanes_dot(rows_dot(ry, buf[k]), rx)
+        setup(three, 0.25**3, planes3, wide3, three.v)
+        src3, _ = presmooth(three, lambda s: planes3, wide3, CDEG)
+
+        zero([tmp3, tmp2])
+        px = twice(interp(iota(LANES, LANES, 1), iota(LANES, LANES, 0)), 0)
+        py = twice(interp(iota(h2, h3, 0) - ROW2, iota(h2, h3, 1) - ROW2), 1)
+        prolong(src3[0], [tmp3], planes3, py, [px], slice(0, h2), 4)
+        correct(two, src2, src2, [tmp3], planes2, wide2)
+        src2, _ = postsmooth(two, src2, dst2, lambda s: planes2, wide2, DEG)
+
+        lanes = iota(LANES, LANES, 1)
+        lanes = jnp.where(lanes < LANES - 2 * x2 + 16, lanes, lanes - LANES) + 2 * x2
+        px = twice(interp(lanes, iota(LANES, LANES, 0)), 0)
+        py = twice(interp(iota(plan.r1, h2, 0) - ROW1 + 2 * y2, iota(plan.r1, h2, 1) - ROW2), 1)
+        one = Level((wx, wy, wz, f, dinv, u1, e1, d1), 1, 2)
+        zero(one.u, one.v)
+        prolong(src2[0], [tmp2], planes2, py, [px], slice(0, plan.r1), 2)
+        correct(one, [u_in], one.v, [tmp2], planes1, plan.wide1)
+        src1, _ = postsmooth(one, one.v, one.u, lambda s: min(planes1, plan.z1 + 6 - s), plan.wide1, DEG)
+        assert src1[0] is e1
+
+    big1 = (planes1 + 2, plan.r1, LANES)
+    scratch = [vmem(planes2 + 2, h2, LANES)] * 8 + [vmem(planes3 + 2, h3, LANES)] * 8 + [vmem(*big1)] * 2
+    scratch += [vmem(planes3, rows2, LANES), vmem(planes3 + 2, h2, LANES), vmem(planes2 + 2, plan.r1, LANES)]
+    scratch += [vmem(2, 3 * block, LANES)]
+    return call(kernel, shape(*big1), scratch)
+
+
+def up0(plan):
+    planes = plan.z + HALO
+    few = HALO // 2 + plan.z1 + 1
+
+    def kernel(coeff, rhs, shift, zrecv, ya, yb, xa, xb, u_in, zrecv2, ya2, yb2, xa2, xb2, e1, out, *scratch):
+        seen_y, seen_x, seen_y2, seen_x2, tmp, tmps = scratch[:6]
+        core = lax.axis_index("pz")
+        ends = stage_in(seen_y, ya, yb, "py") + stage_in(seen_x, xa, xb, "px")
+        ends2 = stage_in(seen_y2, ya2, yb2, "py") + stage_in(seen_x2, xa2, xb2, "px")
+        level = Level(scratch[6:], 2)
+        level0(plan, level, core, coeff, rhs, shift, zrecv, *ends)
+        for p in range(planes):
+            key = ("u", p)
+            plane = u_plane(plan, p, u_in, zrecv2)
+            fill0(plan, level.u, p, plane, plan.yrows2.get(key), *ends2[:2], plan.xu.get(key), *ends2[2:])
+        tmp[0] = jnp.zeros(tmp.shape[1:], F32)
+        tmps[0] = jnp.zeros(tmp.shape[1:], F32)
+        first, count = plan.wide0[0], 8 * len(plan.wide0)
+        py = twice(interp(iota(count, plan.r1, 0) + first - ROW0, iota(count, plan.r1, 1) - ROW1), 1)
+        lane = iota(LANES, LANES, 1)
+        coarse_lane = iota(LANES, LANES, 0)
+        coarse_lane = jnp.where(coarse_lane < plan.x1 + 16, coarse_lane, coarse_lane - LANES)
+        main = twice(interp(lane, coarse_lane), 0)
+        side = twice(interp(jnp.where(lane < LANES // 2, lane + LANES, lane - LANES), coarse_lane), 0)
+        prolong(e1, [tmp, tmps], few, py, [main, side], slice(first, first + count))
+        correct(level, level.u, level.u, [tmp, tmps], planes, plan.wide0)
+        src, _ = postsmooth(level, level.u, level.v, lambda s: planes - 1 - s, plan.wide0, DEG, plan.own0)
+        for p in range(plan.z):
+            out[p + core * (plan.z - 1 - 2 * p)] = src[0][p + 1, ROW0 : ROW0 + plan.y, :]
+
+    seen = [vmem(2, n, LANES) for n in (plan.ycount, plan.xcount, plan.ycount2, plan.xcount2)]
+    tmps = [vmem(few + 2, plan.r0, LANES)] * 2
+    return call(kernel, shape(plan.z, plan.y, LANES), seen + tmps + level0_scratch(plan))
+
+
+def swap(value, axis):
+    return lax.ppermute(value, axis, [(0, 1), (1, 0)])
+
+
+def meet(first, second, axis):
+    n = lax.axis_size(axis)
+    even = [(i, i + 1) for i in range(0, n, 2)]
+    odd = [(i, (i + 1) % n) for i in range(1, n, 2)]
+    both = lambda pairs: pairs + [(j, i) for i, j in pairs]
+    return lax.ppermute(first, axis, both(even)), lax.ppermute(second, axis, both(odd))
+
+
+def local(rhs, coeff, shift):
+    plan = Plan(*rhs.shape)
+    zrecv = swap(zpack(plan)(coeff, rhs, shift), "pz")
+    ac = restrict_coefficients(plan)(coeff, shift)
+    aco = swap(ac, "pz")
+    ends_y = meet(*ypack(plan)(coeff, rhs, shift, zrecv, ac, aco), "py")
+    ends_x = meet(*xpack(plan)(coeff, rhs, shift, zrecv, ac, aco, *ends_y), "px")
+    fine = (coeff, rhs, shift, zrecv, *ends_y, *ends_x)
+    u, f, z_out = down0(plan)(*fine)
+    zrecv2 = swap(z_out, "pz")
+    first, second, pair = ypack2(plan)(u, zrecv2, f)
+    ends_y2 = meet(first, second, "py")
+    ends_x2 = meet(*xpack2(plan)(u, zrecv2, pair, *ends_y2), "px")
+    *one, message = down1(plan)(ac, aco, *ends_y, *ends_x, pair, *ends_y2, *ends_x2)
+    first, second = meet(message, message, "py")
+    wide = jnp.concatenate([first, message, second])
+    blocks = (wide, *meet(wide, wide, "px"))
+    e1 = coarse(plan)(*blocks, *[swap(b, "pz") for b in blocks], *one)
+    return up0(plan)(*fine, u, zrecv2, *ends_y2, *ends_x2, e1)
 
 
 lower_bound = 0.4
@@ -95,7 +902,7 @@
     return stacked.reshape(shape)
 
 
-def prolong(padded):
+def prolong_all(padded):
     for axis_index in range(3):
         padded = refine_axis(padded, axis_index)
     return padded
@@ -113,7 +920,7 @@
     return extended(field, (("pz", 0), ("py", 1), ("px", 2)), 1)
 
 
-def local(rhs, coeff, shift):
+def general(rhs, coeff, shift):
     coeff_pad_zero = extended(coeff, (("pz", 0), ("py", 1), ("px", 2)), 1)
     level_zero = make_level(coeff_pad_zero, shift, 1.0)
     field = smooth(None, rhs, level_zero, DEG, fine_pad)
@@ -139,15 +946,16 @@
     coarse_field = smooth(None, coarse_source, coarse_level, CDEG, coarse_face_pad)
     padded = extended(coarse_field, (("pz", 0), ("py", 1), ("px", 2)), 1)
     for depth in range(LEVELS - 1, 0, -1):
-        field = fields[depth] + prolong(padded)
+        field = fields[depth] + prolong_all(padded)
         field = smooth(field, sources[depth], levels_list[depth], DEG, face_pad)
         padded = extended(field, (("pz", 0), ("py", 1), ("px", 2)), 1)
-    field = fields[0] + prolong(padded)
+    field = fields[0] + prolong_all(padded)
     field = smooth(field, rhs, level_zero, DEG, fine_pad)
     return field
 
 
 def solution(mesh):
-    in_specs = (P("pz", "py", "px"), P("pz", "py", "px"), P("pz", "py", "px"))
-    out_specs = P("pz", "py", "px")
-    return jax.shard_map(local, mesh=mesh, in_specs=in_specs, out_specs=out_specs, check_vma=False)
+    spec = P("pz", "py", "px")
+    body = local if mesh.shape["pz"] == 2 else general
+
+    return jax.shard_map(body, mesh=mesh, in_specs=(spec,) * 3, out_specs=spec, check_vma=False)

time: 1440 us -> 146 us (0.10); the launches traced: 1420 us -> 146 us
  starting transfers between devices: 440 us -> 19.4 us
  local copies, waits for them, and re-layouts: 369 us -> 4.28 us
  waiting for transfers between devices: 362 us -> 48.1 us
  other arithmetic: 246 us -> 0 us
  Pallas kernels: 0 us -> 73.7 us
    ppermute x228 -> x18, starting transfers between devices: 440 us -> 19.4 us  [the longest x6 11.4 us: meet(): lax.ppermute(second, axis, both(odd))]
    ppermute x228 -> x18, waiting for transfers between devices: 362 us -> 48.1 us  [the longest x6 22.2 us: meet(): lax.ppermute(second, axis, both(odd))]
    reshape x7 -> x0, local copies, waits for them, and re-layouts: 224 us -> none  [the longest x5 221 us: restrict(): field.reshape(s0 // 2, 2, s1 // 2, 2, s2 // 2, 2).mean(axis=(1, 3, 5))]
    add x31 -> x0, other arithmetic: 107 us -> none  [the longest x28 103 us: smooth(): field = field + update]
    reduce_sum x9 -> x0, other arithmetic: 83.8 us -> none  [restrict(): field.reshape(s0 // 2, 2, s1 // 2, 2, s2 // 2, 2).mean(axis=(1, 3, 5))]
    pallas_call x0 -> x10, Pallas kernels: none -> 73.7 us  [run(): pl.pallas_call(kernel, out_shape=outs, in_specs=[spec] * len(args), out_s...]
    slice x94 -> x0, local copies, waits for them, and re-layouts: 62 us -> none  [the longest x81 42.7 us: extended(): last = lax.slice_in_dim(array, length - width, length, axis=dim)]
    ppermute x18 -> x0, local copies, waits for them, and re-layouts: 30.3 us -> none  [the longest x9 15.3 us: extended(): after = lax.ppermute(first, axis, down)]
  transfers between devices with their start and end apart: 228 -> 18, of which waited for: 117 -> 15; matrix products, arithmetic and copies ran while one was open for 30% -> 0% of each run, Pallas kernels for 0% -> 1%
where the time goes in v2:
time: 146 us
  Pallas kernels  73.7 us (50%)
  waiting for transfers between devices  48.1 us (33%)
  starting transfers between devices  19.4 us (13%)
  local copies, waits for them, and re-layouts  4.28 us (3%)
    pallas_call x10, Pallas kernels, run(): pl.pallas_call(kernel, out_shape=outs, in_specs=[spec] * len(args), out_s...  73.7 us
    ppermute x6, waiting for transfers between devices, meet(): lax.ppermute(second, axis, both(odd))  22.2 us
    ppermute x6, waiting for transfers between devices, meet(): lax.ppermute(first, axis, both(even))  21.5 us
    ppermute x6, starting transfers between devices, meet(): lax.ppermute(second, axis, both(odd))  11.4 us
    ppermute x6, starting transfers between devices, meet(): lax.ppermute(first, axis, both(even))  6.81 us
    ppermute x6, waiting for transfers between devices, swap(): return lax.ppermute(value, axis, [(0, 1), (1, 0)])  4.43 us
    unnamed x14, local copies, waits for them, and re-layouts  4.28 us
  transfers between devices with their start and end apart: 18, of which 15 were waited for; matrix products, arithmetic and copies ran while one was open for 0% of the time, Pallas kernels for 1%

profile of v2, /device:TPU:0, one launch (start us, length us, event | category | flops | bytes accessed | tf_op | source)
XLA Modules:
  0.0 145.6 jit_solution(17496700560727557964)
XLA Ops:
  0.0 1.2 copy-done
  1.2 1.2 copy-done.2
  2.5 1.2 copy-done.4
  4.9 1.4 shard_map.38.ac
  6.8 1.2 collective-permute-done.1.aco
  8.1 3.0 %collective-permute-start.2 = (f32[424,128]{1,0:T(8,128)S(1)}, f32[424,128]{1,0:T(8,128)S(1)}, u32[]{:S(2)}, u32[]{:S(2)}) collective-permute-start(f32[424,128]{1,0:T(8,128)S(1)} %get-tuple-element.24), channel_id=1, source_target_pairs={{0,2},{4,6},{2,0},{6,4},{1,3},{5,7},{3,1},{7,5},{8,10},{12,14},{10... | collective-permute-start | bytes 651272 | tf_op jit(solution)/shard_map/ppermute | solution.py:794
  11.1 2.5 %collective-permute-start.3 = (f32[424,128]{1,0:T(8,128)S(1)}, f32[424,128]{1,0:T(8,128)S(1)}, u32[]{:S(2)}, u32[]{:S(2)}) collective-permute-start(f32[424,128]{1,0:T(8,128)S(1)} %get-tuple-element.25), channel_id=1, source_target_pairs={{2,4},{6,0},{4,2},{0,6},{3,5},{7,1},{5,3},{1,7},{10,12},{14,8},{12... | collective-permute-start | bytes 651272 | tf_op jit(solution)/shard_map/ppermute | solution.py:794
  13.6 3.3 %collective-permute-done.2.ya = f32[424,128]{1,0:T(8,128)S(1)} collective-permute-done((f32[424,128]{1,0:T(8,128)S(1)}, f32[424,128]{1,0:T(8,128)S(1)}, u32[]{:S(2)}, u32[]{:S(2)}) %collective-permute-start.2) | collective-permute-done | bytes 217120 | tf_op jit(solution)/shard_map/ppermute | solution.py:794
  16.8 6.8 %collective-permute-done.3.yb = f32[424,128]{1,0:T(8,128)S(1)} collective-permute-done((f32[424,128]{1,0:T(8,128)S(1)}, f32[424,128]{1,0:T(8,128)S(1)}, u32[]{:S(2)}, u32[]{:S(2)}) %collective-permute-start.3) | collective-permute-done | bytes 217120 | tf_op jit(solution)/shard_map/ppermute | solution.py:794
  23.7 2.2 %shard_map.40 = (f32[576,128]{1,0:T(8,128)S(1)}, f32[576,128]{1,0:T(8,128)S(1)}) custom-call(f32[16,128,128]{2,1,0:T(8,128)S(1)} %copy-done.1, f32[16,128,128]{2,1,0:T(8,128)S(1)} %copy-done.5, f32[16,128,128]{2,1,0:T(8,128)S(1)} %copy-done.3, f32[13,128,128]{2,1,0:T(8,128)S(1)} %collective-permute-done.zrecv, f32[8,64,128]{2,1,0:T(8,128)S(1)} %shard_map.38.ac, ...), custom_call_target="tpu_custom_call" | custom-call | tf_op jit(solution)/shard_map/pallas_call | solution.py:39
  25.8 1.6 %collective-permute-start.4 = (f32[576,128]{1,0:T(8,128)S(1)}, f32[576,128]{1,0:T(8,128)S(1)}, u32[]{:S(2)}, u32[]{:S(2)}) collective-permute-start(f32[576,128]{1,0:T(8,128)S(1)} %get-tuple-element.26), channel_id=1, source_target_pairs={{0,8},{16,24},{8,0},{24,16},{1,9},{17,25},{9,1},{25,17},{2,10},{18... | collective-permute-start | bytes 884744 | tf_op jit(solution)/shard_map/ppermute | solution.py:794
  27.4 1.5 %collective-permute-start.5 = (f32[576,128]{1,0:T(8,128)S(1)}, f32[576,128]{1,0:T(8,128)S(1)}, u32[]{:S(2)}, u32[]{:S(2)}) collective-permute-start(f32[576,128]{1,0:T(8,128)S(1)} %get-tuple-element.27), channel_id=1, source_target_pairs={{8,16},{24,0},{16,8},{0,24},{9,17},{25,1},{17,9},{1,25},{10,18},{2... | collective-permute-start | bytes 884744 | tf_op jit(solution)/shard_map/ppermute | solution.py:794
  28.9 6.9 %collective-permute-done.4.xa = f32[576,128]{1,0:T(8,128)S(1)} collective-permute-done((f32[576,128]{1,0:T(8,128)S(1)}, f32[576,128]{1,0:T(8,128)S(1)}, u32[]{:S(2)}, u32[]{:S(2)}) %collective-permute-start.4) | collective-permute-done | bytes 294944 | tf_op jit(solution)/shard_map/ppermute | solution.py:794
  35.8 5.5 %collective-permute-done.5.xb = f32[576,128]{1,0:T(8,128)S(1)} collective-permute-done((f32[576,128]{1,0:T(8,128)S(1)}, f32[576,128]{1,0:T(8,128)S(1)}, u32[]{:S(2)}, u32[]{:S(2)}) %collective-permute-start.5) | collective-permute-done | bytes 294944 | tf_op jit(solution)/shard_map/ppermute | solution.py:794
  41.3 22.6 %shard_map.41 = (f32[16,128,128]{2,1,0:T(8,128)S(1)}, f32[8,64,128]{2,1,0:T(8,128)S(1)}, f32[1024,128]{1,0:T(8,128)S(1)}) custom-call(f32[16,128,128]{2,1,0:T(8,128)S(1)} %copy-done.1, f32[16,128,128]{2,1,0:T(8,128)S(1)} %copy-done.5, f32[16,128,128]{2,1,0:T(8,128)S(1)} %copy-done.3, f32[13,128,128]{2,1,0:T(8,128)S(1)} %collective-permute-done.zrecv, ...), custom_call_target="tpu_custom_call" | custom-call | tf_op jit(solution)/shard_map/pallas_call | solution.py:39
  64.0 1.9 %collective-permute-done.6.zrecv.zrecv2 = f32[1024,128]{1,0:T(8,128)S(1)} collective-permute-done((f32[1024,128]{1,0:T(8,128)S(1)}, f32[1024,128]{1,0:T(8,128)S(1)}, u32[]{:S(2)}, u32[]{:S(2)}) %collective-permute-start.6) | collective-permute-done | bytes 524320 | tf_op jit(solution)/shard_map/ppermute | solution.py:786
  66.1 3.0 %collective-permute-start.8 = (f32[184,128]{1,0:T(8,128)S(1)}, f32[184,128]{1,0:T(8,128)S(1)}, u32[]{:S(2)}, u32[]{:S(2)}) collective-permute-start(f32[184,128]{1,0:T(8,128)S(1)} %get-tuple-element.32), channel_id=1, source_target_pairs={{2,4},{6,0},{4,2},{0,6},{3,5},{7,1},{5,3},{1,7},{10,12},{14,8},{12... | collective-permute-start | bytes 282632 | tf_op jit(solution)/shard_map/ppermute | solution.py:794
  69.1 1.7 %collective-permute-done.7.ya.ya2 = f32[184,128]{1,0:T(8,128)S(1)} collective-permute-done((f32[184,128]{1,0:T(8,128)S(1)}, f32[184,128]{1,0:T(8,128)S(1)}, u32[]{:S(2)}, u32[]{:S(2)}) %collective-permute-start.7) | collective-permute-done | bytes 94240 | tf_op jit(solution)/shard_map/ppermute | solution.py:794
  70.8 3.1 %collective-permute-done.8.yb.yb2 = f32[184,128]{1,0:T(8,128)S(1)} collective-permute-done((f32[184,128]{1,0:T(8,128)S(1)}, f32[184,128]{1,0:T(8,128)S(1)}, u32[]{:S(2)}, u32[]{:S(2)}) %collective-permute-start.8) | collective-permute-done | bytes 94240 | tf_op jit(solution)/shard_map/ppermute | solution.py:794
  74.8 1.6 %collective-permute-start.9 = (f32[336,128]{1,0:T(8,128)S(1)}, f32[336,128]{1,0:T(8,128)S(1)}, u32[]{:S(2)}, u32[]{:S(2)}) collective-permute-start(f32[336,128]{1,0:T(8,128)S(1)} %get-tuple-element.34), channel_id=1, source_target_pairs={{0,8},{16,24},{8,0},{24,16},{1,9},{17,25},{9,1},{25,17},{2,10},{18... | collective-permute-start | bytes 516104 | tf_op jit(solution)/shard_map/ppermute | solution.py:794
  76.8 5.3 %collective-permute-done.9.xa2 = f32[336,128]{1,0:T(8,128)S(1)} collective-permute-done((f32[336,128]{1,0:T(8,128)S(1)}, f32[336,128]{1,0:T(8,128)S(1)}, u32[]{:S(2)}, u32[]{:S(2)}) %collective-permute-start.9) | collective-permute-done | bytes 172064 | tf_op jit(solution)/shard_map/ppermute | solution.py:794
  82.1 1.8 %collective-permute-done.10.xb2 = f32[336,128]{1,0:T(8,128)S(1)} collective-permute-done((f32[336,128]{1,0:T(8,128)S(1)}, f32[336,128]{1,0:T(8,128)S(1)}, u32[]{:S(2)}, u32[]{:S(2)}) %collective-permute-start.10) | collective-permute-done | bytes 172064 | tf_op jit(solution)/shard_map/ppermute | solution.py:794
  83.9 7.5 %shard_map.44 = (f32[18,112,128]{2,1,0:T(8,128)S(1)}, f32[18,112,128]{2,1,0:T(8,128)S(1)}, f32[18,112,128]{2,1,0:T(8,128)S(1)}, f32[18,112,128]{2,1,0:T(8,128)S(...) custom-call(f32[8,64,128]{2,1,0:T(8,128)S(1)} %shard_map.38.ac, ...), custom_call_target="tpu_custom_call" | custom-call | tf_op jit(solution)/shard_map/pallas_call | solution.py:39
  91.5 1.5 %collective-permute-start.12 = (f32[96,128]{1,0:T(8,128)S(1)}, f32[96,128]{1,0:T(8,128)S(1)}, u32[]{:S(2)}, u32[]{:S(2)}) collective-permute-start(f32[96,128]{1,0:T(8,128)S(1)} %get-tuple-element.36), channel_id=1, source_target_pairs={{2,4},{6,0},{4,2},{0,6},{3,5},{7,1},{5,3},{1,7},{10,12},{14,8},{12... | collective-permute-start | bytes 147464 | tf_op jit(solution)/shard_map/ppermute | solution.py:794
  93.0 2.8 %collective-permute-done.11 = f32[96,128]{1,0:T(8,128)S(1)} collective-permute-done((f32[96,128]{1,0:T(8,128)S(1)}, f32[96,128]{1,0:T(8,128)S(1)}, u32[]{:S(2)}, u32[]{:S(2)}) %collective-permute-start.11) | collective-permute-done | bytes 49184 | tf_op jit(solution)/shard_map/ppermute | solution.py:794
  95.9 1.7 %collective-permute-done.12 = f32[96,128]{1,0:T(8,128)S(1)} collective-permute-done((f32[96,128]{1,0:T(8,128)S(1)}, f32[96,128]{1,0:T(8,128)S(1)}, u32[]{:S(2)}, u32[]{:S(2)}) %collective-permute-start.12) | collective-permute-done | bytes 49184 | tf_op jit(solution)/shard_map/ppermute | solution.py:794
  97.5 2.5 %collective-permute-start.14 = (f32[288,128]{1,0:T(8,128)S(1)}, f32[288,128]{1,0:T(8,128)S(1)}, u32[]{:S(2)}, u32[]{:S(2)}) collective-permute-start(f32[288,128]{1,0:T(8,128)S(1)} %constant_dynamic-update-slice_fusion.own), channel_id=1, source_target_pairs={{8,16},{24,0},{16,8},{0,24},{9,17},{25,1},{17,9},{1,25},{10,18},{2... | collective-permute-start | bytes 442376 | tf_op jit(solution)/shard_map/ppermute | solution.py:794
  100.5 3.2 %collective-permute-done.14.xb = f32[288,128]{1,0:T(8,128)S(1)} collective-permute-done((f32[288,128]{1,0:T(8,128)S(1)}, f32[288,128]{1,0:T(8,128)S(1)}, u32[]{:S(2)}, u32[]{:S(2)}) %collective-permute-start.14) | collective-permute-done | bytes 147488 | tf_op jit(solution)/shard_map/ppermute | solution.py:794
  103.7 1.5 %collective-permute-done.13.xa = f32[288,128]{1,0:T(8,128)S(1)} collective-permute-done((f32[288,128]{1,0:T(8,128)S(1)}, f32[288,128]{1,0:T(8,128)S(1)}, u32[]{:S(2)}, u32[]{:S(2)}) %collective-permute-start.13) | collective-permute-done | bytes 147488 | tf_op jit(solution)/shard_map/ppermute | solution.py:794
  105.2 1.4 collective-permute-done.16.xao
  106.6 13.2 %shard_map.45.e1 = f32[18,112,128]{2,1,0:T(8,128)S(1)} custom-call(f32[288,128]{1,0:T(8,128)S(1)} %constant_dynamic-update-slice_fusion.own, f32[288,128]{1,0:T(8,128)S(1)} %collective-permute-done.13.xa, f32[288,128]{1,0:T(8,128)S(1)} %collective-permute-done.14.xb, f32[288,128]{1,0:T(8,128)S(1)} %collective-permute-done.15.owno, ...), custom_call_target="tpu_custom_call" | custom-call | tf_op jit(solution)/shard_map/pallas_call | solution.py:39
  119.8 25.8 %shard_map.46 = f32[16,128,128]{2,1,0:T(8,128)} custom-call(f32[16,128,128]{2,1,0:T(8,128)S(1)} %copy-done.1, f32[16,128,128]{2,1,0:T(8,128)S(1)} %copy-done.5, f32[16,128,128]{2,1,0:T(8,128)S(1)} %copy-done.3, f32[13,128,128]{2,1,0:T(8,128)S(1)} %collective-permute-done.zrecv, f32[424,128]{1,0:T(8,128)S(1)} %collective-permute-done.2.ya, ...), custom_call_target="tpu_custom_call" | custom-call | tf_op jit(solution)/shard_map/pallas_call | solution.py:39
  (29 shorter events, 4.0 us)
Async XLA Ops:
  0.0 1.2 copy-start
  1.2 1.2 copy-start.2
  2.5 1.2 copy-start.4
  3.7 1.2 copy-start.1
  3.7 4.2 %copy-start.3 = (f32[16,128,128]{2,1,0:T(8,128)S(1)}, f32[16,128,128]{2,1,0:T(8,128)}, u32[]{:S(2)}) copy-start(f32[16,128,128]{2,1,0:T(8,128)} %shift.11) | copy-start | bytes 3145732
  3.7 4.2 %copy-start.5 = (f32[16,128,128]{2,1,0:T(8,128)S(1)}, f32[16,128,128]{2,1,0:T(8,128)}, u32[]{:S(2)}) copy-start(f32[16,128,128]{2,1,0:T(8,128)} %rhs.9) | copy-start | bytes 3145732
  3.8 4.2 %collective-permute-start = (f32[13,128,128]{2,1,0:T(8,128)S(1)}, f32[13,128,128]{2,1,0:T(8,128)S(1)}, u32[]{:S(2)}, u32[]{:S(2)}) collective-permute-start(f32[13,128,128]{2,1,0:T(8,128)S(1)} %shard_map.37), channel_id=1, source_target_pairs={{0,1},{1,0},{2,3},{3,2},{4,5},{5,4},{6,7},{7,6},{8,9},{9,8},{10,11... | collective-permute-start | bytes 2555912 | tf_op jit(solution)/shard_map/ppermute | solution.py:786
  6.3 1.7 %collective-permute-start.1 = (f32[8,64,128]{2,1,0:T(8,128)S(1)}, f32[8,64,128]{2,1,0:T(8,128)S(1)}, u32[]{:S(2)}, u32[]{:S(2)}) collective-permute-start(f32[8,64,128]{2,1,0:T(8,128)S(1)} %shard_map.38.ac), channel_id=1, source_target_pairs={{0,1},{1,0},{2,3},{3,2},{4,5},{5,4},{6,7},{7,6},{8,9},{9,8},{10,11... | collective-permute-start | bytes 786440 | tf_op jit(solution)/shard_map/ppermute | solution.py:786
  8.1 8.7 %collective-permute-start.2 = (f32[424,128]{1,0:T(8,128)S(1)}, f32[424,128]{1,0:T(8,128)S(1)}, u32[]{:S(2)}, u32[]{:S(2)}) collective-permute-start(f32[424,128]{1,0:T(8,128)S(1)} %get-tuple-element.24), channel_id=1, source_target_pairs={{0,2},{4,6},{2,0},{6,4},{1,3},{5,7},{3,1},{7,5},{8,10},{12,14},{10... | collective-permute-start | bytes 651272 | tf_op jit(solution)/shard_map/ppermute | solution.py:794
  11.1 12.6 %collective-permute-start.3 = (f32[424,128]{1,0:T(8,128)S(1)}, f32[424,128]{1,0:T(8,128)S(1)}, u32[]{:S(2)}, u32[]{:S(2)}) collective-permute-start(f32[424,128]{1,0:T(8,128)S(1)} %get-tuple-element.25), channel_id=1, source_target_pairs={{2,4},{6,0},{4,2},{0,6},{3,5},{7,1},{5,3},{1,7},{10,12},{14,8},{12... | collective-permute-start | bytes 651272 | tf_op jit(solution)/shard_map/ppermute | solution.py:794
  25.8 9.9 %collective-permute-start.4 = (f32[576,128]{1,0:T(8,128)S(1)}, f32[576,128]{1,0:T(8,128)S(1)}, u32[]{:S(2)}, u32[]{:S(2)}) collective-permute-start(f32[576,128]{1,0:T(8,128)S(1)} %get-tuple-element.26), channel_id=1, source_target_pairs={{0,8},{16,24},{8,0},{24,16},{1,9},{17,25},{9,1},{25,17},{2,10},{18... | collective-permute-start | bytes 884744 | tf_op jit(solution)/shard_map/ppermute | solution.py:794
  27.4 13.9 %collective-permute-start.5 = (f32[576,128]{1,0:T(8,128)S(1)}, f32[576,128]{1,0:T(8,128)S(1)}, u32[]{:S(2)}, u32[]{:S(2)}) collective-permute-start(f32[576,128]{1,0:T(8,128)S(1)} %get-tuple-element.27), channel_id=1, source_target_pairs={{8,16},{24,0},{16,8},{0,24},{9,17},{25,1},{17,9},{1,25},{10,18},{2... | collective-permute-start | bytes 884744 | tf_op jit(solution)/shard_map/ppermute | solution.py:794
  63.9 2.0 %collective-permute-start.6 = (f32[1024,128]{1,0:T(8,128)S(1)}, f32[1024,128]{1,0:T(8,128)S(1)}, u32[]{:S(2)}, u32[]{:S(2)}) collective-permute-start(f32[1024,128]{1,0:T(8,128)S(1)} %get-tuple-element.29), channel_id=1, source_target_pairs={{0,1},{1,0},{2,3},{3,2},{4,5},{5,4},{6,7},{7,6},{8,9},{9,8},{10,11... | collective-permute-start | bytes 1572872 | tf_op jit(solution)/shard_map/ppermute | solution.py:786
  66.0 4.8 %collective-permute-start.7 = (f32[184,128]{1,0:T(8,128)S(1)}, f32[184,128]{1,0:T(8,128)S(1)}, u32[]{:S(2)}, u32[]{:S(2)}) collective-permute-start(f32[184,128]{1,0:T(8,128)S(1)} %get-tuple-element.31), channel_id=1, source_target_pairs={{0,2},{4,6},{2,0},{6,4},{1,3},{5,7},{3,1},{7,5},{8,10},{12,14},{10... | collective-permute-start | bytes 282632 | tf_op jit(solution)/shard_map/ppermute | solution.py:794
  66.1 7.8 %collective-permute-start.8 = (f32[184,128]{1,0:T(8,128)S(1)}, f32[184,128]{1,0:T(8,128)S(1)}, u32[]{:S(2)}, u32[]{:S(2)}) collective-permute-start(f32[184,128]{1,0:T(8,128)S(1)} %get-tuple-element.32), channel_id=1, source_target_pairs={{2,4},{6,0},{4,2},{0,6},{3,5},{7,1},{5,3},{1,7},{10,12},{14,8},{12... | collective-permute-start | bytes 282632 | tf_op jit(solution)/shard_map/ppermute | solution.py:794
  74.8 7.3 %collective-permute-start.9 = (f32[336,128]{1,0:T(8,128)S(1)}, f32[336,128]{1,0:T(8,128)S(1)}, u32[]{:S(2)}, u32[]{:S(2)}) collective-permute-start(f32[336,128]{1,0:T(8,128)S(1)} %get-tuple-element.34), channel_id=1, source_target_pairs={{0,8},{16,24},{8,0},{24,16},{1,9},{17,25},{9,1},{25,17},{2,10},{18... | collective-permute-start | bytes 516104 | tf_op jit(solution)/shard_map/ppermute | solution.py:794
  76.3 7.6 %collective-permute-start.10 = (f32[336,128]{1,0:T(8,128)S(1)}, f32[336,128]{1,0:T(8,128)S(1)}, u32[]{:S(2)}, u32[]{:S(2)}) collective-permute-start(f32[336,128]{1,0:T(8,128)S(1)} %get-tuple-element.35), channel_id=1, source_target_pairs={{8,16},{24,0},{16,8},{0,24},{9,17},{25,1},{17,9},{1,25},{10,18},{2... | collective-permute-start | bytes 516104 | tf_op jit(solution)/shard_map/ppermute | solution.py:794
  91.4 4.4 %collective-permute-start.11 = (f32[96,128]{1,0:T(8,128)S(1)}, f32[96,128]{1,0:T(8,128)S(1)}, u32[]{:S(2)}, u32[]{:S(2)}) collective-permute-start(f32[96,128]{1,0:T(8,128)S(1)} %get-tuple-element.36), channel_id=1, source_target_pairs={{0,2},{4,6},{2,0},{6,4},{1,3},{5,7},{3,1},{7,5},{8,10},{12,14},{10... | collective-permute-start | bytes 147464 | tf_op jit(solution)/shard_map/ppermute | solution.py:794
  91.5 6.1 %collective-permute-start.12 = (f32[96,128]{1,0:T(8,128)S(1)}, f32[96,128]{1,0:T(8,128)S(1)}, u32[]{:S(2)}, u32[]{:S(2)}) collective-permute-start(f32[96,128]{1,0:T(8,128)S(1)} %get-tuple-element.36), channel_id=1, source_target_pairs={{2,4},{6,0},{4,2},{0,6},{3,5},{7,1},{5,3},{1,7},{10,12},{14,8},{12... | collective-permute-start | bytes 147464 | tf_op jit(solution)/shard_map/ppermute | solution.py:794
  97.5 6.2 %collective-permute-start.14 = (f32[288,128]{1,0:T(8,128)S(1)}, f32[288,128]{1,0:T(8,128)S(1)}, u32[]{:S(2)}, u32[]{:S(2)}) collective-permute-start(f32[288,128]{1,0:T(8,128)S(1)} %constant_dynamic-update-slice_fusion.own), channel_id=1, source_target_pairs={{8,16},{24,0},{16,8},{0,24},{9,17},{25,1},{17,9},{1,25},{10,18},{2... | collective-permute-start | bytes 442376 | tf_op jit(solution)/shard_map/ppermute | solution.py:794
  100.0 5.2 %collective-permute-start.13 = (f32[288,128]{1,0:T(8,128)S(1)}, f32[288,128]{1,0:T(8,128)S(1)}, u32[]{:S(2)}, u32[]{:S(2)}) collective-permute-start(f32[288,128]{1,0:T(8,128)S(1)} %constant_dynamic-update-slice_fusion.own), channel_id=1, source_target_pairs={{0,8},{16,24},{8,0},{24,16},{1,9},{17,25},{9,1},{25,17},{2,10},{18... | collective-permute-start | bytes 442376 | tf_op jit(solution)/shard_map/ppermute | solution.py:794
  100.5 4.7 %collective-permute-start.15 = (f32[288,128]{1,0:T(8,128)S(1)}, f32[288,128]{1,0:T(8,128)S(1)}, u32[]{:S(2)}, u32[]{:S(2)}) collective-permute-start(f32[288,128]{1,0:T(8,128)S(1)} %constant_dynamic-update-slice_fusion.own), channel_id=1, source_target_pairs={{0,1},{1,0},{2,3},{3,2},{4,5},{5,4},{6,7},{7,6},{8,9},{9,8},{10,11... | collective-permute-start | bytes 442376 | tf_op jit(solution)/shard_map/ppermute | solution.py:786
  103.7 1.5 %collective-permute-start.17 = (f32[288,128]{1,0:T(8,128)S(1)}, f32[288,128]{1,0:T(8,128)S(1)}, u32[]{:S(2)}, u32[]{:S(2)}) collective-permute-start(f32[288,128]{1,0:T(8,128)S(1)} %collective-permute-done.14.xb), channel_id=1, source_target_pairs={{0,1},{1,0},{2,3},{3,2},{4,5},{5,4},{6,7},{7,6},{8,9},{9,8},{10,11... | collective-permute-start | bytes 442376 | tf_op jit(solution)/shard_map/ppermute | solution.py:786
  105.2 1.4 collective-permute-start.16

commit v3 on v2

--- a/solution.py
+++ b/solution.py
@@ -18,6 +18,10 @@
     return pltpu.VMEM(shape, F32)
 
 
+def even(n):
+    return n + n % 2
+
+
 def shape(*dims):
     return jax.ShapeDtypeStruct(dims, F32)
 
@@ -29,21 +33,22 @@
     return total
 
 
-def call(kernel, outs, scratch=(), name=None):
+def call(kernel, outs, scratch=(), raw=False, tight=True):
     spec = pl.BlockSpec(memory_space=pltpu.VMEM)
+    source = pl.BlockSpec(memory_space=pl.ANY) if raw else spec
     single = not isinstance(outs, (list, tuple))
-    held = sum(size(o.shape) for o in ([outs] if single else outs)) + sum(size(r.shape) for r in scratch)
+    outer = sum(size(o.shape) for o in ([outs] if single else outs))
+    held = sum(size(r.shape) for r in scratch if not raw)
 
     def run(*args):
-        grant = held + sum(size(a.shape) for a in args) + 4 * 1024 * 1024
+        grant = (held if tight else held + outer + sum(size(a.shape) for a in args if not raw)) + 3 * 1024 * 1024
         return pl.pallas_call(
             kernel,
             out_shape=outs,
-            in_specs=[spec] * len(args),
+            in_specs=[source] * len(args),
             out_specs=spec if single else [spec] * len(outs),
             scratch_shapes=list(scratch),
             compiler_params=pltpu.CompilerParams(vmem_limit_bytes=min(grant, 62 * 1024 * 1024)),
-            name=name,
         )(*args)
 
     return run
@@ -67,20 +72,18 @@
     return jnp.dot(jnp.concatenate(split(value), axis=1), matrix, preferred_element_type=F32)
 
 
-def loop(count, body, unroll=1):
-    if count <= unroll:
-        for z in range(1, count + 1):
-            body(z)
+def loop(count, body, group=1):
+    if count <= group:
+        body(1, count)
         return
 
     def step(i, carry):
-        for j in range(unroll):
-            body(i * unroll + 1 + j)
+        body(i * group + 1, group)
         return carry
 
-    lax.fori_loop(0, count // unroll, step, 0)
-    for z in range(count - count % unroll + 1, count + 1):
-        body(z)
+    lax.fori_loop(0, count // group, step, 0)
+    if count % group:
+        body(count - count % group + 1, count % group)
 
 
 def iota(rows, cols, axis):
@@ -104,10 +107,10 @@
 
 
 class Level:
-    def __init__(self, refs, tiles=1, unroll=1):
+    def __init__(self, refs, tiles=1, group=2):
         groups = [list(refs[i : i + tiles]) for i in range(0, len(refs), tiles)]
         self.wx, self.wy, self.wz, self.f, self.dinv, self.u, self.v, self.d = groups
-        self.tiles, self.unroll = tiles, unroll
+        self.tiles, self.group = tiles, group
 
     def right(self, values):
         rolled = [roll(v, -1) for v in values]
@@ -144,75 +147,84 @@
     for row in rows:
         put(level.wz, 0, row, each(mean, get(coef, 0, row), get(coef, 1, row)))
 
-    def edge(z):
+    def edge(z, n):
         row = rows[0] - 8
-        put(level.wy, z, row, each(mean, get(coef, z, row), get(coef, z, row + 1)))
-
-    loop(planes, edge, level.unroll)
-
-    def body(z):
+        for i in range(n):
+            put(level.wy, z + i, row, each(mean, get(coef, z + i, row), get(coef, z + i, row + 1)))
+
+    loop(planes, edge, level.group)
+
+    def body(z, n):
         for row in rows:
-            a = get(coef, z, row)
-            wx = each(mean, a, level.right(a))
-            wy = each(mean, a, get(coef, z, row + 1))
-            wz = each(mean, a, get(coef, z + 1, row))
-            den = each(lambda p, q: p + q, wx, level.left(wx))
-            for more in (wy, each(mean, a, get(coef, z, row - 1)), wz, each(mean, a, get(coef, z - 1, row))):
-                den = each(lambda p, q: p + q, den, more)
-            c = get(level.dinv, z, row)
-            den = each(lambda p, q: p + q, den, c)
-            dinv = each(lambda m, v: jnp.where(m > 0.0, 1.0 / jnp.where(m > 0.0, v, 1.0), 0.0), c, den)
-            put(level.f, z, row, each(lambda v, w: v * w, get(level.f, z, row), dinv))
-            put(level.wx, z, row, wx)
-            put(level.wy, z, row, wy)
-            put(level.wz, z, row, wz)
-            put(level.dinv, z, row, dinv)
-
-    loop(planes, body, level.unroll)
-
-
-def scaled_residual(level, src, z, row):
-    u = get(src, z, row)
-    wx = get(level.wx, z, row)
-    total = each(lambda w, v: w * v, wx, level.right(u))
-    total = each(lambda s, v: s + v, total, level.left(each(lambda w, v: w * v, wx, u)))
+            column = [get(coef, z + i, row) for i in range(-1, n + 1)]
+            faces = [each(mean, p, q) for p, q in zip(column, column[1:])]
+            for i in range(n):
+                a = column[i + 1]
+                wx = each(mean, a, level.right(a))
+                wy = each(mean, a, get(coef, z + i, row + 1))
+                den = each(lambda p, q: p + q, wx, level.left(wx))
+                for more in (wy, each(mean, a, get(coef, z + i, row - 1)), faces[i], faces[i + 1]):
+                    den = each(lambda p, q: p + q, den, more)
+                c = get(level.dinv, z + i, row)
+                den = each(lambda p, q: p + q, den, c)
+                dinv = each(lambda m, v: jnp.where(m > 0.0, 1.0 / jnp.where(m > 0.0, v, 1.0), 0.0), c, den)
+                put(level.f, z + i, row, each(lambda v, w: v * w, get(level.f, z + i, row), dinv))
+                put(level.wx, z + i, row, wx)
+                put(level.wy, z + i, row, wy)
+                put(level.wz, z + i, row, faces[i + 1])
+                put(level.dinv, z + i, row, dinv)
+
+    loop(planes, body, level.group)
+
+
+def scaled_residual(level, src, z, n, row):
+    column = [get(src, z + i, row) for i in range(-1, n + 1)]
+    faces = [get(level.wz, z + i, row) for i in range(-1, n)]
     mac = lambda s, w, v: s + w * v
-    total = each(mac, total, get(level.wy, z, row), get(src, z, row + 1))
-    total = each(mac, total, get(level.wy, z, row - 1), get(src, z, row - 1))
-    total = each(mac, total, get(level.wz, z, row), get(src, z + 1, row))
-    total = each(mac, total, get(level.wz, z - 1, row), get(src, z - 1, row))
-    f = get(level.f, z, row)
-    dinv = get(level.dinv, z, row)
-    return u, dinv, each(lambda f_, d_, s, v: f_ + d_ * s - v, f, dinv, total, u)
+    result = []
+    for i in range(n):
+        u = column[i + 1]
+        wx = get(level.wx, z + i, row)
+        total = each(lambda w, v: w * v, wx, level.right(u))
+        total = each(lambda s, v: s + v, total, level.left(each(lambda w, v: w * v, wx, u)))
+        total = each(mac, total, get(level.wy, z + i, row), get(src, z + i, row + 1))
+        total = each(mac, total, get(level.wy, z + i, row - 1), get(src, z + i, row - 1))
+        total = each(mac, total, faces[i + 1], column[i + 2])
+        total = each(mac, total, faces[i], column[i])
+        f = get(level.f, z + i, row)
+        dinv = get(level.dinv, z + i, row)
+        result.append((u, dinv, each(lambda f_, d_, s, v: f_ + d_ * s - v, f, dinv, total, u)))
+    return result
 
 
 def sweep(level, src, dst, planes, rows, weights, last=False):
     keep, gain = weights
 
-    def body(z):
+    def body(z, n):
         for row in rows:
-            u, _, r = scaled_residual(level, src, z, row)
-            if keep == 0.0:
-                d = each(lambda v: gain * v, r)
-            else:
-                d = each(lambda p, v: keep * p + gain * v, get(level.d, z, row), r)
-            if last:
-                put(dst[:1], z, row, [u[0] + d[0]])
-                continue
-            put(level.d, z, row, d)
-            put(dst, z, row, each(lambda p, v: p + v, u, d))
-
-    loop(planes, body, level.unroll)
+            for i, (u, _, r) in enumerate(scaled_residual(level, src, z, n, row)):
+                if keep == 0.0:
+                    d = each(lambda v: gain * v, r)
+                else:
+                    d = each(lambda p, v: keep * p + gain * v, get(level.d, z + i, row), r)
+                if last:
+                    put(dst[:1], z + i, row, [u[0] + d[0]])
+                    continue
+                put(level.d, z + i, row, d)
+                put(dst, z + i, row, each(lambda p, v: p + v, u, d))
+
+    loop(planes, body, level.group)
 
 
 def presmooth(level, planes, rows, degree):
-    def start(z):
-        for row in rows:
-            d = each(lambda v: v * (1.0 / THETA), get(level.f, z, row))
-            put(level.d, z, row, d)
-            put(level.u, z, row, d)
-
-    loop(planes(0), start, level.unroll)
+    def start(z, n):
+        for i in range(n):
+            for row in rows:
+                d = each(lambda v: v * (1.0 / THETA), get(level.f, z + i, row))
+                put(level.d, z + i, row, d)
+                put(level.u, z + i, row, d)
+
+    loop(planes(0), start, level.group)
     src, dst = level.u, level.v
     for step, weights in enumerate(chebyshev(degree)[1:], 1):
         sweep(level, src, dst, planes(step), rows, weights)
@@ -231,8 +243,7 @@
 def residual_pair(level, src, k, rows, buf):
     for i, row in enumerate(rows):
         parts = []
-        for z in (2 * k + 1, 2 * k + 2):
-            _, dinv, r = scaled_residual(level, src, z, row)
+        for _, dinv, r in scaled_residual(level, src, 2 * k + 1, 2, row):
             ok = dinv[0] > 0.0
             parts.append(jnp.where(ok, r[0], 0.0) / jnp.where(ok, dinv[0], 1.0))
         buf[8 * i : 8 * i + 8, :] = parts[0] + parts[1]
@@ -345,16 +356,21 @@
 
 
 def zpack(plan):
-    def kernel(coeff, rhs, shift, out):
+    def kernel(coeff, rhs, shift, out, sems):
         core = lax.axis_index("pz")
-        i = 0
+        copies = []
         for ref, n in ((coeff, HALO + 1), (shift, HALO), (rhs, HALO)):
             for j in range(n):
                 p = plan.z - 1 - j
-                out[i] = ref[p + core * (plan.z - 1 - 2 * p)]
-                i += 1
-
-    return call(kernel, shape(3 * HALO + 1, plan.y, plan.x))
+                i = len(copies)
+                copies.append(pltpu.make_async_copy(ref.at[p + core * (plan.z - 1 - 2 * p)], out.at[i], sems.at[i]))
+        for copy in copies:
+            copy.start()
+        for copy in copies:
+            copy.wait()
+
+    count = 3 * HALO + 1
+    return call(kernel, shape(count, plan.y, plan.x), [pltpu.SemaphoreType.DMA((count,))], raw=True)
 
 
 def restrict_coefficients(plan):
@@ -527,7 +543,7 @@
 
 def zero(*groups):
     for ref in [ref for group in groups for ref in group]:
-        def body(z, ref=ref):
+        def body(z, n, ref=ref):
             ref[z - 1] = jnp.zeros(ref.shape[1:], F32)
         loop(ref.shape[0], body)
 
@@ -558,7 +574,7 @@
 
 
 def level0_scratch(plan):
-    return [vmem(plan.z + HALO + 2, plan.r0, LANES)] * 16
+    return [vmem(plan.z + HALO + 2, plan.r0, LANES)] * 6
 
 
 def fill1(plan, dst, p, own, own_first, yplace, before, after, xplace, base, left, right):
@@ -574,15 +590,16 @@
 
 
 def down0(plan):
-    def kernel(coeff, rhs, shift, zrecv, ya, yb, xa, xb, u_out, f_out, z_out, seen_y, seen_x, buf, *scratch):
+    def kernel(coeff, rhs, shift, zrecv, ya, yb, xa, xb, u_out, f_out, z_out, *rest):
+        kept, (seen_y, seen_x, buf), scratch = rest[:10], rest[10:13], rest[13:]
         core = lax.axis_index("pz")
         ends = stage_in(seen_y, ya, yb, "py") + stage_in(seen_x, xa, xb, "px")
-        level = Level(scratch, 2)
+        level = Level(kept + scratch, 2)
         level0(plan, level, core, coeff, rhs, shift, zrecv, *ends)
-        src, _ = presmooth(level, lambda s: plan.z + HALO - s, plan.wide0, DEG)
+        src, _ = presmooth(level, lambda s: even(plan.z + HALO - s), plan.wide0, DEG)
         main = src[0]
 
-        def keep(z):
+        def keep(z, n):
             u_out[z - 1] = main[z, ROW0 : ROW0 + plan.y, :]
 
         loop(plan.z, keep)
@@ -592,7 +609,7 @@
         rx = twice(pair_lanes(LANES, LANES, 0, 0, plan.x1, 0.125), 0)
         ro = twice(pair_lanes(LANES, LANES, 0, plan.x1, plan.x1, 0.125), 0)
 
-        def residual(z):
+        def residual(z, n):
             residual_pair(level, src, z - 1, plan.own0, buf)
             part = rows_dot(ry, buf[...])
             f_out[z - 1] = lanes_dot(part, rx)
@@ -606,6 +623,7 @@
         shape(plan.z1, plan.y1, LANES),
         shape(HALO * plan.y + plan.z1 * plan.y1, LANES),
     ]
+    outs += [shape(plan.z + HALO + 2, plan.r0, LANES)] * 10
     seen = [vmem(2, plan.ycount, LANES), vmem(2, plan.xcount, LANES)]
     return call(kernel, outs, seen + [vmem(plan.y, LANES)] + level0_scratch(plan))
 
@@ -617,7 +635,7 @@
         seen_y, seen_x, seen_y2, seen_x2, u, d, buf = scratch
         yends, xends = stage_in(seen_y, ya, yb, "py"), stage_in(seen_x, xa, xb, "px")
         yends2, xends2 = stage_in(seen_y2, ya2, yb2, "py"), stage_in(seen_x2, xa2, xb2, "px")
-        level = Level((wx, wy, wz, f, dinv, u, u_out, d), 1, 2)
+        level = Level((wx, wy, wz, f, dinv, u, u_out, d))
         zero(level.u, level.v)
         for o, j in plan.sides:
             p = j if o == 0 else planes - 1 - j
@@ -644,26 +662,29 @@
     return call(kernel, outs, seen + [vmem(*big)] * 2 + [vmem(plan.y1, LANES)])
 
 
-def prolong(src, tmp, planes, py, px, rows, unroll=1):
-    def body(z):
-        for out, matrix in zip(tmp, px):
-            out[z, rows, :] = rows_dot(py, lanes_dot(src[z], matrix))
-
-    loop(planes, body, unroll)
+def prolong(src, tmp, planes, py, px, rows, group=2):
+    def body(z, n):
+        for i in range(n):
+            for out, matrix in zip(tmp, px):
+                out[z + i, rows, :] = rows_dot(py, lanes_dot(src[z + i], matrix))
+
+    loop(planes, body, group)
 
 
 def correct(level, src, dst, tmp, fine_planes, rows):
-    def body(k):
+    def body(k, n):
         for row in rows:
-            own = each(lambda v: 0.75 * v, get(tmp, k, row))
-            for z, far in ((2 * k - 1, k - 1), (2 * k, k + 1)):
-                new = each(
-                    lambda n, f, m, v: v + jnp.where(m > 0.0, n + 0.25 * f, 0.0),
-                    own, get(tmp, far, row), get(level.dinv, z, row), get(src, z, row),
-                )
-                put(dst, z, row, new)
-
-    loop(fine_planes // 2, body, level.unroll)
+            column = [get(tmp, k + i, row) for i in range(-1, n + 1)]
+            for i in range(n):
+                own = each(lambda v: 0.75 * v, column[i + 1])
+                for z, far in ((2 * (k + i) - 1, column[i]), (2 * (k + i), column[i + 2])):
+                    new = each(
+                        lambda p, q, m, v: v + jnp.where(m > 0.0, p + 0.25 * q, 0.0),
+                        own, far, get(level.dinv, z, row), get(src, z, row),
+                    )
+                    put(dst, z, row, new)
+
+    loop(fine_planes // 2, body, level.group)
 
 
 def coarse(plan):
@@ -677,7 +698,7 @@
 
     def kernel(own, xa, xb, owno, xao, xbo, wx, wy, wz, f, dinv, u_in, e1, *scratch):
         l2, l3, (u1, d1, buf, tmp3, tmp2, seen) = scratch[:8], scratch[8:16], scratch[16:]
-        two, three = Level(l2, 1, 4), Level(l3, 1, 8)
+        two, three = Level(l2, 1, 4), Level(l3, 1, 4)
         zero(two.u, two.v, [*l3])
         odd = lax.axis_index("py") & 1
         here = lax.axis_index("py")
@@ -733,11 +754,11 @@
         lanes = jnp.where(lanes < LANES - 2 * x2 + 16, lanes, lanes - LANES) + 2 * x2
         px = twice(interp(lanes, iota(LANES, LANES, 0)), 0)
         py = twice(interp(iota(plan.r1, h2, 0) - ROW1 + 2 * y2, iota(plan.r1, h2, 1) - ROW2), 1)
-        one = Level((wx, wy, wz, f, dinv, u1, e1, d1), 1, 2)
+        one = Level((wx, wy, wz, f, dinv, u1, e1, d1))
         zero(one.u, one.v)
         prolong(src2[0], [tmp2], planes2, py, [px], slice(0, plan.r1), 2)
         correct(one, [u_in], one.v, [tmp2], planes1, plan.wide1)
-        src1, _ = postsmooth(one, one.v, one.u, lambda s: min(planes1, plan.z1 + 6 - s), plan.wide1, DEG)
+        src1, _ = postsmooth(one, one.v, one.u, lambda s: even(min(planes1, plan.z1 + 6 - s)), plan.wide1, DEG)
         assert src1[0] is e1
 
     big1 = (planes1 + 2, plan.r1, LANES)
@@ -751,13 +772,12 @@
     planes = plan.z + HALO
     few = HALO // 2 + plan.z1 + 1
 
-    def kernel(coeff, rhs, shift, zrecv, ya, yb, xa, xb, u_in, zrecv2, ya2, yb2, xa2, xb2, e1, out, *scratch):
-        seen_y, seen_x, seen_y2, seen_x2, tmp, tmps = scratch[:6]
+    def kernel(u_in, zrecv2, ya2, yb2, xa2, xb2, e1, *rest):
+        kept, out, (seen_y2, seen_x2, tmp, tmps), scratch = rest[:10], rest[10], rest[11:15], rest[15:]
         core = lax.axis_index("pz")
-        ends = stage_in(seen_y, ya, yb, "py") + stage_in(seen_x, xa, xb, "px")
         ends2 = stage_in(seen_y2, ya2, yb2, "py") + stage_in(seen_x2, xa2, xb2, "px")
-        level = Level(scratch[6:], 2)
-        level0(plan, level, core, coeff, rhs, shift, zrecv, *ends)
+        level = Level(kept + scratch, 2)
+        zero(level.u, level.v)
         for p in range(planes):
             key = ("u", p)
             plane = u_plane(plan, p, u_in, zrecv2)
@@ -773,11 +793,11 @@
         side = twice(interp(jnp.where(lane < LANES // 2, lane + LANES, lane - LANES), coarse_lane), 0)
         prolong(e1, [tmp, tmps], few, py, [main, side], slice(first, first + count))
         correct(level, level.u, level.u, [tmp, tmps], planes, plan.wide0)
-        src, _ = postsmooth(level, level.u, level.v, lambda s: planes - 1 - s, plan.wide0, DEG, plan.own0)
+        src, _ = postsmooth(level, level.u, level.v, lambda s: even(planes - 1 - s), plan.wide0, DEG, plan.own0)
         for p in range(plan.z):
             out[p + core * (plan.z - 1 - 2 * p)] = src[0][p + 1, ROW0 : ROW0 + plan.y, :]
 
-    seen = [vmem(2, n, LANES) for n in (plan.ycount, plan.xcount, plan.ycount2, plan.xcount2)]
+    seen = [vmem(2, n, LANES) for n in (plan.ycount2, plan.xcount2)]
     tmps = [vmem(few + 2, plan.r0, LANES)] * 2
     return call(kernel, shape(plan.z, plan.y, LANES), seen + tmps + level0_scratch(plan))
 
@@ -786,12 +806,12 @@
     return lax.ppermute(value, axis, [(0, 1), (1, 0)])
 
 
-def meet(first, second, axis):
+def meet(first, second, axis, wrap=False):
     n = lax.axis_size(axis)
-    even = [(i, i + 1) for i in range(0, n, 2)]
-    odd = [(i, (i + 1) % n) for i in range(1, n, 2)]
+    low = [(i, i + 1) for i in range(0, n - 1, 2)]
+    high = [(i, (i + 1) % n) for i in range(1, n if wrap else n - 1, 2)]
     both = lambda pairs: pairs + [(j, i) for i, j in pairs]
-    return lax.ppermute(first, axis, both(even)), lax.ppermute(second, axis, both(odd))
+    return lax.ppermute(first, axis, both(low)), lax.ppermute(second, axis, both(high))
 
 
 def local(rhs, coeff, shift):
@@ -800,19 +820,19 @@
     ac = restrict_coefficients(plan)(coeff, shift)
     aco = swap(ac, "pz")
     ends_y = meet(*ypack(plan)(coeff, rhs, shift, zrecv, ac, aco), "py")
-    ends_x = meet(*xpack(plan)(coeff, rhs, shift, zrecv, ac, aco, *ends_y), "px")
+    ends_x = meet(*xpack(plan)(coeff, rhs, shift, zrecv, ac, aco, *ends_y), "px", True)
     fine = (coeff, rhs, shift, zrecv, *ends_y, *ends_x)
-    u, f, z_out = down0(plan)(*fine)
+    u, f, z_out, *kept = down0(plan)(*fine)
     zrecv2 = swap(z_out, "pz")
     first, second, pair = ypack2(plan)(u, zrecv2, f)
     ends_y2 = meet(first, second, "py")
-    ends_x2 = meet(*xpack2(plan)(u, zrecv2, pair, *ends_y2), "px")
+    ends_x2 = meet(*xpack2(plan)(u, zrecv2, pair, *ends_y2), "px", True)
     *one, message = down1(plan)(ac, aco, *ends_y, *ends_x, pair, *ends_y2, *ends_x2)
     first, second = meet(message, message, "py")
     wide = jnp.concatenate([first, message, second])
-    blocks = (wide, *meet(wide, wide, "px"))
+    blocks = (wide, *meet(wide, wide, "px", True))
     e1 = coarse(plan)(*blocks, *[swap(b, "pz") for b in blocks], *one)
-    return up0(plan)(*fine, u, zrecv2, *ends_y2, *ends_x2, e1)
+    return up0(plan)(u, zrecv2, *ends_y2, *ends_x2, e1, *kept)
 
 
 lower_bound = 0.4

time: 146 us -> 133 us (0.911)
  waiting for transfers between devices: 48.1 us -> 38.3 us
  Pallas kernels: 73.7 us -> 66.9 us
  starting transfers between devices: 19.4 us -> 22.3 us
    ppermute x12, waiting for transfers between devices: 43.7 us -> 33.6 us  [the longest x6 22.3 us: meet(): lax.ppermute(first, axis, both(low))]
    pallas_call x10, Pallas kernels: 73.7 us -> 66.9 us  [run(): pl.pallas_call(kernel, out_shape=outs, in_specs=[source] * len(args), out...]
    ppermute x12, starting transfers between devices: 18.2 us -> 21.6 us  [the longest x6 14.8 us: meet(): lax.ppermute(first, axis, both(low))]
  transfers between devices with their start and end apart: 18 -> 18, of which waited for: 15 -> 12; matrix products, arithmetic and copies ran while one was open for 0% -> 0% of each run, Pallas kernels for 1% -> 1%
where the time goes in v3:
time: 133 us; the launch traced here: 131 us
  Pallas kernels  66.9 us (50%)
  waiting for transfers between devices  38.3 us (29%)
  starting transfers between devices  22.3 us (17%)
  local copies, waits for them, and re-layouts  3.7 us (3%)
    pallas_call x10, Pallas kernels, run(): pl.pallas_call(kernel, out_shape=outs, in_specs=[source] * len(args), out...  66.9 us
    ppermute x6, waiting for transfers between devices, meet(): lax.ppermute(first, axis, both(low))  22.3 us
    ppermute x6, starting transfers between devices, meet(): lax.ppermute(first, axis, both(low))  14.8 us
    ppermute x6, waiting for transfers between devices, meet(): lax.ppermute(second, axis, both(high))  11.3 us
    ppermute x6, starting transfers between devices, meet(): lax.ppermute(second, axis, both(high))  6.75 us
    ppermute x6, waiting for transfers between devices, swap(): return lax.ppermute(value, axis, [(0, 1), (1, 0)])  4.78 us
    unnamed x14, local copies, waits for them, and re-layouts  3.7 us
  transfers between devices with their start and end apart: 18, of which 12 were waited for; matrix products, arithmetic and copies ran while one was open for 0% of the time, Pallas kernels for 1%

profile of v3, /device:TPU:0, one launch (start us, length us, event | category | flops | bytes accessed | tf_op | source)
XLA Modules:
  0.0 131.4 jit_solution(8999008510257573626)
XLA Ops:
  0.0 1.2 copy-done
  1.2 1.2 copy-done.2
  2.5 1.2 copy-done.4
  3.7 1.2 shard_map.37
  5.5 1.4 %shard_map.38.ac = f32[8,64,128]{2,1,0:T(8,128)S(1)} custom-call(f32[16,128,128]{2,1,0:T(8,128)S(1)} %copy-done, f32[16,128,128]{2,1,0:T(8,128)S(1)} %copy-done.3), custom_call_target="tpu_custom_call" | custom-call | tf_op jit(solution)/shard_map/pallas_call | solution.py:45
  6.9 1.5 %collective-permute-done.1.aco = f32[8,64,128]{2,1,0:T(8,128)S(1)} collective-permute-done((f32[8,64,128]{2,1,0:T(8,128)S(1)}, f32[8,64,128]{2,1,0:T(8,128)S(1)}, u32[]{:S(2)}, u32[]{:S(2)}) %collective-permute-start.1) | collective-permute-done | bytes 262176 | tf_op jit(solution)/shard_map/ppermute | solution.py:806
  8.6 2.8 %collective-permute-start.2 = (f32[424,128]{1,0:T(8,128)S(1)}, f32[424,128]{1,0:T(8,128)S(1)}, u32[]{:S(2)}, u32[]{:S(2)}) collective-permute-start(f32[424,128]{1,0:T(8,128)S(1)} %get-tuple-element.34), channel_id=1, source_target_pairs={{0,2},{4,6},{2,0},{6,4},{1,3},{5,7},{3,1},{7,5},{8,10},{12,14},{10... | collective-permute-start | bytes 651272 | tf_op jit(solution)/shard_map/ppermute | solution.py:814
  11.3 0.8 collective-permute-start.3
  12.1 5.1 %collective-permute-done.2.ya = f32[424,128]{1,0:T(8,128)S(1)} collective-permute-done((f32[424,128]{1,0:T(8,128)S(1)}, f32[424,128]{1,0:T(8,128)S(1)}, u32[]{:S(2)}, u32[]{:S(2)}) %collective-permute-start.2) | collective-permute-done | bytes 217120 | tf_op jit(solution)/shard_map/ppermute | solution.py:814
  17.2 2.2 %shard_map.40 = (f32[576,128]{1,0:T(8,128)S(1)}, f32[576,128]{1,0:T(8,128)S(1)}) custom-call(f32[16,128,128]{2,1,0:T(8,128)S(1)} %copy-done.1, f32[16,128,128]{2,1,0:T(8,128)S(1)} %copy-done.4, f32[16,128,128]{2,1,0:T(8,128)S(1)} %copy-done.3, f32[13,128,128]{2,1,0:T(8,128)S(1)} %collective-permute-done.zrecv, f32[8,64,128]{2,1,0:T(8,128)S(1)} %shard_map.38.ac, ...), custom_call_target="tpu_custom_call" | custom-call | tf_op jit(solution)/shard_map/pallas_call | solution.py:45
  19.4 1.7 %collective-permute-start.4 = (f32[576,128]{1,0:T(8,128)S(1)}, f32[576,128]{1,0:T(8,128)S(1)}, u32[]{:S(2)}, u32[]{:S(2)}) collective-permute-start(f32[576,128]{1,0:T(8,128)S(1)} %get-tuple-element.36), channel_id=1, source_target_pairs={{0,8},{16,24},{8,0},{24,16},{1,9},{17,25},{9,1},{25,17},{2,10},{18... | collective-permute-start | bytes 884744 | tf_op jit(solution)/shard_map/ppermute | solution.py:814
  21.1 1.5 %collective-permute-start.5 = (f32[576,128]{1,0:T(8,128)S(1)}, f32[576,128]{1,0:T(8,128)S(1)}, u32[]{:S(2)}, u32[]{:S(2)}) collective-permute-start(f32[576,128]{1,0:T(8,128)S(1)} %get-tuple-element.37), channel_id=1, source_target_pairs={{8,16},{24,0},{16,8},{0,24},{9,17},{25,1},{17,9},{1,25},{10,18},{2... | collective-permute-start | bytes 884744 | tf_op jit(solution)/shard_map/ppermute | solution.py:814
  22.6 6.7 %collective-permute-done.4.xa = f32[576,128]{1,0:T(8,128)S(1)} collective-permute-done((f32[576,128]{1,0:T(8,128)S(1)}, f32[576,128]{1,0:T(8,128)S(1)}, u32[]{:S(2)}, u32[]{:S(2)}) %collective-permute-start.4) | collective-permute-done | bytes 294944 | tf_op jit(solution)/shard_map/ppermute | solution.py:814
  29.3 6.0 %collective-permute-done.5.xb = f32[576,128]{1,0:T(8,128)S(1)} collective-permute-done((f32[576,128]{1,0:T(8,128)S(1)}, f32[576,128]{1,0:T(8,128)S(1)}, u32[]{:S(2)}, u32[]{:S(2)}) %collective-permute-start.5) | collective-permute-done | bytes 294944 | tf_op jit(solution)/shard_map/ppermute | solution.py:814
  35.3 21.5 %shard_map.41 = (f32[16,128,128]{2,1,0:T(8,128)S(1)}, f32[8,64,128]{2,1,0:T(8,128)S(1)}, f32[1024,128]{1,0:T(8,128)S(1)}, f32[22,160,128]{2,1,0:T(8,128)S(1)}, f...) custom-call(f32[16,128,128]{2,1,0:T(8,128)S(1)} %copy-done.1, ...), custom_call_target="tpu_custom_call" | custom-call | tf_op jit(solution)/shard_map/pallas_call | solution.py:45
  57.0 1.9 %collective-permute-done.6.zrecv.zrecv2 = f32[1024,128]{1,0:T(8,128)S(1)} collective-permute-done((f32[1024,128]{1,0:T(8,128)S(1)}, f32[1024,128]{1,0:T(8,128)S(1)}, u32[]{:S(2)}, u32[]{:S(2)}) %collective-permute-start.6) | collective-permute-done | bytes 524320 | tf_op jit(solution)/shard_map/ppermute | solution.py:806
  58.9 4.8 %collective-permute-start.7 = (f32[184,128]{1,0:T(8,128)S(1)}, f32[184,128]{1,0:T(8,128)S(1)}, u32[]{:S(2)}, u32[]{:S(2)}) collective-permute-start(f32[184,128]{1,0:T(8,128)S(1)} %get-tuple-element.41), channel_id=1, source_target_pairs={{0,2},{4,6},{2,0},{6,4},{1,3},{5,7},{3,1},{7,5},{8,10},{12,14},{10... | collective-permute-start | bytes 282632 | tf_op jit(solution)/shard_map/ppermute | solution.py:814
  64.4 2.3 %collective-permute-done.7.ya.ya2 = f32[184,128]{1,0:T(8,128)S(1)} collective-permute-done((f32[184,128]{1,0:T(8,128)S(1)}, f32[184,128]{1,0:T(8,128)S(1)}, u32[]{:S(2)}, u32[]{:S(2)}) %collective-permute-start.7) | collective-permute-done | bytes 94240 | tf_op jit(solution)/shard_map/ppermute | solution.py:814
  66.7 0.8 shard_map.43
  67.6 1.6 %collective-permute-start.9 = (f32[336,128]{1,0:T(8,128)S(1)}, f32[336,128]{1,0:T(8,128)S(1)}, u32[]{:S(2)}, u32[]{:S(2)}) collective-permute-start(f32[336,128]{1,0:T(8,128)S(1)} %get-tuple-element.44), channel_id=1, source_target_pairs={{0,8},{16,24},{8,0},{24,16},{1,9},{17,25},{9,1},{25,17},{2,10},{18... | collective-permute-start | bytes 516104 | tf_op jit(solution)/shard_map/ppermute | solution.py:814
  69.6 5.3 %collective-permute-done.9.xa2 = f32[336,128]{1,0:T(8,128)S(1)} collective-permute-done((f32[336,128]{1,0:T(8,128)S(1)}, f32[336,128]{1,0:T(8,128)S(1)}, u32[]{:S(2)}, u32[]{:S(2)}) %collective-permute-start.9) | collective-permute-done | bytes 172064 | tf_op jit(solution)/shard_map/ppermute | solution.py:814
  74.9 2.2 %collective-permute-done.10.xb2 = f32[336,128]{1,0:T(8,128)S(1)} collective-permute-done((f32[336,128]{1,0:T(8,128)S(1)}, f32[336,128]{1,0:T(8,128)S(1)}, u32[]{:S(2)}, u32[]{:S(2)}) %collective-permute-start.10) | collective-permute-done | bytes 172064 | tf_op jit(solution)/shard_map/ppermute | solution.py:814
  77.1 7.3 %shard_map.44 = (f32[18,112,128]{2,1,0:T(8,128)S(1)}, f32[18,112,128]{2,1,0:T(8,128)S(1)}, f32[18,112,128]{2,1,0:T(8,128)S(1)}, f32[18,112,128]{2,1,0:T(8,128)S(...) custom-call(f32[8,64,128]{2,1,0:T(8,128)S(1)} %shard_map.38.ac, ...), custom_call_target="tpu_custom_call" | custom-call | tf_op jit(solution)/shard_map/pallas_call | solution.py:45
  84.4 3.4 %collective-permute-start.11 = (f32[96,128]{1,0:T(8,128)S(1)}, f32[96,128]{1,0:T(8,128)S(1)}, u32[]{:S(2)}, u32[]{:S(2)}) collective-permute-start(f32[96,128]{1,0:T(8,128)S(1)} %get-tuple-element.46), channel_id=1, source_target_pairs={{0,2},{4,6},{2,0},{6,4},{1,3},{5,7},{3,1},{7,5},{8,10},{12,14},{10... | collective-permute-start | bytes 147464 | tf_op jit(solution)/shard_map/ppermute | solution.py:814
  87.9 0.8 collective-permute-start.12
  88.7 1.2 collective-permute-done.11
  90.0 2.5 %collective-permute-start.14 = (f32[288,128]{1,0:T(8,128)S(1)}, f32[288,128]{1,0:T(8,128)S(1)}, u32[]{:S(2)}, u32[]{:S(2)}) collective-permute-start(f32[288,128]{1,0:T(8,128)S(1)} %constant_dynamic-update-slice_fusion.own), channel_id=1, source_target_pairs={{8,16},{24,0},{16,8},{0,24},{9,17},{25,1},{17,9},{1,25},{10,18},{2... | collective-permute-start | bytes 442376 | tf_op jit(solution)/shard_map/ppermute | solution.py:814
  93.0 3.1 %collective-permute-done.14.xb = f32[288,128]{1,0:T(8,128)S(1)} collective-permute-done((f32[288,128]{1,0:T(8,128)S(1)}, f32[288,128]{1,0:T(8,128)S(1)}, u32[]{:S(2)}, u32[]{:S(2)}) %collective-permute-start.14) | collective-permute-done | bytes 147488 | tf_op jit(solution)/shard_map/ppermute | solution.py:814
  96.1 1.6 %collective-permute-done.13.xa = f32[288,128]{1,0:T(8,128)S(1)} collective-permute-done((f32[288,128]{1,0:T(8,128)S(1)}, f32[288,128]{1,0:T(8,128)S(1)}, u32[]{:S(2)}, u32[]{:S(2)}) %collective-permute-start.13) | collective-permute-done | bytes 147488 | tf_op jit(solution)/shard_map/ppermute | solution.py:814
  97.7 1.4 %collective-permute-done.16.xao = f32[288,128]{1,0:T(8,128)S(1)} collective-permute-done((f32[288,128]{1,0:T(8,128)S(1)}, f32[288,128]{1,0:T(8,128)S(1)}, u32[]{:S(2)}, u32[]{:S(2)}) %collective-permute-start.16) | collective-permute-done | bytes 147488 | tf_op jit(solution)/shard_map/ppermute | solution.py:806
  99.1 13.0 %shard_map.45.e1 = f32[18,112,128]{2,1,0:T(8,128)S(1)} custom-call(f32[288,128]{1,0:T(8,128)S(1)} %constant_dynamic-update-slice_fusion.own, f32[288,128]{1,0:T(8,128)S(1)} %collective-permute-done.13.xa, f32[288,128]{1,0:T(8,128)S(1)} %collective-permute-done.14.xb, f32[288,128]{1,0:T(8,128)S(1)} %collective-permute-done.15.owno, ...), custom_call_target="tpu_custom_call" | custom-call | tf_op jit(solution)/shard_map/pallas_call | solution.py:45
  112.1 19.3 %shard_map.46 = f32[16,128,128]{2,1,0:T(8,128)} custom-call(f32[16,128,128]{2,1,0:T(8,128)S(1)} %get-tuple-element.38.u.u_in, f32[1024,128]{1,0:T(8,128)S(1)} %collective-permute-done.6.zrecv.zrecv2, f32[184,128]{1,0:T(8,128)S(1)} %collective-permute-done.7.ya.ya2, f32[184,128]{1,0:T(8,128)S(1)} %collective-permute-done.8.yb.yb2, ...), custom_call_target="tpu_custom_call" | custom-call | tf_op jit(solution)/shard_map/pallas_call | solution.py:45
  (29 shorter events, 2.6 us)
Async XLA Ops:
  0.0 1.2 copy-start
  1.2 1.2 copy-start.2
  2.5 1.2 copy-start.4
  3.7 1.8 %copy-start.3 = (f32[16,128,128]{2,1,0:T(8,128)S(1)}, f32[16,128,128]{2,1,0:T(8,128)}, u32[]{:S(2)}) copy-start(f32[16,128,128]{2,1,0:T(8,128)} %shift.9) | copy-start | bytes 3145732
  4.9 3.5 %copy-start.1 = (f32[16,128,128]{2,1,0:T(8,128)S(1)}, f32[16,128,128]{2,1,0:T(8,128)}, u32[]{:S(2)}) copy-start(f32[16,128,128]{2,1,0:T(8,128)} %coeff.9) | copy-start | bytes 3145732
  4.9 3.5 %collective-permute-start = (f32[13,128,128]{2,1,0:T(8,128)S(1)}, f32[13,128,128]{2,1,0:T(8,128)S(1)}, u32[]{:S(2)}, u32[]{:S(2)}) collective-permute-start(f32[13,128,128]{2,1,0:T(8,128)S(1)} %shard_map.37), channel_id=1, source_target_pairs={{0,1},{1,0},{2,3},{3,2},{4,5},{5,4},{6,7},{7,6},{8,9},{9,8},{10,11... | collective-permute-start | bytes 2555912 | tf_op jit(solution)/shard_map/ppermute | solution.py:806
  6.8 1.6 %collective-permute-start.1 = (f32[8,64,128]{2,1,0:T(8,128)S(1)}, f32[8,64,128]{2,1,0:T(8,128)S(1)}, u32[]{:S(2)}, u32[]{:S(2)}) collective-permute-start(f32[8,64,128]{2,1,0:T(8,128)S(1)} %shard_map.38.ac), channel_id=1, source_target_pairs={{0,1},{1,0},{2,3},{3,2},{4,5},{5,4},{6,7},{7,6},{8,9},{9,8},{10,11... | collective-permute-start | bytes 786440 | tf_op jit(solution)/shard_map/ppermute | solution.py:806
  8.6 8.6 %collective-permute-start.2 = (f32[424,128]{1,0:T(8,128)S(1)}, f32[424,128]{1,0:T(8,128)S(1)}, u32[]{:S(2)}, u32[]{:S(2)}) collective-permute-start(f32[424,128]{1,0:T(8,128)S(1)} %get-tuple-element.34), channel_id=1, source_target_pairs={{0,2},{4,6},{2,0},{6,4},{1,3},{5,7},{3,1},{7,5},{8,10},{12,14},{10... | collective-permute-start | bytes 651272 | tf_op jit(solution)/shard_map/ppermute | solution.py:814
  11.3 24.0 %copy-start.5 = (f32[16,128,128]{2,1,0:T(8,128)S(1)}, f32[16,128,128]{2,1,0:T(8,128)}, u32[]{:S(2)}) copy-start(f32[16,128,128]{2,1,0:T(8,128)} %rhs.7) | copy-start | bytes 3145732
  11.3 5.9 %collective-permute-start.3 = (f32[424,128]{1,0:T(8,128)S(1)}, f32[424,128]{1,0:T(8,128)S(1)}, u32[]{:S(2)}, u32[]{:S(2)}) collective-permute-start(f32[424,128]{1,0:T(8,128)S(1)} %get-tuple-element.35), channel_id=1, source_target_pairs={{2,4},{4,2},{3,5},{5,3},{10,12},{12,10},{11,13},{13,11},{18,20},{2... | collective-permute-start | bytes 651272 | tf_op jit(solution)/shard_map/ppermute | solution.py:814
  19.4 9.9 %collective-permute-start.4 = (f32[576,128]{1,0:T(8,128)S(1)}, f32[576,128]{1,0:T(8,128)S(1)}, u32[]{:S(2)}, u32[]{:S(2)}) collective-permute-start(f32[576,128]{1,0:T(8,128)S(1)} %get-tuple-element.36), channel_id=1, source_target_pairs={{0,8},{16,24},{8,0},{24,16},{1,9},{17,25},{9,1},{25,17},{2,10},{18... | collective-permute-start | bytes 884744 | tf_op jit(solution)/shard_map/ppermute | solution.py:814
  21.1 14.2 %collective-permute-start.5 = (f32[576,128]{1,0:T(8,128)S(1)}, f32[576,128]{1,0:T(8,128)S(1)}, u32[]{:S(2)}, u32[]{:S(2)}) collective-permute-start(f32[576,128]{1,0:T(8,128)S(1)} %get-tuple-element.37), channel_id=1, source_target_pairs={{8,16},{24,0},{16,8},{0,24},{9,17},{25,1},{17,9},{1,25},{10,18},{2... | collective-permute-start | bytes 884744 | tf_op jit(solution)/shard_map/ppermute | solution.py:814
  56.9 2.0 %collective-permute-start.6 = (f32[1024,128]{1,0:T(8,128)S(1)}, f32[1024,128]{1,0:T(8,128)S(1)}, u32[]{:S(2)}, u32[]{:S(2)}) collective-permute-start(f32[1024,128]{1,0:T(8,128)S(1)} %get-tuple-element.39), channel_id=1, source_target_pairs={{0,1},{1,0},{2,3},{3,2},{4,5},{5,4},{6,7},{7,6},{8,9},{9,8},{10,11... | collective-permute-start | bytes 1572872 | tf_op jit(solution)/shard_map/ppermute | solution.py:806
  58.9 7.8 %collective-permute-start.7 = (f32[184,128]{1,0:T(8,128)S(1)}, f32[184,128]{1,0:T(8,128)S(1)}, u32[]{:S(2)}, u32[]{:S(2)}) collective-permute-start(f32[184,128]{1,0:T(8,128)S(1)} %get-tuple-element.41), channel_id=1, source_target_pairs={{0,2},{4,6},{2,0},{6,4},{1,3},{5,7},{3,1},{7,5},{8,10},{12,14},{10... | collective-permute-start | bytes 282632 | tf_op jit(solution)/shard_map/ppermute | solution.py:814
  63.7 3.0 %collective-permute-start.8 = (f32[184,128]{1,0:T(8,128)S(1)}, f32[184,128]{1,0:T(8,128)S(1)}, u32[]{:S(2)}, u32[]{:S(2)}) collective-permute-start(f32[184,128]{1,0:T(8,128)S(1)} %get-tuple-element.42), channel_id=1, source_target_pairs={{2,4},{4,2},{3,5},{5,3},{10,12},{12,10},{11,13},{13,11},{18,20},{2... | collective-permute-start | bytes 282632 | tf_op jit(solution)/shard_map/ppermute | solution.py:814
  67.6 7.3 %collective-permute-start.9 = (f32[336,128]{1,0:T(8,128)S(1)}, f32[336,128]{1,0:T(8,128)S(1)}, u32[]{:S(2)}, u32[]{:S(2)}) collective-permute-start(f32[336,128]{1,0:T(8,128)S(1)} %get-tuple-element.44), channel_id=1, source_target_pairs={{0,8},{16,24},{8,0},{24,16},{1,9},{17,25},{9,1},{25,17},{2,10},{18... | collective-permute-start | bytes 516104 | tf_op jit(solution)/shard_map/ppermute | solution.py:814
  69.1 8.0 %collective-permute-start.10 = (f32[336,128]{1,0:T(8,128)S(1)}, f32[336,128]{1,0:T(8,128)S(1)}, u32[]{:S(2)}, u32[]{:S(2)}) collective-permute-start(f32[336,128]{1,0:T(8,128)S(1)} %get-tuple-element.45), channel_id=1, source_target_pairs={{8,16},{24,0},{16,8},{0,24},{9,17},{25,1},{17,9},{1,25},{10,18},{2... | collective-permute-start | bytes 516104 | tf_op jit(solution)/shard_map/ppermute | solution.py:814
  84.4 5.5 %collective-permute-start.11 = (f32[96,128]{1,0:T(8,128)S(1)}, f32[96,128]{1,0:T(8,128)S(1)}, u32[]{:S(2)}, u32[]{:S(2)}) collective-permute-start(f32[96,128]{1,0:T(8,128)S(1)} %get-tuple-element.46), channel_id=1, source_target_pairs={{0,2},{4,6},{2,0},{6,4},{1,3},{5,7},{3,1},{7,5},{8,10},{12,14},{10... | collective-permute-start | bytes 147464 | tf_op jit(solution)/shard_map/ppermute | solution.py:814
  87.9 2.1 %collective-permute-start.12 = (f32[96,128]{1,0:T(8,128)S(1)}, f32[96,128]{1,0:T(8,128)S(1)}, u32[]{:S(2)}, u32[]{:S(2)}) collective-permute-start(f32[96,128]{1,0:T(8,128)S(1)} %get-tuple-element.46), channel_id=1, source_target_pairs={{2,4},{4,2},{3,5},{5,3},{10,12},{12,10},{11,13},{13,11},{18,20},{2... | collective-permute-start | bytes 147464 | tf_op jit(solution)/shard_map/ppermute | solution.py:814
  90.0 6.1 %collective-permute-start.14 = (f32[288,128]{1,0:T(8,128)S(1)}, f32[288,128]{1,0:T(8,128)S(1)}, u32[]{:S(2)}, u32[]{:S(2)}) collective-permute-start(f32[288,128]{1,0:T(8,128)S(1)} %constant_dynamic-update-slice_fusion.own), channel_id=1, source_target_pairs={{8,16},{24,0},{16,8},{0,24},{9,17},{25,1},{17,9},{1,25},{10,18},{2... | collective-permute-start | bytes 442376 | tf_op jit(solution)/shard_map/ppermute | solution.py:814
  92.5 5.2 %collective-permute-start.13 = (f32[288,128]{1,0:T(8,128)S(1)}, f32[288,128]{1,0:T(8,128)S(1)}, u32[]{:S(2)}, u32[]{:S(2)}) collective-permute-start(f32[288,128]{1,0:T(8,128)S(1)} %constant_dynamic-update-slice_fusion.own), channel_id=1, source_target_pairs={{0,8},{16,24},{8,0},{24,16},{1,9},{17,25},{9,1},{25,17},{2,10},{18... | collective-permute-start | bytes 442376 | tf_op jit(solution)/shard_map/ppermute | solution.py:814
  93.0 4.7 %collective-permute-start.15 = (f32[288,128]{1,0:T(8,128)S(1)}, f32[288,128]{1,0:T(8,128)S(1)}, u32[]{:S(2)}, u32[]{:S(2)}) collective-permute-start(f32[288,128]{1,0:T(8,128)S(1)} %constant_dynamic-update-slice_fusion.own), channel_id=1, source_target_pairs={{0,1},{1,0},{2,3},{3,2},{4,5},{5,4},{6,7},{7,6},{8,9},{9,8},{10,11... | collective-permute-start | bytes 442376 | tf_op jit(solution)/shard_map/ppermute | solution.py:806
  96.1 1.6 %collective-permute-start.17 = (f32[288,128]{1,0:T(8,128)S(1)}, f32[288,128]{1,0:T(8,128)S(1)}, u32[]{:S(2)}, u32[]{:S(2)}) collective-permute-start(f32[288,128]{1,0:T(8,128)S(1)} %collective-permute-done.14.xb), channel_id=1, source_target_pairs={{0,1},{1,0},{2,3},{3,2},{4,5},{5,4},{6,7},{7,6},{8,9},{9,8},{10,11... | collective-permute-start | bytes 442376 | tf_op jit(solution)/shard_map/ppermute | solution.py:806
  97.7 1.4 %collective-permute-start.16 = (f32[288,128]{1,0:T(8,128)S(1)}, f32[288,128]{1,0:T(8,128)S(1)}, u32[]{:S(2)}, u32[]{:S(2)}) collective-permute-start(f32[288,128]{1,0:T(8,128)S(1)} %collective-permute-done.13.xa), channel_id=1, source_target_pairs={{0,1},{1,0},{2,3},{3,2},{4,5},{5,4},{6,7},{7,6},{8,9},{9,8},{10,11... | collective-permute-start | bytes 442376 | tf_op jit(solution)/shard_map/ppermute | solution.py:806
